TPU v7x, 32 devices: a whole 2x2x4 slice. The times are simulated.
32 devices in a mesh: wide: 8 (over y, x, core), narrow: 4 (over z).
Axes of the slice: x: 2, y: 2, z: 4, core: 2. Of those that a mesh axis runs over, the one named last changes fastest.
Arguments:
- hidden: bfloat16 [1024, 4096], P('wide', 'narrow'), may hold values from -6 to 6
- head_weight: bfloat16 [32768, 4096], P('wide', 'narrow'), may hold values from -0.25 to 0.25
- lse: float32 [1024], replicated, may hold values from 12 to 14
- targets: int32 [1024], replicated, may hold values from 0 to 32767
- loss_weight: float32 [1024], replicated, may hold values from 16 to 48
- block_tiles: int32 [8, 8, 4], P(None, 'wide'), may hold values from 0 to 31, as said below
- block_counts: int32 [8, 8], P(None, 'wide'), may hold values from 0 to 4, as said below
- gate_pre: bfloat16 [1024, 7168], P('wide', 'narrow'), may hold values from -6 to 6
- up_pre: bfloat16 [1024, 7168], P('wide', 'narrow'), may hold values from -6 to 6
- down_weight: bfloat16 [7168, 4096], P('narrow'), may hold values from -0.0625 to 0.0625
Outputs:
- head_grad: bfloat16 [1024, 4096], P('wide', 'narrow')
- gate_grad: bfloat16 [1024, 7168], P('wide', 'narrow')
- up_grad: bfloat16 [1024, 7168], P('wide', 'narrow')
Inputs may be any that keep to these rules, and one draw needn't show every extreme that they name: The first block_counts[b, s] entries of block_tiles[b, s] are distinct; the other entries are ignored. `block_counts`: some row block has 4 active tiles in some shard; one shard has exactly 16 active tiles over all row blocks, and no shard has more.
All inputs are finite; a program needn't handle non-finite values.
Results may differ from a plain program's by a relative error of at most 0.0035.
The roundings to bfloat16 on the way count: a program that leaves them out, or rounds other values in their place, can miss the bound.
Values may be sent and summed in bfloat16 or wider, within the bound.
No kernel may reach another device: no remote copies, remote signals or barrier semaphores. Data moves between devices by JAX's collectives and lax.ppermute only.
A program may use at most 128 MiB of HBM per device.

v0:
```python
import functools

import jax
import jax.numpy as jnp
from jax import lax
from jax.experimental import pallas as pl
from jax.experimental.pallas import tpu as pltpu
from jax.sharding import PartitionSpec as P


TILE = 128
PAD = 8
GROUPS = 2
HALVES = 2
LARGE = 50
MEDIUM = 46
LEVELS = 32767.0
VMEM = pl.BlockSpec(memory_space=pltpu.VMEM)
SMEM = pl.BlockSpec(memory_space=pltpu.SMEM)
ANY = pl.BlockSpec(memory_space=pl.ANY)
HBM = pl.BlockSpec(memory_space=pltpu.HBM)


def swap(x, axis, mask):
    if mask == 0:
        return x
    size = lax.axis_size(axis)
    return lax.ppermute(x, axis, [(i, i ^ mask) for i in range(size)])


def step_of(code):
    return jnp.exp2(code * 0.125) * (1.0 / LEVELS)


def encode(x):
    peak = jnp.max(jnp.abs(x), axis=0, keepdims=True)
    code = jnp.ceil(8.0 * jnp.log2(jnp.maximum(peak, 1e-30)) + 0.25)
    levels = jnp.round(x * (1.0 / step_of(code)))
    return levels.astype(jnp.int32).astype(jnp.int16), code.astype(jnp.int32)


def decode(levels, code):
    return levels.astype(jnp.int32).astype(jnp.float32) * step_of(code.astype(jnp.float32))


def slots_kernel(slots, tiles_ref, counts_ref, blocks_out, tiles_out, live_out):
    blocks, _, per_block = tiles_ref.shape
    for slot in range(slots):
        blocks_out[slot] = 0
        tiles_out[slot] = 0
    live = jnp.int32(0)
    for block in range(blocks):
        count = counts_ref[block, 0]
        for j in range(per_block):

            @pl.when(j < count)
            def _(block=block, j=j, slot=live + j):
                blocks_out[slot] = block
                tiles_out[slot] = tiles_ref[block, 0, j]

        live = live + count
    live_out[0] = live


def logits_kernel(wide, narrow, slots, group, blocks_ref, tiles_ref, where_ref, head, *refs):
    me_w, me_n = where_ref[0], where_ref[1]
    per = slots // narrow
    share = per // GROUPS
    parts, own, sends = refs[:wide], refs[wide], refs[wide + 1 : wide + narrow]
    tiles, rows, row_sem, tile_sem = refs[wide + narrow :]
    order = [(k, i) for k in [*range(1, narrow), 0] for i in range(share)]

    def slot_of(k, i):
        return (me_n ^ k) * per + group * share + i

    def fetch(k, i):
        at = k * share + i
        start = pl.multiple_of(tiles_ref[slot_of(k, i)] * TILE, TILE)
        return pltpu.make_async_copy(
            head.at[pl.ds(start, TILE), :], tiles.at[pl.ds(at * TILE, TILE), :], tile_sem.at[at]
        )

    for k, i in order:
        fetch(k, i).start()
    copies = [pltpu.make_async_copy(parts[k], rows.at[k], row_sem.at[k]) for k in range(wide)]
    for copy in copies:
        copy.start()
    for send in sends:
        send[share * TILE :, :] = jnp.zeros((send.shape[0] - share * TILE, TILE), jnp.int16)
    for copy in copies:
        copy.wait()
    for k, i in order:
        at = k * share + i
        fetch(k, i).wait()
        part = lax.dot_general(
            rows[blocks_ref[slot_of(k, i)] ^ me_w],
            tiles[at * TILE : (at + 1) * TILE, :],
            (((1,), (1,)), ((), ())),
            preferred_element_type=jnp.float32,
        )
        if k == 0:
            own[i * TILE : (i + 1) * TILE, :] = part
        else:
            levels, code = encode(part)
            sends[k - 1][i * TILE : (i + 1) * TILE, :] = levels
            sends[k - 1][share * TILE + i : share * TILE + i + 1, :] = code.astype(jnp.int16)


def probs_kernel(narrow, slots, group, blocks_ref, live_ref, where_ref, own, *refs):
    recvs, lse, weight, out = refs[: narrow - 1], refs[-3], refs[-2], refs[-1]
    per = slots // narrow
    share = per // GROUPS
    codes = [recv[share * TILE :, :] for recv in recvs]
    for i in range(share):
        slot = where_ref[1] * per + group * share + i
        total = own[i * TILE : (i + 1) * TILE, :]
        for recv, code in zip(recvs, codes):
            total = total + decode(recv[i * TILE : (i + 1) * TILE, :], code[i : i + 1, :])
        rows = pl.ds(pl.multiple_of(blocks_ref[slot] * TILE, TILE), TILE)
        scaled = jnp.exp(total - lse[rows, :]) * weight[rows, :]
        out[i * TILE : (i + 1) * TILE, :] = jnp.where(slot < live_ref[0], scaled, 0.0).astype(
            jnp.bfloat16
        )


def grads_kernel(wide, narrow, slots, half, blocks_ref, where_ref, *refs):
    probs = refs[: narrow * GROUPS]
    tiles = refs[narrow * GROUPS : narrow * GROUPS + GROUPS]
    target_rows, factor, mine, other, total = refs[narrow * GROUPS + GROUPS :]
    me_w, me_n = where_ref[0], where_ref[1]
    per = slots // narrow
    share = per // GROUPS
    width = mine.shape[1]
    for block in range(factor.shape[0] // TILE):
        rows = slice(block * TILE, (block + 1) * TILE)
        weight = -factor[rows, :]
        for lane in range(0, width, TILE):
            at = half * width + lane
            total[block ^ me_w, :, lane : lane + TILE] = weight * target_rows[
                rows, at : at + TILE
            ].astype(jnp.float32)
    for k in range(narrow):
        for group in range(GROUPS):
            for i in range(share):
                slot = (me_n ^ k) * per + group * share + i
                total[blocks_ref[slot] ^ me_w] += jnp.dot(
                    probs[k * GROUPS + group][i * TILE : (i + 1) * TILE, :],
                    tiles[group][
                        (k * share + i) * TILE : (k * share + i + 1) * TILE,
                        half * width : (half + 1) * width,
                    ],
                    preferred_element_type=jnp.float32,
                )
    for chip in range(wide // 2):
        mine[chip * TILE : (chip + 1) * TILE, :] = total[2 * chip]
        other[chip * TILE : (chip + 1) * TILE, :] = total[2 * chip + 1]


def pack_kernel(chips, mine, other, own, *sends):
    for chip in [*range(1, chips), 0]:
        rows = slice(chip * TILE, (chip + 1) * TILE)
        if chip == 0:
            own[...] = mine[rows, :] + other[rows, :]
            continue
        send = sends[chip - 1]
        for lane in range(0, own.shape[1], TILE):
            lanes = slice(lane, lane + TILE)
            levels, code = encode(mine[rows, lanes] + other[rows, lanes])
            send[:TILE, lanes] = levels
            send[TILE:, lanes] = jnp.broadcast_to(code, (PAD, TILE)).astype(jnp.int16)


def merge_kernel(own, *refs):
    recvs, out = refs[:-1], refs[-1]
    for lane in range(0, own.shape[1], TILE):
        lanes = slice(lane, lane + TILE)
        total = own[:, lanes]
        for recv in recvs:
            total = total + decode(recv[:TILE, lanes], recv[TILE : TILE + 1, lanes])
        out[:, lanes] = total.astype(jnp.bfloat16)


def down_copies(keys, where_ref, down, out, sem, rows):
    width = out.shape[-1]

    def copy(at):
        mask, half = keys[at]
        start = pl.multiple_of((where_ref[1] ^ mask) * (width * HALVES) + half * width, width)
        return pltpu.make_async_copy(down.at[rows, pl.ds(start, width)], out.at[at], sem.at[at])

    return [copy(at) for at in range(len(keys))]


def hold_kernel(keys, where_ref, down, out, sem):
    copies = down_copies(keys, where_ref, down, out, sem, slice(None))
    for copy in copies:
        copy.start()
    for copy in copies:
        copy.wait()


def unit_kernel(keys, splits, kind, chunk, where_ref, *refs):
    count, inputs = len(keys), sum(splits)
    arrived, down, refs = list(refs[:inputs]), refs[inputs], refs[inputs + 1 :]
    units = down.shape[-2]
    width = arrived[0].shape[1]
    pieces = []
    for split in splits:
        piece = arrived.pop(0)[...]
        for _ in range(split - 1):
            piece = piece + arrived.pop(0)[...]
        pieces.append(piece)
    if kind == "last":
        summed, gate, up, gate_out, up_out = refs
    else:
        *refs, down_v, sem = refs
        if kind == "first":
            sum_out, grad_out = refs
            for at in range(count):
                grad_out[:, at * width : (at + 1) * width] = pieces[at]
        else:
            summed, sum_out = refs
    steps = [pl.ds(at, chunk) for at in range(0, units, chunk)]
    if kind != "last":
        copies = [
            down_copies(keys, where_ref, down, down_v.at[step], sem.at[step], rows)
            for step, rows in enumerate(steps)
        ]
        for copy in sum(copies, []):
            copy.start()
    for step, rows in enumerate(steps):
        total = None if kind == "first" else summed[:, rows]
        for at in range(count):
            if kind != "last":
                copies[step][at].wait()
            part = lax.dot_general(
                pieces[at],
                down[at, rows, :] if kind == "last" else down_v[step, at],
                (((1,), (1,)), ((), ())),
                preferred_element_type=jnp.float32,
            )
            total = part if total is None else total + part
        if kind != "last":
            sum_out[:, rows] = total
            continue
        g = gate[:, rows].astype(jnp.float32)
        u = up[:, rows].astype(jnp.float32)
        s = 1.0 / (1.0 + jnp.exp(-g))
        up_out[:, rows] = (total * g * s).astype(jnp.bfloat16)
        gate_out[:, rows] = (total * u * s * (1.0 + g * (1.0 - s))).astype(jnp.bfloat16)


def shape_of(shape, dtype):
    return jax.ShapeDtypeStruct(shape, dtype)


def call(kernel, outs, ins, args, flops, moved, scratch=(), mib=16, scalars=0):
    return pl.pallas_call(
        kernel,
        out_shape=outs,
        in_specs=ins,
        out_specs=[SMEM] * scalars + [VMEM] * (len(outs) - scalars),
        scratch_shapes=list(scratch),
        compiler_params=pltpu.CompilerParams(vmem_limit_bytes=mib * 1024 * 1024),
        cost_estimate=pl.CostEstimate(flops=flops, bytes_accessed=moved, transcendentals=0),
    )(*args)


def on_device(
    hidden,
    head_weight,
    lse,
    targets,
    loss_weight,
    block_tiles,
    block_counts,
    gate_pre,
    up_pre,
    down_weight,
):
    f32, bf16, i16 = jnp.float32, jnp.bfloat16, jnp.int16
    _, features = hidden.shape
    vocab_here = head_weight.shape[0]
    wide, narrow = lax.axis_size("wide"), lax.axis_size("narrow")
    chips = wide // 2
    me_w, me_n = lax.axis_index("wide"), lax.axis_index("narrow")
    where = jnp.stack([me_w, me_n]).astype(jnp.int32)
    blocks, per_block = block_tiles.shape[0], block_tiles.shape[2]
    slots = blocks // 2 * per_block
    share = slots // narrow // GROUPS
    width = features // HALVES

    far = [swap(hidden, "wide", 2 * chip) for chip in range(chips)]

    local_ids = targets - me_w * vocab_here
    inside = (local_ids >= 0) & (local_ids < vocab_here)
    clipped = jnp.clip(local_ids, 0, vocab_here - 1)
    target_rows = head_weight.at[clipped].get(mode="promise_in_bounds")

    def over_lanes(x):
        return jnp.broadcast_to(x[:, None], (blocks * TILE, TILE))

    far[1], target_rows = lax.optimization_barrier((far[1], target_rows))
    near = [swap(part, "wide", 1) for part in far]
    lse_rows, weight_rows = over_lanes(lse), over_lanes(loss_weight)
    factor = over_lanes(jnp.where(inside, loss_weight, 0.0))
    counts, target_rows, lse_rows, weight_rows, factor = lax.optimization_barrier(
        (block_counts, target_rows, lse_rows, weight_rows, factor)
    )
    slot_blocks, slot_tiles, live = call(
        functools.partial(slots_kernel, slots),
        [shape_of((slots,), jnp.int32)] * 2 + [shape_of((1,), jnp.int32)],
        [SMEM, SMEM],
        (block_tiles, counts),
        0,
        slots * 8,
        scalars=3,
    )
    parts = [part for pair in zip(far, near) for part in pair]

    units = gate_pre.shape[1]
    last_keys = [(k, HALVES - 1) for k in range(2, narrow)]
    probs, tiles = [], []
    for group in range(GROUPS):
        *result, tile = call(
            functools.partial(logits_kernel, wide, narrow, slots, group),
            [shape_of((share * TILE, TILE), f32)]
            + [shape_of((share * TILE + PAD, TILE), i16)] * (narrow - 1)
            + [shape_of((slots // GROUPS * TILE, features), bf16)],
            [SMEM] * 3 + [HBM] + [ANY] * wide,
            (slot_blocks, slot_tiles, where, head_weight, *parts),
            2 * slots * TILE * TILE * features // GROUPS,
            slots * TILE * features,
            [
                pltpu.VMEM((wide, TILE, features), bf16),
                pltpu.SemaphoreType.DMA((wide,)),
                pltpu.SemaphoreType.DMA((slots // GROUPS,)),
            ],
            MEDIUM,
        )
        tiles.append(tile)
        own, *sends = result
        recvs = [swap(send, "narrow", k + 1) for k, send in enumerate(sends)]
        (prob,) = call(
            functools.partial(probs_kernel, narrow, slots, group),
            [shape_of((share * TILE, TILE), bf16)],
            [SMEM] * 3 + [VMEM] * (narrow + 2),
            (slot_blocks, live, where, own, *recvs, lse_rows, weight_rows),
            share * TILE * TILE * 20,
            share * TILE * TILE * 12,
        )
        probs.append([swap(prob, "narrow", k) for k in range(narrow)])
    (held,) = call(
        functools.partial(hold_kernel, last_keys),
        [shape_of((len(last_keys), units, width), bf16)],
        [SMEM, HBM],
        (where, down_weight),
        0,
        len(last_keys) * units * width * 2,
        [pltpu.SemaphoreType.DMA((len(last_keys),))],
        MEDIUM,
    )
    tiles[0], held = lax.optimization_barrier((tiles[0], held))
    all_probs = [probs[group][k] for k in range(narrow) for group in range(GROUPS)]

    halves = []
    for half in range(HALVES):
        mine, other = call(
            functools.partial(grads_kernel, wide, narrow, slots, half),
            [shape_of((chips * TILE, width), f32)] * 2,
            [SMEM] * 2 + [VMEM] * (narrow * GROUPS + GROUPS + 2),
            (slot_blocks, where, *all_probs, *tiles, target_rows, factor),
            2 * slots * TILE * TILE * width,
            slots * TILE * width * 4,
            [pltpu.VMEM((wide, TILE, width), f32)],
        )
        halves.append((mine, swap(other, "wide", 1)))
    grads = []
    for half, (mine, other) in enumerate(halves):
        if half > 0:
            mine, grads[-1] = lax.optimization_barrier((mine, grads[-1]))
        kept, *packed = call(
            functools.partial(pack_kernel, chips),
            [shape_of((TILE, width), f32)]
            + [shape_of((TILE + PAD, width), i16)] * (chips - 1),
            [VMEM] * 2,
            (mine, other),
            chips * TILE * width * 8,
            chips * TILE * width * 10,
        )
        arrived = [swap(part, "wide", 2 * (k + 1)) for k, part in enumerate(packed)]
        (grad,) = call(
            merge_kernel,
            [shape_of((TILE, width), bf16)],
            [VMEM] * chips,
            (kept, *arrived),
            chips * TILE * width * 4,
            chips * TILE * width * 3,
        )
        grads.append(grad)

    pieces = {
        (k, half): (swap(grad, "narrow", k),)
        for half, grad in enumerate(grads)
        for k in range(narrow)
    }
    if narrow == 4:
        near_ends = lax.ppermute(grads[0], "narrow", [(1, 2), (2, 1)])
        ends = lax.ppermute(pieces[2, 0][0], "narrow", [(1, 0), (2, 3)])
        pieces[3, 0] = (near_ends, ends)
    chunk = units // 2 if units // 2 % TILE == 0 else units

    def unit(keys, kind, *extra):
        count = len(keys)
        last = kind == "last"
        inputs = [part for key in keys for part in pieces[key]]
        outs = [shape_of((TILE, units), f32)]
        if kind == "first":
            outs.append(shape_of((TILE, features), bf16))
        if last:
            outs = [shape_of((TILE, units), bf16)] * 2
        return call(
            functools.partial(unit_kernel, keys, [len(pieces[key]) for key in keys], kind, chunk),
            outs,
            [SMEM] + [VMEM] * len(inputs) + [VMEM if last else HBM] + [VMEM] * len(extra),
            (where, *inputs, held if last else down_weight, *extra),
            2 * count * TILE * units * width,
            count * units * width * 2,
            ()
            if last
            else (
                pltpu.VMEM((units // chunk, count, chunk, width), bf16),
                pltpu.SemaphoreType.DMA((units // chunk, count)),
            ),
            16 if last else LARGE,
        )

    summed, head_grad = unit([(0, half) for half in range(HALVES)], "first")
    (summed,) = unit([(k, 0) for k in range(1, narrow)], "more", summed)
    (summed,) = unit([(1, 1)], "more", summed)
    gate_grad, up_grad = unit(last_keys, "last", summed, gate_pre, up_pre)
    return head_grad, gate_grad, up_grad


def solution(mesh):
    in_specs = (
        P("wide", "narrow"),
        P("wide", "narrow"),
        P(),
        P(),
        P(),
        P(None, "wide", None),
        P(None, "wide"),
        P("wide", "narrow"),
        P("wide", "narrow"),
        P("narrow", None),
    )
    out_specs = (P("wide", "narrow"), P("wide", "narrow"), P("wide", "narrow"))

    return jax.shard_map(
        on_device, mesh=mesh, in_specs=in_specs, out_specs=out_specs, check_vma=False
    )
```

profile of v0, /device:TPU:0, one launch (start us, length us, event | category | flops | bytes accessed | tf_op | source)
XLA Modules:
  0.0 102.2 jit_solution(10471413794469350601)
XLA Ops:
  0.6 3.0 %collective-permute-start = (bf16[128,1024]{1,0:T(8,128)(2,1)}, bf16[128,1024]{1,0:T(8,128)(2,1)}, u32[]{:S(2)}, u32[]{:S(2)}) collective-permute-start(bf16[128,1024]{1,0:T(8,128)(2,1)} %refs_0_.3), channel_id=1, source_target_pairs={{0,8},{4,12},{8,0},{12,4},{16,24},{20,28},{24,16},{28,20},{1,9},{5... | collective-permute-start | bytes 786440 | tf_op jit(solution)/shard_map/ppermute | solution.py:28
  3.7 1.5 %collective-permute-start.3 = (bf16[128,1024]{1,0:T(8,128)(2,1)}, bf16[128,1024]{1,0:T(8,128)(2,1)}, u32[]{:S(2)}, u32[]{:S(2)}) collective-permute-start(bf16[128,1024]{1,0:T(8,128)(2,1)} %refs_0_.3), channel_id=1, source_target_pairs={{0,16},{4,20},{8,24},{12,28},{16,0},{20,4},{24,8},{28,12},{1,17},{... | collective-permute-start | bytes 786440 | tf_op jit(solution)/shard_map/ppermute | solution.py:28
  6.0 9.5 %gather_fusion = bf16[1024,1024]{1,0:T(8,128)(2,1)S(1)} fusion(bf16[4096,1024]{1,0:T(8,128)(2,1)} %head.3, s32[1024]{0:T(1024)S(1)} %fusion), kind=kCustom, calls=%fused_computation | custom fusion | bytes 4198400 | tf_op jit(solution)/shard_map/gather | solution.py:298
  20.9 5.5 %shard_map.124 = (f32[256,128]{1,0:T(8,128)S(1)}, s16[264,128]{1,0:T(8,128)(2,1)S(1)}, s16[264,128]{1,0:T(8,128)(2,1)S(1)}, s16[264,128]{1,0:T(8,128)(2,1)S(1)}, bf16[1024,1024]{1,0:T(8,128)(2,1)S(1)}) custom-call(s32[16]{0:T(128)S(1)} %get-tuple-element.45.blocks_ref, s32[16]{0:T(128)S(1)} %get-tuple-element.47.tiles_ref, s32[2]{0:T(128)S(1)} %pad_add_fusion.where_ref, ...), custom_call_target="tpu_custom_call" | custom-call | flops 268435456 | bytes 2097152 | tf_op jit(solution)/shard_map/pallas_call | solution.py:258
  26.4 1.6 %collective-permute-start.10 = (s16[264,128]{1,0:T(8,128)(2,1)S(1)}, s16[264,128]{1,0:T(8,128)(2,1)S(1)}, u32[]{:S(2)}, u32[]{:S(2)}) collective-permute-start(s16[264,128]{1,0:T(8,128)(2,1)S(1)} %get-tuple-element.56), channel_id=1, source_target_pairs={{0,1},{1,0},{2,3},{3,2},{4,5},{5,4},{6,7},{7,6},{8,9},{9,8},{10,11... | collective-permute-start | bytes 202760 | tf_op jit(solution)/shard_map/ppermute | solution.py:28
  28.0 2.6 %collective-permute-start.11 = (s16[264,128]{1,0:T(8,128)(2,1)S(1)}, s16[264,128]{1,0:T(8,128)(2,1)S(1)}, u32[]{:S(2)}, u32[]{:S(2)}) collective-permute-start(s16[264,128]{1,0:T(8,128)(2,1)S(1)} %get-tuple-element.57), channel_id=1, source_target_pairs={{0,2},{1,3},{2,0},{3,1},{4,6},{5,7},{6,4},{7,5},{8,10},{9,11},{10,... | collective-permute-start | bytes 202760 | tf_op jit(solution)/shard_map/ppermute | solution.py:28
  30.9 5.4 %shard_map.122 = (f32[256,128]{1,0:T(8,128)S(1)}, s16[264,128]{1,0:T(8,128)(2,1)S(1)}, s16[264,128]{1,0:T(8,128)(2,1)S(1)}, s16[264,128]{1,0:T(8,128)(2,1)S(1)}, bf16[1024,1024]{1,0:T(8,128)(2,1)S(1)}) custom-call(s32[16]{0:T(128)S(1)} %get-tuple-element.45.blocks_ref, s32[16]{0:T(128)S(1)} %get-tuple-element.47.tiles_ref, s32[2]{0:T(128)S(1)} %pad_add_fusion.where_ref, ...), custom_call_target="tpu_custom_call" | custom-call | flops 268435456 | bytes 2097152 | tf_op jit(solution)/shard_map/pallas_call | solution.py:258
  37.0 3.5 %collective-permute-start.8 = (s16[264,128]{1,0:T(8,128)(2,1)S(1)}, s16[264,128]{1,0:T(8,128)(2,1)S(1)}, u32[]{:S(2)}, u32[]{:S(2)}) collective-permute-start(s16[264,128]{1,0:T(8,128)(2,1)S(1)} %get-tuple-element.51), channel_id=1, source_target_pairs={{0,2},{1,3},{2,0},{3,1},{4,6},{5,7},{6,4},{7,5},{8,10},{9,11},{10,... | collective-permute-start | bytes 202760 | tf_op jit(solution)/shard_map/ppermute | solution.py:28
  42.4 3.8 %collective-permute-start.16 = (bf16[256,128]{1,0:T(8,128)(2,1)S(1)}, bf16[256,128]{1,0:T(8,128)(2,1)S(1)}, u32[]{:S(2)}, u32[]{:S(2)}) collective-permute-start(bf16[256,128]{1,0:T(8,128)(2,1)S(1)} %shard_map.125.refs_1_), channel_id=1, source_target_pairs={{0,2},{1,3},{2,0},{3,1},{4,6},{5,7},{6,4},{7,5},{8,10},{9,11},{10,... | collective-permute-start | bytes 196616 | tf_op jit(solution)/shard_map/ppermute | solution.py:28
  49.5 2.5 %collective-permute-start.15 = (bf16[256,128]{1,0:T(8,128)(2,1)S(1)}, bf16[256,128]{1,0:T(8,128)(2,1)S(1)}, u32[]{:S(2)}, u32[]{:S(2)}) collective-permute-start(bf16[256,128]{1,0:T(8,128)(2,1)S(1)} %shard_map.123.refs_0_), channel_id=1, source_target_pairs={{0,2},{1,3},{2,0},{3,1},{4,6},{5,7},{6,4},{7,5},{8,10},{9,11},{10,... | collective-permute-start | bytes 196616 | tf_op jit(solution)/shard_map/ppermute | solution.py:28
  53.2 2.6 %shard_map.126.refs_2_ = bf16[2,1792,512]{2,1,0:T(8,128)(2,1)S(1)} custom-call(s32[2]{0:T(128)S(1)} %pad_add_fusion.where_ref, bf16[1792,4096]{1,0:T(8,128)(2,1)} %refs_1_.1), custom_call_target="tpu_custom_call" | custom-call | bytes 3670016 | tf_op jit(solution)/shard_map/pallas_call | solution.py:258
  56.2 1.9 %collective-permute-done.17.refs_6_ = bf16[256,128]{1,0:T(8,128)(2,1)S(1)} collective-permute-done((bf16[256,128]{1,0:T(8,128)(2,1)S(1)}, bf16[256,128]{1,0:T(8,128)(2,1)S(1)}, u32[]{:S(2)}, u32[]{:S(2)}) %collective-permute-start.17) | collective-permute-done | bytes 65568 | tf_op jit(solution)/shard_map/ppermute | solution.py:28
  58.1 1.7 %shard_map.128 = (f32[512,512]{1,0:T(8,128)S(1)}, f32[512,512]{1,0:T(8,128)S(1)}) custom-call(s32[16]{0:T(128)S(1)} %get-tuple-element.45.blocks_ref, s32[2]{0:T(128)S(1)} %pad_add_fusion.where_ref, bf16[256,128]{1,0:T(8,128)(2,1)S(1)} %shard_map.123.refs_0_, bf16[256,128]{1,0:T(8,128)(2,1)S(1)} %shard_map.125.refs_1_, ...), custom_call_target="tpu_custom_call" | custom-call | flops 268435456 | bytes 4194304 | tf_op jit(solution)/shard_map/pallas_call | solution.py:258
  59.8 1.7 %shard_map.127 = (f32[512,512]{1,0:T(8,128)S(1)}, f32[512,512]{1,0:T(8,128)S(1)}) custom-call(s32[16]{0:T(128)S(1)} %get-tuple-element.45.blocks_ref, s32[2]{0:T(128)S(1)} %pad_add_fusion.where_ref, bf16[256,128]{1,0:T(8,128)(2,1)S(1)} %shard_map.123.refs_0_, bf16[256,128]{1,0:T(8,128)(2,1)S(1)} %shard_map.125.refs_1_, ...), custom_call_target="tpu_custom_call" | custom-call | flops 268435456 | bytes 4194304 | tf_op jit(solution)/shard_map/pallas_call | solution.py:258
  64.6 1.6 %collective-permute-start.22 = (s16[136,512]{1,0:T(8,128)(2,1)S(1)}, s16[136,512]{1,0:T(8,128)(2,1)S(1)}, u32[]{:S(2)}, u32[]{:S(2)}) collective-permute-start(s16[136,512]{1,0:T(8,128)(2,1)S(1)} %get-tuple-element.70), channel_id=1, source_target_pairs={{0,24},{4,28},{8,16},{12,20},{16,8},{20,12},{24,0},{28,4},{1,25},{... | collective-permute-start | bytes 417800 | tf_op jit(solution)/shard_map/ppermute | solution.py:28
  66.2 3.1 %collective-permute-done.20.refs_0_ = s16[136,512]{1,0:T(8,128)(2,1)S(1)} collective-permute-done((s16[136,512]{1,0:T(8,128)(2,1)S(1)}, s16[136,512]{1,0:T(8,128)(2,1)S(1)}, u32[]{:S(2)}, u32[]{:S(2)}) %collective-permute-start.20) | collective-permute-done | bytes 139296 | tf_op jit(solution)/shard_map/ppermute | solution.py:28
  70.8 1.8 %collective-permute-done.22.refs_2_ = s16[136,512]{1,0:T(8,128)(2,1)S(1)} collective-permute-done((s16[136,512]{1,0:T(8,128)(2,1)S(1)}, s16[136,512]{1,0:T(8,128)(2,1)S(1)}, u32[]{:S(2)}, u32[]{:S(2)}) %collective-permute-start.22) | collective-permute-done | bytes 139296 | tf_op jit(solution)/shard_map/ppermute | solution.py:28
  77.9 2.8 %collective-permute-done.31.refs_1_ = bf16[128,512]{1,0:T(8,128)(2,1)S(1)} collective-permute-done((bf16[128,512]{1,0:T(8,128)(2,1)S(1)}, bf16[128,512]{1,0:T(8,128)(2,1)S(1)}, u32[]{:S(2)}, u32[]{:S(2)}) %collective-permute-start.31) | collective-permute-done | bytes 131104 | tf_op jit(solution)/shard_map/ppermute | solution.py:28
  82.9 3.1 %collective-permute-start.29 = (bf16[128,512]{1,0:T(8,128)(2,1)S(1)}, bf16[128,512]{1,0:T(8,128)(2,1)S(1)}, u32[]{:S(2)}, u32[]{:S(2)}) collective-permute-start(bf16[128,512]{1,0:T(8,128)(2,1)S(1)} %shard_map.132.refs_1_), channel_id=1, source_target_pairs={{0,1},{1,0},{2,3},{3,2},{4,5},{5,4},{6,7},{7,6},{8,9},{9,8},{10,11... | collective-permute-start | bytes 393224 | tf_op jit(solution)/shard_map/ppermute | solution.py:28
  86.3 2.2 %collective-permute-start.28 = (bf16[128,512]{1,0:T(8,128)(2,1)S(1)}, bf16[128,512]{1,0:T(8,128)(2,1)S(1)}, u32[]{:S(2)}, u32[]{:S(2)}) collective-permute-start(bf16[128,512]{1,0:T(8,128)(2,1)S(1)} %shard_map.132.refs_1_), channel_id=1, source_target_pairs={{0,3},{1,2},{2,1},{3,0},{4,7},{5,6},{6,5},{7,4},{8,11},{9,10},{10,... | collective-permute-start | bytes 393224 | tf_op jit(solution)/shard_map/ppermute | solution.py:28
  88.5 3.6 %shard_map.133 = (f32[128,1792]{1,0:T(8,128)S(1)}, bf16[128,1024]{1,0:T(8,128)(2,1)}) custom-call(s32[2]{0:T(128)S(1)} %pad_add_fusion.where_ref, bf16[128,512]{1,0:T(8,128)(2,1)S(1)} %shard_map.130.refs_0_, bf16[128,512]{1,0:T(8,128)(2,1)S(1)} %shard_map.132.refs_1_, bf16[1792,4096]{1,0:T(8,128)(2,1)} %refs_1_.1), custom_call_target="tpu_custom_call" | custom-call | flops 469762048 | bytes 3670016 | tf_op jit(solution)/shard_map/pallas_call | solution.py:258
  92.2 4.4 %shard_map.134.refs_2_ = f32[128,1792]{1,0:T(8,128)S(1)} custom-call(s32[2]{0:T(128)S(1)} %pad_add_fusion.where_ref, bf16[128,512]{1,0:T(8,128)(2,1)S(1)} %collective-permute-done.30.refs_0_, bf16[128,512]{1,0:T(8,128)(2,1)S(1)} %collective-permute-done.31.refs_1_, bf16[128,512]{1,0:T(8,128)(2,1)S(1)} %collective-permute-done.32.refs_2_, ...), custom_call_target="tpu_custom_call" | custom-call | flops 704643072 | bytes 5505024 | tf_op jit(solution)/shard_map/pallas_call | solution.py:258
  96.6 2.7 %shard_map.135.refs_3_ = f32[128,1792]{1,0:T(8,128)S(1)} custom-call(s32[2]{0:T(128)S(1)} %pad_add_fusion.where_ref, bf16[128,512]{1,0:T(8,128)(2,1)S(1)} %collective-permute-done.29.refs_0_, bf16[1792,4096]{1,0:T(8,128)(2,1)} %refs_1_.1, f32[128,1792]{1,0:T(8,128)S(1)} %shard_map.134.refs_2_), custom_call_target="tpu_custom_call" | custom-call | flops 234881024 | bytes 1835008 | tf_op jit(solution)/shard_map/pallas_call | solution.py:258
  99.4 2.9 %shard_map.136 = (bf16[128,1792]{1,0:T(8,128)(2,1)}, bf16[128,1792]{1,0:T(8,128)(2,1)}) custom-call(s32[2]{0:T(128)S(1)} %pad_add_fusion.where_ref, bf16[128,512]{1,0:T(8,128)(2,1)S(1)} %collective-permute-done.27.refs_0_, bf16[128,512]{1,0:T(8,128)(2,1)S(1)} %collective-permute-done.28.refs_1_, bf16[2,1792,512]{2,1,0:T(8,128)(2,1)S(1)} %shard_map.126.refs_2_, ...), custom_call_target="tpu_custom_call" | custom-call | flops 469762048 | bytes 3670016 | tf_op jit(solution)/shard_map/pallas_call | solution.py:258
  (87 shorter events, 26.2 us)
Async XLA Ops:
  0.6 14.8 %collective-permute-start = (bf16[128,1024]{1,0:T(8,128)(2,1)}, bf16[128,1024]{1,0:T(8,128)(2,1)}, u32[]{:S(2)}, u32[]{:S(2)}) collective-permute-start(bf16[128,1024]{1,0:T(8,128)(2,1)} %refs_0_.3), channel_id=1, source_target_pairs={{0,8},{4,12},{8,0},{12,4},{16,24},{20,28},{24,16},{28,20},{1,9},{5... | collective-permute-start | bytes 786440 | tf_op jit(solution)/shard_map/ppermute | solution.py:28
  3.7 13.7 %collective-permute-start.3 = (bf16[128,1024]{1,0:T(8,128)(2,1)}, bf16[128,1024]{1,0:T(8,128)(2,1)}, u32[]{:S(2)}, u32[]{:S(2)}) collective-permute-start(bf16[128,1024]{1,0:T(8,128)(2,1)} %refs_0_.3), channel_id=1, source_target_pairs={{0,16},{4,20},{8,24},{12,28},{16,0},{20,4},{24,8},{28,12},{1,17},{... | collective-permute-start | bytes 786440 | tf_op jit(solution)/shard_map/ppermute | solution.py:28
  5.2 12.2 %collective-permute-start.5 = (bf16[128,1024]{1,0:T(8,128)(2,1)}, bf16[128,1024]{1,0:T(8,128)(2,1)}, u32[]{:S(2)}, u32[]{:S(2)}) collective-permute-start(bf16[128,1024]{1,0:T(8,128)(2,1)} %refs_0_.3), channel_id=1, source_target_pairs={{0,24},{4,28},{8,16},{12,20},{16,8},{20,12},{24,0},{28,4},{1,25},{... | collective-permute-start | bytes 786440 | tf_op jit(solution)/shard_map/ppermute | solution.py:28
  5.2 15.7 %collective-permute-start.1 = (bf16[128,1024]{1,0:T(8,128)(2,1)}, bf16[128,1024]{1,0:T(8,128)(2,1)}, u32[]{:S(2)}, u32[]{:S(2)}) collective-permute-start(bf16[128,1024]{1,0:T(8,128)(2,1)} %refs_0_.3), channel_id=1, source_target_pairs={{0,4},{4,0},{8,12},{12,8},{16,20},{20,16},{24,28},{28,24},{1,5},{5... | collective-permute-start | bytes 786440 | tf_op jit(solution)/shard_map/ppermute | solution.py:28
  26.4 14.1 %collective-permute-start.10 = (s16[264,128]{1,0:T(8,128)(2,1)S(1)}, s16[264,128]{1,0:T(8,128)(2,1)S(1)}, u32[]{:S(2)}, u32[]{:S(2)}) collective-permute-start(s16[264,128]{1,0:T(8,128)(2,1)S(1)} %get-tuple-element.56), channel_id=1, source_target_pairs={{0,1},{1,0},{2,3},{3,2},{4,5},{5,4},{6,7},{7,6},{8,9},{9,8},{10,11... | collective-permute-start | bytes 202760 | tf_op jit(solution)/shard_map/ppermute | solution.py:28
  28.0 12.7 %collective-permute-start.11 = (s16[264,128]{1,0:T(8,128)(2,1)S(1)}, s16[264,128]{1,0:T(8,128)(2,1)S(1)}, u32[]{:S(2)}, u32[]{:S(2)}) collective-permute-start(s16[264,128]{1,0:T(8,128)(2,1)S(1)} %get-tuple-element.57), channel_id=1, source_target_pairs={{0,2},{1,3},{2,0},{3,1},{4,6},{5,7},{6,4},{7,5},{8,10},{9,11},{10,... | collective-permute-start | bytes 202760 | tf_op jit(solution)/shard_map/ppermute | solution.py:28
  30.6 10.1 %collective-permute-start.12 = (s16[264,128]{1,0:T(8,128)(2,1)S(1)}, s16[264,128]{1,0:T(8,128)(2,1)S(1)}, u32[]{:S(2)}, u32[]{:S(2)}) collective-permute-start(s16[264,128]{1,0:T(8,128)(2,1)S(1)} %get-tuple-element.58), channel_id=1, source_target_pairs={{0,3},{1,2},{2,1},{3,0},{4,7},{5,6},{6,5},{7,4},{8,11},{9,10},{10,... | collective-permute-start | bytes 202760 | tf_op jit(solution)/shard_map/ppermute | solution.py:28
  36.2 10.0 %collective-permute-start.7 = (s16[264,128]{1,0:T(8,128)(2,1)S(1)}, s16[264,128]{1,0:T(8,128)(2,1)S(1)}, u32[]{:S(2)}, u32[]{:S(2)}) collective-permute-start(s16[264,128]{1,0:T(8,128)(2,1)S(1)} %get-tuple-element.50), channel_id=1, source_target_pairs={{0,1},{1,0},{2,3},{3,2},{4,5},{5,4},{6,7},{7,6},{8,9},{9,8},{10,11... | collective-permute-start | bytes 202760 | tf_op jit(solution)/shard_map/ppermute | solution.py:28
  37.0 9.5 %collective-permute-start.8 = (s16[264,128]{1,0:T(8,128)(2,1)S(1)}, s16[264,128]{1,0:T(8,128)(2,1)S(1)}, u32[]{:S(2)}, u32[]{:S(2)}) collective-permute-start(s16[264,128]{1,0:T(8,128)(2,1)S(1)} %get-tuple-element.51), channel_id=1, source_target_pairs={{0,2},{1,3},{2,0},{3,1},{4,6},{5,7},{6,4},{7,5},{8,10},{9,11},{10,... | collective-permute-start | bytes 202760 | tf_op jit(solution)/shard_map/ppermute | solution.py:28
  42.0 10.0 %collective-permute-start.14 = (bf16[256,128]{1,0:T(8,128)(2,1)S(1)}, bf16[256,128]{1,0:T(8,128)(2,1)S(1)}, u32[]{:S(2)}, u32[]{:S(2)}) collective-permute-start(bf16[256,128]{1,0:T(8,128)(2,1)S(1)} %shard_map.125.refs_1_), channel_id=1, source_target_pairs={{0,1},{1,0},{2,3},{3,2},{4,5},{5,4},{6,7},{7,6},{8,9},{9,8},{10,11... | collective-permute-start | bytes 196616 | tf_op jit(solution)/shard_map/ppermute | solution.py:28
  42.4 13.4 %collective-permute-start.16 = (bf16[256,128]{1,0:T(8,128)(2,1)S(1)}, bf16[256,128]{1,0:T(8,128)(2,1)S(1)}, u32[]{:S(2)}, u32[]{:S(2)}) collective-permute-start(bf16[256,128]{1,0:T(8,128)(2,1)S(1)} %shard_map.125.refs_1_), channel_id=1, source_target_pairs={{0,2},{1,3},{2,0},{3,1},{4,6},{5,7},{6,4},{7,5},{8,10},{9,11},{10,... | collective-permute-start | bytes 196616 | tf_op jit(solution)/shard_map/ppermute | solution.py:28
  46.2 9.6 %collective-permute-start.18 = (bf16[256,128]{1,0:T(8,128)(2,1)S(1)}, bf16[256,128]{1,0:T(8,128)(2,1)S(1)}, u32[]{:S(2)}, u32[]{:S(2)}) collective-permute-start(bf16[256,128]{1,0:T(8,128)(2,1)S(1)} %shard_map.125.refs_1_), channel_id=1, source_target_pairs={{0,3},{1,2},{2,1},{3,0},{4,7},{5,6},{6,5},{7,4},{8,11},{9,10},{10,... | collective-permute-start | bytes 196616 | tf_op jit(solution)/shard_map/ppermute | solution.py:28
  61.5 11.2 %collective-permute-start.23 = (f32[512,512]{1,0:T(8,128)S(1)}, f32[512,512]{1,0:T(8,128)S(1)}, u32[]{:S(2)}, u32[]{:S(2)}) collective-permute-start(f32[512,512]{1,0:T(8,128)S(1)} %get-tuple-element.73), channel_id=1, source_target_pairs={{0,4},{4,0},{8,12},{12,8},{16,20},{20,16},{24,28},{28,24},{1,5},{5... | collective-permute-start | bytes 3145736 | tf_op jit(solution)/shard_map/ppermute | solution.py:28
  63.3 7.5 %collective-permute-start.21 = (s16[136,512]{1,0:T(8,128)(2,1)S(1)}, s16[136,512]{1,0:T(8,128)(2,1)S(1)}, u32[]{:S(2)}, u32[]{:S(2)}) collective-permute-start(s16[136,512]{1,0:T(8,128)(2,1)S(1)} %get-tuple-element.69), channel_id=1, source_target_pairs={{0,16},{4,20},{8,24},{12,28},{16,0},{20,4},{24,8},{28,12},{1,17},{... | collective-permute-start | bytes 417800 | tf_op jit(solution)/shard_map/ppermute | solution.py:28
  64.6 8.0 %collective-permute-start.22 = (s16[136,512]{1,0:T(8,128)(2,1)S(1)}, s16[136,512]{1,0:T(8,128)(2,1)S(1)}, u32[]{:S(2)}, u32[]{:S(2)}) collective-permute-start(s16[136,512]{1,0:T(8,128)(2,1)S(1)} %get-tuple-element.70), channel_id=1, source_target_pairs={{0,24},{4,28},{8,16},{12,20},{16,8},{20,12},{24,0},{28,4},{1,25},{... | collective-permute-start | bytes 417800 | tf_op jit(solution)/shard_map/ppermute | solution.py:28
  73.0 8.3 %collective-permute-start.24 = (s16[136,512]{1,0:T(8,128)(2,1)S(1)}, s16[136,512]{1,0:T(8,128)(2,1)S(1)}, u32[]{:S(2)}, u32[]{:S(2)}) collective-permute-start(s16[136,512]{1,0:T(8,128)(2,1)S(1)} %get-tuple-element.75), channel_id=1, source_target_pairs={{0,8},{4,12},{8,0},{12,4},{16,24},{20,28},{24,16},{28,20},{1,9},{5... | collective-permute-start | bytes 417800 | tf_op jit(solution)/shard_map/ppermute | solution.py:28
  74.9 7.9 %collective-permute-start.25 = (s16[136,512]{1,0:T(8,128)(2,1)S(1)}, s16[136,512]{1,0:T(8,128)(2,1)S(1)}, u32[]{:S(2)}, u32[]{:S(2)}) collective-permute-start(s16[136,512]{1,0:T(8,128)(2,1)S(1)} %get-tuple-element.76), channel_id=1, source_target_pairs={{0,16},{4,20},{8,24},{12,28},{16,0},{20,4},{24,8},{28,12},{1,17},{... | collective-permute-start | bytes 417800 | tf_op jit(solution)/shard_map/ppermute | solution.py:28
  75.6 7.2 %collective-permute-start.26 = (s16[136,512]{1,0:T(8,128)(2,1)S(1)}, s16[136,512]{1,0:T(8,128)(2,1)S(1)}, u32[]{:S(2)}, u32[]{:S(2)}) collective-permute-start(s16[136,512]{1,0:T(8,128)(2,1)S(1)} %get-tuple-element.77), channel_id=1, source_target_pairs={{0,24},{4,28},{8,16},{12,20},{16,8},{20,12},{24,0},{28,4},{1,25},{... | collective-permute-start | bytes 417800 | tf_op jit(solution)/shard_map/ppermute | solution.py:28
  76.8 9.5 %collective-permute-start.30 = (bf16[128,512]{1,0:T(8,128)(2,1)S(1)}, bf16[128,512]{1,0:T(8,128)(2,1)S(1)}, u32[]{:S(2)}, u32[]{:S(2)}) collective-permute-start(bf16[128,512]{1,0:T(8,128)(2,1)S(1)} %shard_map.130.refs_0_), channel_id=1, source_target_pairs={{0,1},{1,0},{2,3},{3,2},{4,5},{5,4},{6,7},{7,6},{8,9},{9,8},{10,11... | collective-permute-start | bytes 393224 | tf_op jit(solution)/shard_map/ppermute | solution.py:28
  80.6 11.5 %collective-permute-start.32 = (bf16[128,512]{1,0:T(8,128)(2,1)S(1)}, bf16[128,512]{1,0:T(8,128)(2,1)S(1)}, u32[]{:S(2)}, u32[]{:S(2)}) collective-permute-start(bf16[128,512]{1,0:T(8,128)(2,1)S(1)} %shard_map.130.refs_0_), channel_id=1, source_target_pairs={{1,2},{2,1},{5,6},{6,5},{9,10},{10,9},{13,14},{14,13},{17,18},{18,... | collective-permute-start | bytes 393224 | tf_op jit(solution)/shard_map/ppermute | solution.py:408
  81.3 10.9 %collective-permute-start.33 = (bf16[128,512]{1,0:T(8,128)(2,1)S(1)}, bf16[128,512]{1,0:T(8,128)(2,1)S(1)}, u32[]{:S(2)}, u32[]{:S(2)}) collective-permute-start(bf16[128,512]{1,0:T(8,128)(2,1)S(1)} %collective-permute-done.31.refs_1_), channel_id=1, source_target_pairs={{1,0},{2,3},{5,4},{6,7},{9,8},{10,11},{13,12},{14,15},{17,16},{18,... | collective-permute-start | bytes 393224 | tf_op jit(solution)/shard_map/ppermute | solution.py:409
  82.9 13.7 %collective-permute-start.29 = (bf16[128,512]{1,0:T(8,128)(2,1)S(1)}, bf16[128,512]{1,0:T(8,128)(2,1)S(1)}, u32[]{:S(2)}, u32[]{:S(2)}) collective-permute-start(bf16[128,512]{1,0:T(8,128)(2,1)S(1)} %shard_map.132.refs_1_), channel_id=1, source_target_pairs={{0,1},{1,0},{2,3},{3,2},{4,5},{5,4},{6,7},{7,6},{8,9},{9,8},{10,11... | collective-permute-start | bytes 393224 | tf_op jit(solution)/shard_map/ppermute | solution.py:28
  86.1 13.2 %collective-permute-start.27 = (bf16[128,512]{1,0:T(8,128)(2,1)S(1)}, bf16[128,512]{1,0:T(8,128)(2,1)S(1)}, u32[]{:S(2)}, u32[]{:S(2)}) collective-permute-start(bf16[128,512]{1,0:T(8,128)(2,1)S(1)} %shard_map.132.refs_1_), channel_id=1, source_target_pairs={{0,2},{1,3},{2,0},{3,1},{4,6},{5,7},{6,4},{7,5},{8,10},{9,11},{10,... | collective-permute-start | bytes 393224 | tf_op jit(solution)/shard_map/ppermute | solution.py:28
  86.3 13.0 %collective-permute-start.28 = (bf16[128,512]{1,0:T(8,128)(2,1)S(1)}, bf16[128,512]{1,0:T(8,128)(2,1)S(1)}, u32[]{:S(2)}, u32[]{:S(2)}) collective-permute-start(bf16[128,512]{1,0:T(8,128)(2,1)S(1)} %shard_map.132.refs_1_), channel_id=1, source_target_pairs={{0,3},{1,2},{2,1},{3,0},{4,7},{5,6},{6,5},{7,4},{8,11},{9,10},{10,... | collective-permute-start | bytes 393224 | tf_op jit(solution)/shard_map/ppermute | solution.py:28
  (19 other events, 148.3 us)
where the time goes:
time: 102 us
  starting transfers between devices  40.3 us (40%)
  Pallas kernels  35 us (34%)
  waiting for transfers between devices  14.1 us (14%)
  local copies, waits for them, and re-layouts  11.1 us (11%)
  between operations  1.04 us (1%)
    ppermute x32, starting transfers between devices, swap(): return lax.ppermute(x, axis, [(i, i ^ mask) for i in range(size)])  38.1 us
    pallas_call x16, Pallas kernels, call(): pl.pallas_call(kernel, out_shape=outs, in_specs=ins, out_specs=[SMEM] * s...  35 us
    ppermute x32, waiting for transfers between devices, swap(): return lax.ppermute(x, axis, [(i, i ^ mask) for i in range(size)])  14.1 us
    gather x1, local copies, waits for them, and re-layouts, on_device(): target_rows = head_weight.at[clipped].get(mode='promise_in_bounds')  9.48 us
  transfers between devices with their start and end apart: 34, of which 9 were waited for; matrix products, arithmetic and copies ran while one was open for 12% of the time, Pallas kernels for 24%

commit v1 on v0

v1 whole, which is shorter than its diff:
```python
import functools

import jax
import jax.numpy as jnp
from jax import lax
from jax.experimental import pallas as pl
from jax.experimental.pallas import tpu as pltpu
from jax.sharding import PartitionSpec as P


TILE = 128
PAD = 8
GROUPS = 2
HALVES = 2
LARGE = 50
MEDIUM = 46
LEVELS = 32767.0
VMEM = pl.BlockSpec(memory_space=pltpu.VMEM)
SMEM = pl.BlockSpec(memory_space=pltpu.SMEM)
ANY = pl.BlockSpec(memory_space=pl.ANY)
HBM = pl.BlockSpec(memory_space=pltpu.HBM)


def swap(x, axis, mask):
    if mask == 0:
        return x
    size = lax.axis_size(axis)
    return lax.ppermute(x, axis, [(i, i ^ mask) for i in range(size)])


def step_of(code):
    return jnp.exp2(code * 0.125) * (1.0 / LEVELS)


def encode(x):
    peak = jnp.max(jnp.abs(x), axis=0, keepdims=True)
    code = jnp.ceil(8.0 * jnp.log2(jnp.maximum(peak, 1e-30)) + 0.25)
    levels = jnp.round(x * (1.0 / step_of(code)))
    return levels.astype(jnp.int32).astype(jnp.int16), code.astype(jnp.int32)


def decode(levels, code):
    return levels.astype(jnp.int32).astype(jnp.float32) * step_of(code.astype(jnp.float32))


def tiles_kernel(slots, tiles_ref, counts_ref, head, blocks_out, tiles_out, live_out, out, sem):
    blocks, _, per_block = tiles_ref.shape

    def copy(tile, slot):
        return pltpu.make_async_copy(
            head.at[pl.ds(pl.multiple_of(tile * TILE, TILE), TILE), :],
            out.at[pl.ds(pl.multiple_of(slot * TILE, TILE), TILE), :],
            sem.at[slot],
        )

    def place(slot, block, tile):
        blocks_out[slot] = block
        tiles_out[slot] = tile
        copy(tile, slot).start()

    live = jnp.int32(0)
    for block in range(blocks):
        count = counts_ref[block, 0]
        for j in range(per_block):
            pl.when(j < count)(
                functools.partial(place, live + j, block, tiles_ref[block, 0, j])
            )
        live = live + count
    live_out[0] = live
    for slot in range(slots):
        pl.when(slot >= live)(functools.partial(place, slot, 0, 0))
    for slot in range(slots):
        copy(0, slot).wait()


def logits_kernel(wide, narrow, slots, group, blocks_ref, where_ref, tiles, *refs):
    me_w, me_n = where_ref[0], where_ref[1]
    per = slots // narrow
    share = per // GROUPS
    parts, own, sends = refs[:wide], refs[wide], refs[wide + 1 : wide + narrow]
    rows, sem = refs[wide + narrow :]
    copies = [pltpu.make_async_copy(parts[k], rows.at[k], sem.at[k]) for k in range(wide)]
    for copy in copies:
        copy.start()
    for send in sends:
        send[share * TILE :, :] = jnp.zeros((send.shape[0] - share * TILE, TILE), jnp.int16)
    for copy in copies:
        copy.wait()
    for k in [*range(1, narrow), 0]:
        for i in range(share):
            slot = (me_n ^ k) * per + group * share + i
            part = lax.dot_general(
                rows[blocks_ref[slot] ^ me_w],
                tiles[pl.ds(pl.multiple_of(slot * TILE, TILE), TILE), :],
                (((1,), (1,)), ((), ())),
                preferred_element_type=jnp.float32,
            )
            if k == 0:
                own[i * TILE : (i + 1) * TILE, :] = part
            else:
                levels, code = encode(part)
                sends[k - 1][i * TILE : (i + 1) * TILE, :] = levels
                sends[k - 1][share * TILE + i : share * TILE + i + 1, :] = code.astype(jnp.int16)


def probs_kernel(narrow, slots, group, blocks_ref, live_ref, where_ref, own, *refs):
    recvs, lse, weight, out = refs[: narrow - 1], refs[-3], refs[-2], refs[-1]
    per = slots // narrow
    share = per // GROUPS
    codes = [recv[share * TILE :, :] for recv in recvs]
    for i in range(share):
        slot = where_ref[1] * per + group * share + i
        total = own[i * TILE : (i + 1) * TILE, :]
        for recv, code in zip(recvs, codes):
            total = total + decode(recv[i * TILE : (i + 1) * TILE, :], code[i : i + 1, :])
        rows = pl.ds(pl.multiple_of(blocks_ref[slot] * TILE, TILE), TILE)
        scaled = jnp.exp(total - lse[rows, :]) * weight[rows, :]
        out[i * TILE : (i + 1) * TILE, :] = jnp.where(slot < live_ref[0], scaled, 0.0).astype(
            jnp.bfloat16
        )


def grads_kernel(wide, narrow, slots, half, blocks_ref, tiles_ref, where_ref, head, *refs):
    probs = refs[: narrow * GROUPS]
    target_rows, factor, mine, other, total, tiles, sem = refs[narrow * GROUPS :]
    me_w, me_n = where_ref[0], where_ref[1]
    per = slots // narrow
    share = per // GROUPS
    width = mine.shape[1]

    def fetch(slot):
        start = pl.multiple_of(tiles_ref[slot] * TILE, TILE)
        part = head.at[pl.ds(start, TILE), pl.ds(half * width, width)]
        return pltpu.make_async_copy(part, tiles.at[slot], sem.at[slot])

    for slot in range(slots):
        fetch(slot).start()
    for block in range(factor.shape[0] // TILE):
        rows = slice(block * TILE, (block + 1) * TILE)
        weight = -factor[rows, :]
        for lane in range(0, width, TILE):
            at = half * width + lane
            total[block ^ me_w, :, lane : lane + TILE] = weight * target_rows[
                rows, at : at + TILE
            ].astype(jnp.float32)
    for slot in range(slots):
        fetch(slot).wait()
    for k in range(narrow):
        for group in range(GROUPS):
            for i in range(share):
                slot = (me_n ^ k) * per + group * share + i
                total[blocks_ref[slot] ^ me_w] += jnp.dot(
                    probs[k * GROUPS + group][i * TILE : (i + 1) * TILE, :],
                    tiles[slot],
                    preferred_element_type=jnp.float32,
                )
    for chip in range(wide // 2):
        mine[chip * TILE : (chip + 1) * TILE, :] = total[2 * chip]
        other[chip * TILE : (chip + 1) * TILE, :] = total[2 * chip + 1]


def pack_kernel(chips, mine, other, own, *sends):
    for chip in [*range(1, chips), 0]:
        rows = slice(chip * TILE, (chip + 1) * TILE)
        if chip == 0:
            own[...] = mine[rows, :] + other[rows, :]
            continue
        send = sends[chip - 1]
        for lane in range(0, own.shape[1], TILE):
            lanes = slice(lane, lane + TILE)
            levels, code = encode(mine[rows, lanes] + other[rows, lanes])
            send[:TILE, lanes] = levels
            send[TILE:, lanes] = jnp.broadcast_to(code, (PAD, TILE)).astype(jnp.int16)


def merge_kernel(chips, before, own, *refs):
    recvs, befores, outs = refs[: chips - 1], refs[chips - 1 : chips - 1 + before], refs[-1 - before :]
    width = own.shape[1]
    for lane in range(0, width, TILE):
        lanes = slice(lane, lane + TILE)
        total = own[:, lanes]
        for recv in recvs:
            total = total + decode(recv[:TILE, lanes], recv[TILE : TILE + 1, lanes])
        outs[0][:, lanes] = total.astype(jnp.bfloat16)
    if before:
        for at, part in enumerate([*befores, outs[0]]):
            outs[1][:, at * width : (at + 1) * width] = part[...]


def down_copies(keys, where_ref, down, out, sem, rows):
    width = out.shape[-1]

    def copy(at):
        mask, half = keys[at]
        start = pl.multiple_of((where_ref[1] ^ mask) * (width * HALVES) + half * width, width)
        return pltpu.make_async_copy(down.at[rows, pl.ds(start, width)], out.at[at], sem.at[at])

    return [copy(at) for at in range(len(keys))]


def hold_kernel(keys, where_ref, down, out, sem):
    copies = down_copies(keys, where_ref, down, out, sem, slice(None))
    for copy in copies:
        copy.start()
    for copy in copies:
        copy.wait()


def unit_kernel(keys, splits, kind, chunk, skip, where_ref, *refs):
    count, inputs = len(keys), sum(splits)
    arrived, down, refs = list(refs[:inputs]), refs[inputs], list(refs[inputs + 1 :])
    units = down.shape[-2]
    pieces = []
    for split in splits:
        piece = arrived.pop(0)[...]
        for _ in range(split - 1):
            piece = piece + arrived.pop(0)[...]
        pieces.append(piece)
    summed = None if kind == "first" else refs.pop(0)
    if kind == "last":
        gate, up, gate_out, up_out = refs[:4]
    else:
        sum_out = refs[0]
    steps = [pl.ds(at, chunk) for at in range(0, units, chunk)]
    if skip is None:
        down_v, sem = refs[-2:]
        copies = [
            down_copies(keys, where_ref, down, down_v.at[step], sem.at[step], rows)
            for step, rows in enumerate(steps)
        ]
        for copy in sum(copies, []):
            copy.start()
    for step, rows in enumerate(steps):
        total = None if summed is None else summed[:, rows]
        for at in range(count):
            if skip is None:
                copies[step][at].wait()
            part = lax.dot_general(
                pieces[at],
                down_v[step, at] if skip is None else down[skip + at, rows, :],
                (((1,), (1,)), ((), ())),
                preferred_element_type=jnp.float32,
            )
            total = part if total is None else total + part
        if kind != "last":
            sum_out[:, rows] = total
            continue
        g = gate[:, rows].astype(jnp.float32)
        u = up[:, rows].astype(jnp.float32)
        s = 1.0 / (1.0 + jnp.exp(-g))
        up_out[:, rows] = (total * g * s).astype(jnp.bfloat16)
        gate_out[:, rows] = (total * u * s * (1.0 + g * (1.0 - s))).astype(jnp.bfloat16)


def shape_of(shape, dtype):
    return jax.ShapeDtypeStruct(shape, dtype)


def call(kernel, outs, ins, args, flops, moved, scratch=(), mib=16, scalars=0):
    return pl.pallas_call(
        kernel,
        out_shape=outs,
        in_specs=ins,
        out_specs=[SMEM] * scalars + [VMEM] * (len(outs) - scalars),
        scratch_shapes=list(scratch),
        compiler_params=pltpu.CompilerParams(vmem_limit_bytes=mib * 1024 * 1024),
        cost_estimate=pl.CostEstimate(flops=flops, bytes_accessed=moved, transcendentals=0),
    )(*args)


def on_device(
    hidden,
    head_weight,
    lse,
    targets,
    loss_weight,
    block_tiles,
    block_counts,
    gate_pre,
    up_pre,
    down_weight,
):
    f32, bf16, i16 = jnp.float32, jnp.bfloat16, jnp.int16
    _, features = hidden.shape
    vocab_here = head_weight.shape[0]
    wide, narrow = lax.axis_size("wide"), lax.axis_size("narrow")
    chips = wide // 2
    me_w, me_n = lax.axis_index("wide"), lax.axis_index("narrow")
    where = jnp.stack([me_w, me_n]).astype(jnp.int32)
    blocks, per_block = block_tiles.shape[0], block_tiles.shape[2]
    slots = blocks // 2 * per_block
    share = slots // narrow // GROUPS
    width = features // HALVES

    far = [swap(hidden, "wide", 2 * chip) for chip in range(chips)]

    local_ids = targets - me_w * vocab_here
    inside = (local_ids >= 0) & (local_ids < vocab_here)
    clipped = jnp.clip(local_ids, 0, vocab_here - 1)

    def over_lanes(x):
        return jnp.broadcast_to(x[:, None], (blocks * TILE, TILE))

    lse_rows, weight_rows = over_lanes(lse), over_lanes(loss_weight)
    factor = over_lanes(jnp.where(inside, loss_weight, 0.0))
    counts, where, lse_rows, weight_rows, factor = lax.optimization_barrier(
        (block_counts, where, lse_rows, weight_rows, factor)
    )
    slot_blocks, slot_tiles, live, tiles = call(
        functools.partial(tiles_kernel, slots),
        [shape_of((slots,), jnp.int32)] * 2
        + [shape_of((1,), jnp.int32), shape_of((slots * TILE, features), bf16)],
        [SMEM, SMEM, HBM],
        (block_tiles, counts, head_weight),
        0,
        slots * TILE * features * 2,
        [pltpu.SemaphoreType.DMA((slots,))],
        MEDIUM,
        3,
    )
    far[1], tiles = lax.optimization_barrier((far[1], tiles))
    near = [swap(part, "wide", 1) for part in far]
    parts = [part for pair in zip(far, near) for part in pair]

    probs = []
    for group in range(GROUPS):
        result = call(
            functools.partial(logits_kernel, wide, narrow, slots, group),
            [shape_of((share * TILE, TILE), f32)]
            + [shape_of((share * TILE + PAD, TILE), i16)] * (narrow - 1),
            [SMEM] * 2 + [VMEM] + [ANY] * wide,
            (slot_blocks, where, tiles, *parts),
            2 * slots * TILE * TILE * features // GROUPS,
            slots * TILE * features,
            [pltpu.VMEM((wide, TILE, features), bf16), pltpu.SemaphoreType.DMA((wide,))],
        )
        own, *sends = result
        recvs = [swap(send, "narrow", k + 1) for k, send in enumerate(sends)]
        (prob,) = call(
            functools.partial(probs_kernel, narrow, slots, group),
            [shape_of((share * TILE, TILE), bf16)],
            [SMEM] * 3 + [VMEM] * (narrow + 2),
            (slot_blocks, live, where, own, *recvs, lse_rows, weight_rows),
            share * TILE * TILE * 20,
            share * TILE * TILE * 12,
        )
        if group == GROUPS - 1:
            prob, clipped = lax.optimization_barrier((prob, clipped))
        probs.append([swap(prob, "narrow", k) for k in range(narrow)])
    target_rows = head_weight.at[clipped].get(mode="promise_in_bounds")
    all_probs = [probs[group][k] for k in range(narrow) for group in range(GROUPS)]

    halves = []
    for half in range(HALVES):
        mine, other = call(
            functools.partial(grads_kernel, wide, narrow, slots, half),
            [shape_of((chips * TILE, width), f32)] * 2,
            [SMEM] * 3 + [HBM] + [VMEM] * (narrow * GROUPS + 2),
            (slot_blocks, slot_tiles, where, head_weight, *all_probs, target_rows, factor),
            2 * slots * TILE * TILE * width,
            slots * TILE * width * 4,
            [
                pltpu.VMEM((wide, TILE, width), f32),
                pltpu.VMEM((slots, TILE, width), bf16),
                pltpu.SemaphoreType.DMA((slots,)),
            ],
            MEDIUM,
        )
        halves.append((mine, swap(other, "wide", 1)))
    units = gate_pre.shape[1]
    held_keys = [(k, HALVES - 1) for k in range(1, narrow)]
    chunk = units // 2 if units // 2 % TILE == 0 else units

    def unit(keys, kind, skip, *extra):
        last = kind == "last"
        inputs = [part for key in keys for part in pieces[key]]
        count = len(keys)
        return call(
            functools.partial(
                unit_kernel, keys, [len(pieces[key]) for key in keys], kind, chunk, skip
            ),
            [shape_of((TILE, units), bf16)] * 2 if last else [shape_of((TILE, units), f32)],
            [SMEM]
            + [VMEM] * len(inputs)
            + [HBM if skip is None else VMEM]
            + [VMEM] * len(extra),
            (where, *inputs, down_weight if skip is None else held, *extra),
            2 * count * TILE * units * width,
            count * units * width * 2,
            (
                pltpu.VMEM((units // chunk, count, chunk, width), bf16),
                pltpu.SemaphoreType.DMA((units // chunk, count)),
            )
            if skip is None
            else (),
            LARGE if skip is None else 16,
        )

    pieces = {}
    grads = []
    for half, (mine, other) in enumerate(halves):
        if half > 0:
            mine, grads[-1] = lax.optimization_barrier((mine, grads[-1]))
        kept, *packed = call(
            functools.partial(pack_kernel, chips),
            [shape_of((TILE, width), f32)]
            + [shape_of((TILE + PAD, width), i16)] * (chips - 1),
            [VMEM] * 2,
            (mine, other),
            chips * TILE * width * 8,
            chips * TILE * width * 10,
        )
        arrived = [swap(part, "wide", 2 * (k + 1)) for k, part in enumerate(packed)]
        if half == 0:
            kept, here = lax.optimization_barrier((kept, where))
            (held,) = call(
                functools.partial(hold_kernel, held_keys),
                [shape_of((len(held_keys), units, width), bf16)],
                [SMEM, HBM],
                (here, down_weight),
                0,
                len(held_keys) * units * width * 2,
                [pltpu.SemaphoreType.DMA((len(held_keys),))],
                MEDIUM,
            )
            kept, held = lax.optimization_barrier((kept, held))
        if half == HALVES - 1:
            (summed,) = unit([(0, at) for at in range(half)], "first", None)
            kept, summed = lax.optimization_barrier((kept, summed))
        before = list(grads) if half == HALVES - 1 else []
        full = [shape_of((TILE, features), bf16)] if before else []
        grad, *head_grad = call(
            functools.partial(merge_kernel, chips, len(before)),
            [shape_of((TILE, width), bf16)] + full,
            [VMEM] * (chips + len(before)),
            (kept, *arrived, *before),
            chips * TILE * width * 4,
            chips * TILE * width * 3,
        )
        grads.append(grad)
        for k in range(narrow):
            pieces[k, half] = (swap(grad, "narrow", k),)

    if narrow == 4:
        near_ends = lax.ppermute(grads[0], "narrow", [(1, 2), (2, 1)])
        ends = lax.ppermute(pieces[2, 0][0], "narrow", [(1, 0), (2, 3)])
        pieces[3, 0] = (near_ends, ends)
    (summed,) = unit([(0, 1), *[(k, 0) for k in range(1, narrow)]], "more", None, summed)
    (summed,) = unit(held_keys[:1], "more", 0, summed)
    gate_grad, up_grad = unit(held_keys[1:], "last", 1, summed, gate_pre, up_pre)
    (head_grad,) = head_grad
    return head_grad, gate_grad, up_grad


def solution(mesh):
    in_specs = (
        P("wide", "narrow"),
        P("wide", "narrow"),
        P(),
        P(),
        P(),
        P(None, "wide", None),
        P(None, "wide"),
        P("wide", "narrow"),
        P("wide", "narrow"),
        P("narrow", None),
    )
    out_specs = (P("wide", "narrow"), P("wide", "narrow"), P("wide", "narrow"))

    return jax.shard_map(
        on_device, mesh=mesh, in_specs=in_specs, out_specs=out_specs, check_vma=False
    )
```

time: 102 us -> 105 us (1.029)
  local copies, waits for them, and re-layouts: 11.1 us -> 12.9 us
  starting transfers between devices: 40.3 us -> 41.9 us
    ppermute x32, starting transfers between devices: 38.1 us -> 39.8 us  [swap(): return lax.ppermute(x, axis, [(i, i ^ mask) for i in range(size)])]
  transfers between devices with their start and end apart: 34 -> 34, of which waited for: 9 -> 9; matrix products, arithmetic and copies ran while one was open for 12% -> 13% of each run, Pallas kernels for 24% -> 25%
where the time goes in v1:
time: 105 us
  starting transfers between devices  41.9 us (40%)
  Pallas kernels  34.2 us (33%)
  waiting for transfers between devices  14.2 us (14%)
  local copies, waits for them, and re-layouts  12.9 us (12%)
    ppermute x32, starting transfers between devices, swap(): return lax.ppermute(x, axis, [(i, i ^ mask) for i in range(size)])  39.8 us
    pallas_call x16, Pallas kernels, call(): pl.pallas_call(kernel, out_shape=outs, in_specs=ins, out_specs=[SMEM] * s...  34.2 us
    ppermute x32, waiting for transfers between devices, swap(): return lax.ppermute(x, axis, [(i, i ^ mask) for i in range(size)])  14.2 us
    gather x1, local copies, waits for them, and re-layouts, on_device(): target_rows = head_weight.at[clipped].get(mode='promise_in_bounds')  9.43 us
  transfers between devices with their start and end apart: 34, of which 9 were waited for; matrix products, arithmetic and copies ran while one was open for 13% of the time, Pallas kernels for 25%

profile of v1, /device:TPU:0, one launch (start us, length us, event | category | flops | bytes accessed | tf_op | source)
XLA Modules:
  0.0 104.9 jit_solution(4582012934808464107)
XLA Ops:
  0.6 4.0 %collective-permute-start.5 = (bf16[128,1024]{1,0:T(8,128)(2,1)}, bf16[128,1024]{1,0:T(8,128)(2,1)S(1)}, u32[]{:S(2)}, u32[]{:S(2)}) collective-permute-start(bf16[128,1024]{1,0:T(8,128)(2,1)} %refs_0_.3), channel_id=1, source_target_pairs={{0,24},{4,28},{8,16},{12,20},{16,8},{20,12},{24,0},{28,4},{1,25},{... | collective-permute-start | bytes 786440 | tf_op jit(solution)/shard_map/ppermute | solution.py:28
  9.5 4.3 %shard_map.121 = (s32[16]{0:T(128)S(1)}, s32[16]{0:T(128)S(1)}, s32[1]{0:T(128)}, bf16[2048,1024]{1,0:T(8,128)(2,1)S(1)}) custom-call(s32[8,1,4]{2,1,0:T(1,128)S(1)} %copy.13.tiles_ref, s32[8,1]{1,0:T(8,128)S(1)} %copy.14.counts_ref, bf16[4096,1024]{1,0:T(8,128)(2,1)} %head.5), custom_call_target="tpu_custom_call" | custom-call | bytes 4194304 | tf_op jit(solution)/shard_map/pallas_call | solution.py:260
  13.9 3.2 %collective-permute-done.refs_2_ = bf16[128,1024]{1,0:T(8,128)(2,1)S(1)} collective-permute-done((bf16[128,1024]{1,0:T(8,128)(2,1)}, bf16[128,1024]{1,0:T(8,128)(2,1)S(1)}, u32[]{:S(2)}, u32[]{:S(2)}) %collective-permute-start) | collective-permute-done | bytes 262176 | tf_op jit(solution)/shard_map/ppermute | solution.py:28
  19.3 1.5 %shard_map.124 = (f32[256,128]{1,0:T(8,128)S(1)}, s16[264,128]{1,0:T(8,128)(2,1)S(1)}, s16[264,128]{1,0:T(8,128)(2,1)S(1)}, s16[264,128]{1,0:T(8,128)(2,1)S(1)}) custom-call(s32[16]{0:T(128)S(1)} %get-tuple-element.49.blocks_ref, s32[2]{0:T(128)S(1)} %pad_add_fusion.where_ref, bf16[2048,1024]{1,0:T(8,128)(2,1)S(1)} %get-tuple-element.54.tiles, ...), custom_call_target="tpu_custom_call" | custom-call | flops 268435456 | bytes 2097152 | tf_op jit(solution)/shard_map/pallas_call | solution.py:260
  20.9 1.6 %collective-permute-start.10 = (s16[264,128]{1,0:T(8,128)(2,1)S(1)}, s16[264,128]{1,0:T(8,128)(2,1)S(1)}, u32[]{:S(2)}, u32[]{:S(2)}) collective-permute-start(s16[264,128]{1,0:T(8,128)(2,1)S(1)} %get-tuple-element.63), channel_id=1, source_target_pairs={{0,1},{1,0},{2,3},{3,2},{4,5},{5,4},{6,7},{7,6},{8,9},{9,8},{10,11... | collective-permute-start | bytes 202760 | tf_op jit(solution)/shard_map/ppermute | solution.py:28
  22.5 2.6 %collective-permute-start.11 = (s16[264,128]{1,0:T(8,128)(2,1)S(1)}, s16[264,128]{1,0:T(8,128)(2,1)S(1)}, u32[]{:S(2)}, u32[]{:S(2)}) collective-permute-start(s16[264,128]{1,0:T(8,128)(2,1)S(1)} %get-tuple-element.64), channel_id=1, source_target_pairs={{0,2},{1,3},{2,0},{3,1},{4,6},{5,7},{6,4},{7,5},{8,10},{9,11},{10,... | collective-permute-start | bytes 202760 | tf_op jit(solution)/shard_map/ppermute | solution.py:28
  27.6 3.5 %collective-permute-start.8 = (s16[264,128]{1,0:T(8,128)(2,1)S(1)}, s16[264,128]{1,0:T(8,128)(2,1)S(1)}, u32[]{:S(2)}, u32[]{:S(2)}) collective-permute-start(s16[264,128]{1,0:T(8,128)(2,1)S(1)} %get-tuple-element.58), channel_id=1, source_target_pairs={{0,2},{1,3},{2,0},{3,1},{4,6},{5,7},{6,4},{7,5},{8,10},{9,11},{10,... | collective-permute-start | bytes 202760 | tf_op jit(solution)/shard_map/ppermute | solution.py:28
  33.0 3.2 %collective-permute-start.18 = (bf16[256,128]{1,0:T(8,128)(2,1)S(1)}, bf16[256,128]{1,0:T(8,128)(2,1)S(1)}, u32[]{:S(2)}, u32[]{:S(2)}) collective-permute-start(bf16[256,128]{1,0:T(8,128)(2,1)S(1)} %shard_map.125.refs_1_), channel_id=1, source_target_pairs={{0,3},{1,2},{2,1},{3,0},{4,7},{5,6},{6,5},{7,4},{8,11},{9,10},{10,... | collective-permute-start | bytes 196616 | tf_op jit(solution)/shard_map/ppermute | solution.py:28
  39.2 2.8 %collective-permute-start.17 = (bf16[256,128]{1,0:T(8,128)(2,1)S(1)}, bf16[256,128]{1,0:T(8,128)(2,1)S(1)}, u32[]{:S(2)}, u32[]{:S(2)}) collective-permute-start(bf16[256,128]{1,0:T(8,128)(2,1)S(1)} %shard_map.123.refs_0_), channel_id=1, source_target_pairs={{0,3},{1,2},{2,1},{3,0},{4,7},{5,6},{6,5},{7,4},{8,11},{9,10},{10,... | collective-permute-start | bytes 196616 | tf_op jit(solution)/shard_map/ppermute | solution.py:28
  42.0 2.0 %collective-permute-start.15 = (bf16[256,128]{1,0:T(8,128)(2,1)S(1)}, bf16[256,128]{1,0:T(8,128)(2,1)S(1)}, u32[]{:S(2)}, u32[]{:S(2)}) collective-permute-start(bf16[256,128]{1,0:T(8,128)(2,1)S(1)} %shard_map.123.refs_0_), channel_id=1, source_target_pairs={{0,2},{1,3},{2,0},{3,1},{4,6},{5,7},{6,4},{7,5},{8,10},{9,11},{10,... | collective-permute-start | bytes 196616 | tf_op jit(solution)/shard_map/ppermute | solution.py:28
  44.5 9.4 %gather_fusion = bf16[1024,1024]{1,0:T(8,128)(2,1)S(1)} fusion(bf16[4096,1024]{1,0:T(8,128)(2,1)} %head.5, s32[1024]{0:T(1024)S(1)} %fusion), kind=kCustom, calls=%fused_computation | custom fusion | bytes 4198400 | tf_op jit(solution)/shard_map/gather | solution.py:350
  54.0 3.7 %shard_map.127 = (f32[512,512]{1,0:T(8,128)S(1)}, f32[512,512]{1,0:T(8,128)S(1)}) custom-call(s32[16]{0:T(128)S(1)} %get-tuple-element.49.blocks_ref, s32[16]{0:T(128)S(1)} %get-tuple-element.50.tiles_ref, s32[2]{0:T(128)S(1)} %pad_add_fusion.where_ref, bf16[4096,1024]{1,0:T(8,128)(2,1)} %head.5, bf16[256,128]{1,0:T(8,128)(2,1)S(1)} %shard_map.123.refs_0_, ...), custom_call_target="tpu_custom_call" | custom-call | flops 268435456 | bytes 4194304 | tf_op jit(solution)/shard_map/pallas_call | solution.py:260
  57.8 4.1 %shard_map.126 = (f32[512,512]{1,0:T(8,128)S(1)}, f32[512,512]{1,0:T(8,128)S(1)}) custom-call(s32[16]{0:T(128)S(1)} %get-tuple-element.49.blocks_ref, s32[16]{0:T(128)S(1)} %get-tuple-element.50.tiles_ref, s32[2]{0:T(128)S(1)} %pad_add_fusion.where_ref, bf16[4096,1024]{1,0:T(8,128)(2,1)} %head.5, bf16[256,128]{1,0:T(8,128)(2,1)S(1)} %shard_map.123.refs_0_, ...), custom_call_target="tpu_custom_call" | custom-call | flops 268435456 | bytes 4194304 | tf_op jit(solution)/shard_map/pallas_call | solution.py:260
  64.0 2.6 %collective-permute-start.22 = (s16[136,512]{1,0:T(8,128)(2,1)S(1)}, s16[136,512]{1,0:T(8,128)(2,1)S(1)}, u32[]{:S(2)}, u32[]{:S(2)}) collective-permute-start(s16[136,512]{1,0:T(8,128)(2,1)S(1)} %get-tuple-element.78), channel_id=1, source_target_pairs={{0,24},{4,28},{8,16},{12,20},{16,8},{20,12},{24,0},{28,4},{1,25},{... | collective-permute-start | bytes 417800 | tf_op jit(solution)/shard_map/ppermute | solution.py:28
  66.6 3.2 %shard_map.129.refs_1_.refs_2_ = bf16[3,1792,512]{2,1,0:T(8,128)(2,1)S(1)} custom-call(s32[2]{0:T(128)S(1)} %pad_add_fusion.where_ref, bf16[1792,4096]{1,0:T(8,128)(2,1)} %refs_5_.2), custom_call_target="tpu_custom_call" | custom-call | bytes 5505024 | tf_op jit(solution)/shard_map/pallas_call | solution.py:260
  69.9 2.4 %collective-permute-done.22.refs_2_ = s16[136,512]{1,0:T(8,128)(2,1)S(1)} collective-permute-done((s16[136,512]{1,0:T(8,128)(2,1)S(1)}, s16[136,512]{1,0:T(8,128)(2,1)S(1)}, u32[]{:S(2)}, u32[]{:S(2)}) %collective-permute-start.22) | collective-permute-done | bytes 139296 | tf_op jit(solution)/shard_map/ppermute | solution.py:28
  73.9 2.9 %collective-permute-start.31 = (bf16[128,512]{1,0:T(8,128)(2,1)S(1)}, bf16[128,512]{1,0:T(8,128)(2,1)S(1)}, u32[]{:S(2)}, u32[]{:S(2)}) collective-permute-start(bf16[128,512]{1,0:T(8,128)(2,1)S(1)} %shard_map.130.refs_0_.refs_3_), channel_id=1, source_target_pairs={{0,2},{1,3},{2,0},{3,1},{4,6},{5,7},{6,4},{7,5},{8,10},{9,11},{10,... | collective-permute-start | bytes 393224 | tf_op jit(solution)/shard_map/ppermute | solution.py:28
  79.7 2.3 %collective-permute-done.31.refs_2_ = bf16[128,512]{1,0:T(8,128)(2,1)S(1)} collective-permute-done((bf16[128,512]{1,0:T(8,128)(2,1)S(1)}, bf16[128,512]{1,0:T(8,128)(2,1)S(1)}, u32[]{:S(2)}, u32[]{:S(2)}) %collective-permute-start.31) | collective-permute-done | bytes 131104 | tf_op jit(solution)/shard_map/ppermute | solution.py:28
  83.5 2.6 %shard_map.132.refs_6_ = f32[128,1792]{1,0:T(8,128)S(1)} custom-call(s32[2]{0:T(128)S(1)} %pad_add_fusion.where_ref, bf16[128,512]{1,0:T(8,128)(2,1)S(1)} %shard_map.130.refs_0_.refs_3_, bf16[1792,4096]{1,0:T(8,128)(2,1)} %refs_5_.2), custom_call_target="tpu_custom_call" | custom-call | flops 234881024 | bytes 1835008 | tf_op jit(solution)/shard_map/pallas_call | solution.py:260
  87.0 2.6 %collective-permute-start.29 = (bf16[128,512]{1,0:T(8,128)(2,1)S(1)}, bf16[128,512]{1,0:T(8,128)(2,1)S(1)}, u32[]{:S(2)}, u32[]{:S(2)}) collective-permute-start(bf16[128,512]{1,0:T(8,128)(2,1)S(1)} %get-tuple-element.88.refs_0_), channel_id=1, source_target_pairs={{0,1},{1,0},{2,3},{3,2},{4,5},{5,4},{6,7},{7,6},{8,9},{9,8},{10,11... | collective-permute-start | bytes 393224 | tf_op jit(solution)/shard_map/ppermute | solution.py:28
  89.7 2.2 %collective-permute-start.28 = (bf16[128,512]{1,0:T(8,128)(2,1)S(1)}, bf16[128,512]{1,0:T(8,128)(2,1)S(1)}, u32[]{:S(2)}, u32[]{:S(2)}) collective-permute-start(bf16[128,512]{1,0:T(8,128)(2,1)S(1)} %get-tuple-element.88.refs_0_), channel_id=1, source_target_pairs={{0,3},{1,2},{2,1},{3,0},{4,7},{5,6},{6,5},{7,4},{8,11},{9,10},{10,... | collective-permute-start | bytes 393224 | tf_op jit(solution)/shard_map/ppermute | solution.py:28
  91.9 5.2 %shard_map.134.refs_2_ = f32[128,1792]{1,0:T(8,128)S(1)} custom-call(s32[2]{0:T(128)S(1)} %pad_add_fusion.where_ref, bf16[128,512]{1,0:T(8,128)(2,1)S(1)} %get-tuple-element.88.refs_0_, bf16[128,512]{1,0:T(8,128)(2,1)S(1)} %collective-permute-done.30.refs_1_, bf16[128,512]{1,0:T(8,128)(2,1)S(1)} %collective-permute-done.31.refs_2_, ...), custom_call_target="tpu_custom_call" | custom-call | flops 939524096 | bytes 7340032 | tf_op jit(solution)/shard_map/pallas_call | solution.py:260
  98.4 3.7 %collective-permute-done.27.refs_0_ = bf16[128,512]{1,0:T(8,128)(2,1)S(1)} collective-permute-done((bf16[128,512]{1,0:T(8,128)(2,1)S(1)}, bf16[128,512]{1,0:T(8,128)(2,1)S(1)}, u32[]{:S(2)}, u32[]{:S(2)}) %collective-permute-start.27) | collective-permute-done | bytes 131104 | tf_op jit(solution)/shard_map/ppermute | solution.py:28
  102.1 2.9 %shard_map.136 = (bf16[128,1792]{1,0:T(8,128)(2,1)}, bf16[128,1792]{1,0:T(8,128)(2,1)}) custom-call(s32[2]{0:T(128)S(1)} %pad_add_fusion.where_ref, bf16[128,512]{1,0:T(8,128)(2,1)S(1)} %collective-permute-done.27.refs_0_, bf16[128,512]{1,0:T(8,128)(2,1)S(1)} %collective-permute-done.28.refs_1_, bf16[3,1792,512]{2,1,0:T(8,128)(2,1)S(1)} %shard_map.129.refs_1_.refs_2_, ...), custom_call_target="tpu_custom_call" | custom-call | flops 469762048 | bytes 3670016 | tf_op jit(solution)/shard_map/pallas_call | solution.py:260
  (78 shorter events, 25.4 us)
Async XLA Ops:
  0.6 16.4 %collective-permute-start.5 = (bf16[128,1024]{1,0:T(8,128)(2,1)}, bf16[128,1024]{1,0:T(8,128)(2,1)S(1)}, u32[]{:S(2)}, u32[]{:S(2)}) collective-permute-start(bf16[128,1024]{1,0:T(8,128)(2,1)} %refs_0_.3), channel_id=1, source_target_pairs={{0,24},{4,28},{8,16},{12,20},{16,8},{20,12},{24,0},{28,4},{1,25},{... | collective-permute-start | bytes 786440 | tf_op jit(solution)/shard_map/ppermute | solution.py:28
  4.6 12.4 %collective-permute-start.3 = (bf16[128,1024]{1,0:T(8,128)(2,1)}, bf16[128,1024]{1,0:T(8,128)(2,1)S(1)}, u32[]{:S(2)}, u32[]{:S(2)}) collective-permute-start(bf16[128,1024]{1,0:T(8,128)(2,1)} %refs_0_.3), channel_id=1, source_target_pairs={{0,16},{4,20},{8,24},{12,28},{16,0},{20,4},{24,8},{28,12},{1,17},{... | collective-permute-start | bytes 786440 | tf_op jit(solution)/shard_map/ppermute | solution.py:28
  5.1 12.5 %collective-permute-start.1 = (bf16[128,1024]{1,0:T(8,128)(2,1)}, bf16[128,1024]{1,0:T(8,128)(2,1)S(1)}, u32[]{:S(2)}, u32[]{:S(2)}) collective-permute-start(bf16[128,1024]{1,0:T(8,128)(2,1)} %refs_0_.3), channel_id=1, source_target_pairs={{0,4},{4,0},{8,12},{12,8},{16,20},{20,16},{24,28},{28,24},{1,5},{5... | collective-permute-start | bytes 786440 | tf_op jit(solution)/shard_map/ppermute | solution.py:28
  5.1 11.9 %collective-permute-start = (bf16[128,1024]{1,0:T(8,128)(2,1)}, bf16[128,1024]{1,0:T(8,128)(2,1)S(1)}, u32[]{:S(2)}, u32[]{:S(2)}) collective-permute-start(bf16[128,1024]{1,0:T(8,128)(2,1)} %refs_0_.3), channel_id=1, source_target_pairs={{0,8},{4,12},{8,0},{12,4},{16,24},{20,28},{24,16},{28,20},{1,9},{5... | collective-permute-start | bytes 786440 | tf_op jit(solution)/shard_map/ppermute | solution.py:28
  20.9 10.2 %collective-permute-start.10 = (s16[264,128]{1,0:T(8,128)(2,1)S(1)}, s16[264,128]{1,0:T(8,128)(2,1)S(1)}, u32[]{:S(2)}, u32[]{:S(2)}) collective-permute-start(s16[264,128]{1,0:T(8,128)(2,1)S(1)} %get-tuple-element.63), channel_id=1, source_target_pairs={{0,1},{1,0},{2,3},{3,2},{4,5},{5,4},{6,7},{7,6},{8,9},{9,8},{10,11... | collective-permute-start | bytes 202760 | tf_op jit(solution)/shard_map/ppermute | solution.py:28
  22.5 8.8 %collective-permute-start.11 = (s16[264,128]{1,0:T(8,128)(2,1)S(1)}, s16[264,128]{1,0:T(8,128)(2,1)S(1)}, u32[]{:S(2)}, u32[]{:S(2)}) collective-permute-start(s16[264,128]{1,0:T(8,128)(2,1)S(1)} %get-tuple-element.64), channel_id=1, source_target_pairs={{0,2},{1,3},{2,0},{3,1},{4,6},{5,7},{6,4},{7,5},{8,10},{9,11},{10,... | collective-permute-start | bytes 202760 | tf_op jit(solution)/shard_map/ppermute | solution.py:28
  26.8 10.1 %collective-permute-start.7 = (s16[264,128]{1,0:T(8,128)(2,1)S(1)}, s16[264,128]{1,0:T(8,128)(2,1)S(1)}, u32[]{:S(2)}, u32[]{:S(2)}) collective-permute-start(s16[264,128]{1,0:T(8,128)(2,1)S(1)} %get-tuple-element.57), channel_id=1, source_target_pairs={{0,1},{1,0},{2,3},{3,2},{4,5},{5,4},{6,7},{7,6},{8,9},{9,8},{10,11... | collective-permute-start | bytes 202760 | tf_op jit(solution)/shard_map/ppermute | solution.py:28
  27.6 10.4 %collective-permute-start.8 = (s16[264,128]{1,0:T(8,128)(2,1)S(1)}, s16[264,128]{1,0:T(8,128)(2,1)S(1)}, u32[]{:S(2)}, u32[]{:S(2)}) collective-permute-start(s16[264,128]{1,0:T(8,128)(2,1)S(1)} %get-tuple-element.58), channel_id=1, source_target_pairs={{0,2},{1,3},{2,0},{3,1},{4,6},{5,7},{6,4},{7,5},{8,10},{9,11},{10,... | collective-permute-start | bytes 202760 | tf_op jit(solution)/shard_map/ppermute | solution.py:28
  33.0 11.0 %collective-permute-start.18 = (bf16[256,128]{1,0:T(8,128)(2,1)S(1)}, bf16[256,128]{1,0:T(8,128)(2,1)S(1)}, u32[]{:S(2)}, u32[]{:S(2)}) collective-permute-start(bf16[256,128]{1,0:T(8,128)(2,1)S(1)} %shard_map.125.refs_1_), channel_id=1, source_target_pairs={{0,3},{1,2},{2,1},{3,0},{4,7},{5,6},{6,5},{7,4},{8,11},{9,10},{10,... | collective-permute-start | bytes 196616 | tf_op jit(solution)/shard_map/ppermute | solution.py:28
  36.2 17.7 %collective-permute-start.16 = (bf16[256,128]{1,0:T(8,128)(2,1)S(1)}, bf16[256,128]{1,0:T(8,128)(2,1)S(1)}, u32[]{:S(2)}, u32[]{:S(2)}) collective-permute-start(bf16[256,128]{1,0:T(8,128)(2,1)S(1)} %shard_map.125.refs_1_), channel_id=1, source_target_pairs={{0,2},{1,3},{2,0},{3,1},{4,6},{5,7},{6,4},{7,5},{8,10},{9,11},{10,... | collective-permute-start | bytes 196616 | tf_op jit(solution)/shard_map/ppermute | solution.py:28
  36.9 17.1 %collective-permute-start.14 = (bf16[256,128]{1,0:T(8,128)(2,1)S(1)}, bf16[256,128]{1,0:T(8,128)(2,1)S(1)}, u32[]{:S(2)}, u32[]{:S(2)}) collective-permute-start(bf16[256,128]{1,0:T(8,128)(2,1)S(1)} %shard_map.125.refs_1_), channel_id=1, source_target_pairs={{0,1},{1,0},{2,3},{3,2},{4,5},{5,4},{6,7},{7,6},{8,9},{9,8},{10,11... | collective-permute-start | bytes 196616 | tf_op jit(solution)/shard_map/ppermute | solution.py:28
  39.2 14.8 %collective-permute-start.17 = (bf16[256,128]{1,0:T(8,128)(2,1)S(1)}, bf16[256,128]{1,0:T(8,128)(2,1)S(1)}, u32[]{:S(2)}, u32[]{:S(2)}) collective-permute-start(bf16[256,128]{1,0:T(8,128)(2,1)S(1)} %shard_map.123.refs_0_), channel_id=1, source_target_pairs={{0,3},{1,2},{2,1},{3,0},{4,7},{5,6},{6,5},{7,4},{8,11},{9,10},{10,... | collective-permute-start | bytes 196616 | tf_op jit(solution)/shard_map/ppermute | solution.py:28
  42.0 12.0 %collective-permute-start.15 = (bf16[256,128]{1,0:T(8,128)(2,1)S(1)}, bf16[256,128]{1,0:T(8,128)(2,1)S(1)}, u32[]{:S(2)}, u32[]{:S(2)}) collective-permute-start(bf16[256,128]{1,0:T(8,128)(2,1)S(1)} %shard_map.123.refs_0_), channel_id=1, source_target_pairs={{0,2},{1,3},{2,0},{3,1},{4,6},{5,7},{6,4},{7,5},{8,10},{9,11},{10,... | collective-permute-start | bytes 196616 | tf_op jit(solution)/shard_map/ppermute | solution.py:28
  44.0 10.0 %collective-permute-start.13 = (bf16[256,128]{1,0:T(8,128)(2,1)S(1)}, bf16[256,128]{1,0:T(8,128)(2,1)S(1)}, u32[]{:S(2)}, u32[]{:S(2)}) collective-permute-start(bf16[256,128]{1,0:T(8,128)(2,1)S(1)} %shard_map.123.refs_0_), channel_id=1, source_target_pairs={{0,1},{1,0},{2,3},{3,2},{4,5},{5,4},{6,7},{7,6},{8,9},{9,8},{10,11... | collective-permute-start | bytes 196616 | tf_op jit(solution)/shard_map/ppermute | solution.py:28
  61.9 10.4 %collective-permute-start.23 = (f32[512,512]{1,0:T(8,128)S(1)}, f32[512,512]{1,0:T(8,128)S(1)}, u32[]{:S(2)}, u32[]{:S(2)}) collective-permute-start(f32[512,512]{1,0:T(8,128)S(1)} %get-tuple-element.80), channel_id=1, source_target_pairs={{0,4},{4,0},{8,12},{12,8},{16,20},{20,16},{24,28},{28,24},{1,5},{5... | collective-permute-start | bytes 3145736 | tf_op jit(solution)/shard_map/ppermute | solution.py:28
  72.6 9.4 %collective-permute-start.24 = (s16[136,512]{1,0:T(8,128)(2,1)S(1)}, s16[136,512]{1,0:T(8,128)(2,1)S(1)}, u32[]{:S(2)}, u32[]{:S(2)}) collective-permute-start(s16[136,512]{1,0:T(8,128)(2,1)S(1)} %get-tuple-element.83), channel_id=1, source_target_pairs={{0,8},{4,12},{8,0},{12,4},{16,24},{20,28},{24,16},{28,20},{1,9},{5... | collective-permute-start | bytes 417800 | tf_op jit(solution)/shard_map/ppermute | solution.py:28
  76.8 9.3 %collective-permute-start.25 = (s16[136,512]{1,0:T(8,128)(2,1)S(1)}, s16[136,512]{1,0:T(8,128)(2,1)S(1)}, u32[]{:S(2)}, u32[]{:S(2)}) collective-permute-start(s16[136,512]{1,0:T(8,128)(2,1)S(1)} %get-tuple-element.84), channel_id=1, source_target_pairs={{0,16},{4,20},{8,24},{12,28},{16,0},{20,4},{24,8},{28,12},{1,17},{... | collective-permute-start | bytes 417800 | tf_op jit(solution)/shard_map/ppermute | solution.py:28
  77.9 8.3 %collective-permute-start.26 = (s16[136,512]{1,0:T(8,128)(2,1)S(1)}, s16[136,512]{1,0:T(8,128)(2,1)S(1)}, u32[]{:S(2)}, u32[]{:S(2)}) collective-permute-start(s16[136,512]{1,0:T(8,128)(2,1)S(1)} %get-tuple-element.85), channel_id=1, source_target_pairs={{0,24},{4,28},{8,16},{12,20},{16,8},{20,12},{24,0},{28,4},{1,25},{... | collective-permute-start | bytes 417800 | tf_op jit(solution)/shard_map/ppermute | solution.py:28
  79.1 12.8 %collective-permute-start.32 = (bf16[128,512]{1,0:T(8,128)(2,1)S(1)}, bf16[128,512]{1,0:T(8,128)(2,1)S(1)}, u32[]{:S(2)}, u32[]{:S(2)}) collective-permute-start(bf16[128,512]{1,0:T(8,128)(2,1)S(1)} %shard_map.130.refs_0_.refs_3_), channel_id=1, source_target_pairs={{1,2},{2,1},{5,6},{6,5},{9,10},{10,9},{13,14},{14,13},{17,18},{18,... | collective-permute-start | bytes 393224 | tf_op jit(solution)/shard_map/ppermute | solution.py:445
  82.0 9.9 %collective-permute-start.30 = (bf16[128,512]{1,0:T(8,128)(2,1)S(1)}, bf16[128,512]{1,0:T(8,128)(2,1)S(1)}, u32[]{:S(2)}, u32[]{:S(2)}) collective-permute-start(bf16[128,512]{1,0:T(8,128)(2,1)S(1)} %shard_map.130.refs_0_.refs_3_), channel_id=1, source_target_pairs={{0,1},{1,0},{2,3},{3,2},{4,5},{5,4},{6,7},{7,6},{8,9},{9,8},{10,11... | collective-permute-start | bytes 393224 | tf_op jit(solution)/shard_map/ppermute | solution.py:28
  82.0 9.9 %collective-permute-start.33 = (bf16[128,512]{1,0:T(8,128)(2,1)S(1)}, bf16[128,512]{1,0:T(8,128)(2,1)S(1)}, u32[]{:S(2)}, u32[]{:S(2)}) collective-permute-start(bf16[128,512]{1,0:T(8,128)(2,1)S(1)} %collective-permute-done.31.refs_2_), channel_id=1, source_target_pairs={{1,0},{2,3},{5,4},{6,7},{9,8},{10,11},{13,12},{14,15},{17,16},{18,... | collective-permute-start | bytes 393224 | tf_op jit(solution)/shard_map/ppermute | solution.py:446
  87.0 10.1 %collective-permute-start.29 = (bf16[128,512]{1,0:T(8,128)(2,1)S(1)}, bf16[128,512]{1,0:T(8,128)(2,1)S(1)}, u32[]{:S(2)}, u32[]{:S(2)}) collective-permute-start(bf16[128,512]{1,0:T(8,128)(2,1)S(1)} %get-tuple-element.88.refs_0_), channel_id=1, source_target_pairs={{0,1},{1,0},{2,3},{3,2},{4,5},{5,4},{6,7},{7,6},{8,9},{9,8},{10,11... | collective-permute-start | bytes 393224 | tf_op jit(solution)/shard_map/ppermute | solution.py:28
  89.7 8.7 %collective-permute-start.28 = (bf16[128,512]{1,0:T(8,128)(2,1)S(1)}, bf16[128,512]{1,0:T(8,128)(2,1)S(1)}, u32[]{:S(2)}, u32[]{:S(2)}) collective-permute-start(bf16[128,512]{1,0:T(8,128)(2,1)S(1)} %get-tuple-element.88.refs_0_), channel_id=1, source_target_pairs={{0,3},{1,2},{2,1},{3,0},{4,7},{5,6},{6,5},{7,4},{8,11},{9,10},{10,... | collective-permute-start | bytes 393224 | tf_op jit(solution)/shard_map/ppermute | solution.py:28
  91.9 10.2 %collective-permute-start.27 = (bf16[128,512]{1,0:T(8,128)(2,1)S(1)}, bf16[128,512]{1,0:T(8,128)(2,1)S(1)}, u32[]{:S(2)}, u32[]{:S(2)}) collective-permute-start(bf16[128,512]{1,0:T(8,128)(2,1)S(1)} %get-tuple-element.88.refs_0_), channel_id=1, source_target_pairs={{0,2},{1,3},{2,0},{3,1},{4,6},{5,7},{6,4},{7,5},{8,10},{9,11},{10,... | collective-permute-start | bytes 393224 | tf_op jit(solution)/shard_map/ppermute | solution.py:28
  (14 other events, 83.8 us)

commit v2 on v1

--- a/solution.py
+++ b/solution.py
@@ -12,6 +12,8 @@
 PAD = 8
 GROUPS = 2
 HALVES = 2
+GROUP_ROWS = 8
+AT_ONCE = 32
 LARGE = 50
 MEDIUM = 46
 LEVELS = 32767.0
@@ -43,7 +45,7 @@
     return levels.astype(jnp.int32).astype(jnp.float32) * step_of(code.astype(jnp.float32))
 
 
-def tiles_kernel(slots, tiles_ref, counts_ref, head, blocks_out, tiles_out, live_out, out, sem):
+def tiles_kernel(slots, tiles_ref, counts_ref, head, blocks_out, live_out, out, sem):
     blocks, _, per_block = tiles_ref.shape
 
     def copy(tile, slot):
@@ -55,7 +57,6 @@
 
     def place(slot, block, tile):
         blocks_out[slot] = block
-        tiles_out[slot] = tile
         copy(tile, slot).start()
 
     live = jnp.int32(0)
@@ -103,6 +104,54 @@
                 sends[k - 1][share * TILE + i : share * TILE + i + 1, :] = code.astype(jnp.int16)
 
 
+def targets_kernel(list_ref, count_ref, code, head, out, groups, more, sem, more_sem):
+    blocks = code.shape[0]
+
+    def copy(block, j, buffer, at, sem):
+        start = pl.multiple_of(list_ref[block * TILE + j] * GROUP_ROWS, GROUP_ROWS)
+        return pltpu.make_async_copy(
+            head.at[pl.ds(start, GROUP_ROWS), :],
+            buffer.at[pl.ds(pl.multiple_of(at * GROUP_ROWS, GROUP_ROWS), GROUP_ROWS), :],
+            sem,
+        )
+
+    def place(block, chunk, buffer):
+        depth = AT_ONCE * GROUP_ROWS
+        wanted = code[block : block + 1, :] - chunk * depth
+        spot = lax.broadcasted_iota(jnp.int32, (depth, TILE), 0)
+        hit = jnp.where(spot == wanted, 1.0, 0.0).astype(jnp.bfloat16)
+        return lax.dot_general(
+            hit, buffer[...], (((0,), (0,)), ((), ())), preferred_element_type=jnp.float32
+        )
+
+    for block in range(blocks):
+        for j in range(AT_ONCE):
+            copy(block, j, groups.at[block], j, sem.at[block]).start()
+    for block in range(blocks):
+        rows = pl.ds(block * TILE, TILE)
+        pltpu.make_async_copy(
+            head.at[pl.ds(0, AT_ONCE * GROUP_ROWS), :], groups.at[block], sem.at[block]
+        ).wait()
+        out[rows, :] = place(block, 0, groups.at[block]).astype(jnp.bfloat16)
+
+        @pl.when(count_ref[block] > AT_ONCE)
+        def _(block=block, rows=rows):
+            def body(chunk, carry):
+                def start(j, carry):
+                    copy(block, chunk * AT_ONCE + j, more, j, more_sem).start()
+                    return carry
+
+                lax.fori_loop(0, AT_ONCE, start, 0)
+                pltpu.make_async_copy(
+                    head.at[pl.ds(0, AT_ONCE * GROUP_ROWS), :], more, more_sem
+                ).wait()
+                added = out[rows, :].astype(jnp.float32) + place(block, chunk, more)
+                out[rows, :] = added.astype(jnp.bfloat16)
+                return carry
+
+            lax.fori_loop(1, (count_ref[block] + AT_ONCE - 1) // AT_ONCE, body, 0)
+
+
 def probs_kernel(narrow, slots, group, blocks_ref, live_ref, where_ref, own, *refs):
     recvs, lse, weight, out = refs[: narrow - 1], refs[-3], refs[-2], refs[-1]
     per = slots // narrow
@@ -120,21 +169,13 @@
         )
 
 
-def grads_kernel(wide, narrow, slots, half, blocks_ref, tiles_ref, where_ref, head, *refs):
+def grads_kernel(wide, narrow, slots, half, blocks_ref, where_ref, tiles, *refs):
     probs = refs[: narrow * GROUPS]
-    target_rows, factor, mine, other, total, tiles, sem = refs[narrow * GROUPS :]
+    target_rows, factor, mine, other, total = refs[narrow * GROUPS :]
     me_w, me_n = where_ref[0], where_ref[1]
     per = slots // narrow
     share = per // GROUPS
     width = mine.shape[1]
-
-    def fetch(slot):
-        start = pl.multiple_of(tiles_ref[slot] * TILE, TILE)
-        part = head.at[pl.ds(start, TILE), pl.ds(half * width, width)]
-        return pltpu.make_async_copy(part, tiles.at[slot], sem.at[slot])
-
-    for slot in range(slots):
-        fetch(slot).start()
     for block in range(factor.shape[0] // TILE):
         rows = slice(block * TILE, (block + 1) * TILE)
         weight = -factor[rows, :]
@@ -143,15 +184,16 @@
             total[block ^ me_w, :, lane : lane + TILE] = weight * target_rows[
                 rows, at : at + TILE
             ].astype(jnp.float32)
-    for slot in range(slots):
-        fetch(slot).wait()
     for k in range(narrow):
         for group in range(GROUPS):
             for i in range(share):
                 slot = (me_n ^ k) * per + group * share + i
                 total[blocks_ref[slot] ^ me_w] += jnp.dot(
                     probs[k * GROUPS + group][i * TILE : (i + 1) * TILE, :],
-                    tiles[slot],
+                    tiles[
+                        pl.ds(pl.multiple_of(slot * TILE, TILE), TILE),
+                        half * width : (half + 1) * width,
+                    ],
                     preferred_element_type=jnp.float32,
                 )
     for chip in range(wide // 2):
@@ -173,18 +215,14 @@
             send[TILE:, lanes] = jnp.broadcast_to(code, (PAD, TILE)).astype(jnp.int16)
 
 
-def merge_kernel(chips, before, own, *refs):
-    recvs, befores, outs = refs[: chips - 1], refs[chips - 1 : chips - 1 + before], refs[-1 - before :]
-    width = own.shape[1]
-    for lane in range(0, width, TILE):
+def merge_kernel(own, *refs):
+    recvs, out = refs[:-1], refs[-1]
+    for lane in range(0, own.shape[1], TILE):
         lanes = slice(lane, lane + TILE)
         total = own[:, lanes]
         for recv in recvs:
             total = total + decode(recv[:TILE, lanes], recv[TILE : TILE + 1, lanes])
-        outs[0][:, lanes] = total.astype(jnp.bfloat16)
-    if before:
-        for at, part in enumerate([*befores, outs[0]]):
-            outs[1][:, at * width : (at + 1) * width] = part[...]
+        out[:, lanes] = total.astype(jnp.bfloat16)
 
 
 def down_copies(keys, where_ref, down, out, sem, rows):
@@ -210,6 +248,7 @@
     count, inputs = len(keys), sum(splits)
     arrived, down, refs = list(refs[:inputs]), refs[inputs], list(refs[inputs + 1 :])
     units = down.shape[-2]
+    width = arrived[0].shape[1]
     pieces = []
     for split in splits:
         piece = arrived.pop(0)[...]
@@ -221,6 +260,9 @@
         gate, up, gate_out, up_out = refs[:4]
     else:
         sum_out = refs[0]
+    if kind == "first":
+        for at in range(HALVES):
+            refs[1][:, at * width : (at + 1) * width] = pieces[at]
     steps = [pl.ds(at, chunk) for at in range(0, units, chunk)]
     if skip is None:
         down_v, sem = refs[-2:]
@@ -294,29 +336,44 @@
 
     far = [swap(hidden, "wide", 2 * chip) for chip in range(chips)]
 
-    local_ids = targets - me_w * vocab_here
+    local_ids = (targets - me_w * vocab_here).reshape(blocks, TILE)
     inside = (local_ids >= 0) & (local_ids < vocab_here)
-    clipped = jnp.clip(local_ids, 0, vocab_here - 1)
+    order = jnp.arange(TILE, dtype=jnp.int32)
+    earlier = (order[None, :] < order[:, None])[None] & inside[:, None, :]
+    rank = jnp.sum(earlier.astype(jnp.int32), axis=2)
+    target_code = jnp.where(inside, rank * GROUP_ROWS + local_ids % GROUP_ROWS, -1)
+    chosen = (rank[:, None, :] == order[None, :, None]) & inside[:, None, :]
+    target_list = jnp.sum(jnp.where(chosen, (local_ids // GROUP_ROWS)[:, None, :], 0), axis=2)
+    target_count = jnp.sum(inside.astype(jnp.int32), axis=1)
 
     def over_lanes(x):
         return jnp.broadcast_to(x[:, None], (blocks * TILE, TILE))
 
     lse_rows, weight_rows = over_lanes(lse), over_lanes(loss_weight)
-    factor = over_lanes(jnp.where(inside, loss_weight, 0.0))
-    counts, where, lse_rows, weight_rows, factor = lax.optimization_barrier(
-        (block_counts, where, lse_rows, weight_rows, factor)
+    factor = over_lanes(jnp.where(inside.reshape(-1), loss_weight, 0.0))
+    target_list = target_list.reshape(-1)
+    counts, where, lse_rows, weight_rows, factor, target_list, target_count, target_code = (
+        lax.optimization_barrier(
+            (
+                *(block_counts, where, lse_rows, weight_rows, factor),
+                *(target_list, target_count, target_code),
+            )
+        )
     )
-    slot_blocks, slot_tiles, live, tiles = call(
+    slot_blocks, live, tiles = call(
         functools.partial(tiles_kernel, slots),
-        [shape_of((slots,), jnp.int32)] * 2
-        + [shape_of((1,), jnp.int32), shape_of((slots * TILE, features), bf16)],
+        [
+            shape_of((slots,), jnp.int32),
+            shape_of((1,), jnp.int32),
+            shape_of((slots * TILE, features), bf16),
+        ],
         [SMEM, SMEM, HBM],
         (block_tiles, counts, head_weight),
         0,
         slots * TILE * features * 2,
         [pltpu.SemaphoreType.DMA((slots,))],
         MEDIUM,
-        3,
+        2,
     )
     far[1], tiles = lax.optimization_barrier((far[1], tiles))
     near = [swap(part, "wide", 1) for part in far]
@@ -345,9 +402,23 @@
             share * TILE * TILE * 12,
         )
         if group == GROUPS - 1:
-            prob, clipped = lax.optimization_barrier((prob, clipped))
+            prob, target_code = lax.optimization_barrier((prob, target_code))
         probs.append([swap(prob, "narrow", k) for k in range(narrow)])
-    target_rows = head_weight.at[clipped].get(mode="promise_in_bounds")
+    (target_rows,) = call(
+        targets_kernel,
+        [shape_of((blocks * TILE, features), bf16)],
+        [SMEM, SMEM, VMEM, HBM],
+        (target_list, target_count, target_code, head_weight),
+        2 * blocks * AT_ONCE * GROUP_ROWS * TILE * features,
+        blocks * AT_ONCE * GROUP_ROWS * features * 2,
+        [
+            pltpu.VMEM((blocks, AT_ONCE * GROUP_ROWS, features), bf16),
+            pltpu.VMEM((AT_ONCE * GROUP_ROWS, features), bf16),
+            pltpu.SemaphoreType.DMA((blocks,)),
+            pltpu.SemaphoreType.DMA(()),
+        ],
+        MEDIUM,
+    )
     all_probs = [probs[group][k] for k in range(narrow) for group in range(GROUPS)]
 
     halves = []
@@ -355,16 +426,11 @@
         mine, other = call(
             functools.partial(grads_kernel, wide, narrow, slots, half),
             [shape_of((chips * TILE, width), f32)] * 2,
-            [SMEM] * 3 + [HBM] + [VMEM] * (narrow * GROUPS + 2),
-            (slot_blocks, slot_tiles, where, head_weight, *all_probs, target_rows, factor),
+            [SMEM] * 2 + [VMEM] * (narrow * GROUPS + 3),
+            (slot_blocks, where, tiles, *all_probs, target_rows, factor),
             2 * slots * TILE * TILE * width,
             slots * TILE * width * 4,
-            [
-                pltpu.VMEM((wide, TILE, width), f32),
-                pltpu.VMEM((slots, TILE, width), bf16),
-                pltpu.SemaphoreType.DMA((slots,)),
-            ],
-            MEDIUM,
+            [pltpu.VMEM((wide, TILE, width), f32)],
         )
         halves.append((mine, swap(other, "wide", 1)))
     units = gate_pre.shape[1]
@@ -379,7 +445,10 @@
             functools.partial(
                 unit_kernel, keys, [len(pieces[key]) for key in keys], kind, chunk, skip
             ),
-            [shape_of((TILE, units), bf16)] * 2 if last else [shape_of((TILE, units), f32)],
+            [shape_of((TILE, units), bf16)] * 2
+            if last
+            else [shape_of((TILE, units), f32)]
+            + [shape_of((TILE, features), bf16)] * (kind == "first"),
             [SMEM]
             + [VMEM] * len(inputs)
             + [HBM if skip is None else VMEM]
@@ -399,8 +468,6 @@
     pieces = {}
     grads = []
     for half, (mine, other) in enumerate(halves):
-        if half > 0:
-            mine, grads[-1] = lax.optimization_barrier((mine, grads[-1]))
         kept, *packed = call(
             functools.partial(pack_kernel, chips),
             [shape_of((TILE, width), f32)]
@@ -424,16 +491,11 @@
                 MEDIUM,
             )
             kept, held = lax.optimization_barrier((kept, held))
-        if half == HALVES - 1:
-            (summed,) = unit([(0, at) for at in range(half)], "first", None)
-            kept, summed = lax.optimization_barrier((kept, summed))
-        before = list(grads) if half == HALVES - 1 else []
-        full = [shape_of((TILE, features), bf16)] if before else []
-        grad, *head_grad = call(
-            functools.partial(merge_kernel, chips, len(before)),
-            [shape_of((TILE, width), bf16)] + full,
-            [VMEM] * (chips + len(before)),
-            (kept, *arrived, *before),
+        (grad,) = call(
+            merge_kernel,
+            [shape_of((TILE, width), bf16)],
+            [VMEM] * chips,
+            (kept, *arrived),
             chips * TILE * width * 4,
             chips * TILE * width * 3,
         )
@@ -445,10 +507,10 @@
         near_ends = lax.ppermute(grads[0], "narrow", [(1, 2), (2, 1)])
         ends = lax.ppermute(pieces[2, 0][0], "narrow", [(1, 0), (2, 3)])
         pieces[3, 0] = (near_ends, ends)
-    (summed,) = unit([(0, 1), *[(k, 0) for k in range(1, narrow)]], "more", None, summed)
+    early = [(0, half) for half in range(HALVES)] + [(k, 0) for k in range(1, narrow)]
+    summed, head_grad = unit(early, "first", None)
     (summed,) = unit(held_keys[:1], "more", 0, summed)
     gate_grad, up_grad = unit(held_keys[1:], "last", 1, summed, gate_pre, up_pre)
-    (head_grad,) = head_grad
     return head_grad, gate_grad, up_grad
 
 

time: 105 us -> 97.5 us (0.929)
  local copies, waits for them, and re-layouts: 12.9 us -> 3.46 us
  waiting for transfers between devices: 14.2 us -> 8.06 us
  starting transfers between devices: 41.9 us -> 45 us
  Pallas kernels: 34.2 us -> 36.8 us
  other arithmetic: 0.79 us -> 2.75 us
    gather x1 -> x0, local copies, waits for them, and re-layouts: 9.43 us -> none  [on_device(): target_rows = head_weight.at[clipped].get(mode='promise_in_bounds')]
    ppermute x32, waiting for transfers between devices: 14.2 us -> 4.85 us  [swap(): return lax.ppermute(x, axis, [(i, i ^ mask) for i in range(size)])]
    ppermute x1, waiting for transfers between devices: 0.01 us -> 3.21 us  [on_device(): ends = lax.ppermute(pieces[2, 0][0], 'narrow', [(1, 0), (2, 3)])]
    ppermute x32, starting transfers between devices: 39.8 us -> 42.9 us  [swap(): return lax.ppermute(x, axis, [(i, i ^ mask) for i in range(size)])]
    pallas_call x16, Pallas kernels: 34.2 us -> 36.8 us  [call(): pl.pallas_call(kernel, out_shape=outs, in_specs=ins, out_specs=[SMEM] * s...]
    reduce_sum x0 -> x3, other arithmetic: none -> 1.24 us  [the longest x1 0.81 us: on_device(): target_count = jnp.sum(inside.astype(jnp.int32), axis=1)]
  transfers between devices with their start and end apart: 34 -> 34, of which waited for: 9 -> 10; matrix products, arithmetic and copies ran while one was open for 13% -> 6% of each run, Pallas kernels for 25% -> 32%
where the time goes in v2:
time: 97.5 us; the launch traced here: 97 us
  starting transfers between devices  45 us (46%)
  Pallas kernels  36.8 us (38%)
  waiting for transfers between devices  8.06 us (8%)
  local copies, waits for them, and re-layouts  3.46 us (4%)
  other arithmetic  2.75 us (3%)
    ppermute x32, starting transfers between devices, swap(): return lax.ppermute(x, axis, [(i, i ^ mask) for i in range(size)])  42.9 us
    pallas_call x16, Pallas kernels, call(): pl.pallas_call(kernel, out_shape=outs, in_specs=ins, out_specs=[SMEM] * s...  36.8 us
    ppermute x32, waiting for transfers between devices, swap(): return lax.ppermute(x, axis, [(i, i ^ mask) for i in range(size)])  4.85 us
    ppermute x1, waiting for transfers between devices, on_device(): ends = lax.ppermute(pieces[2, 0][0], 'narrow', [(1, 0), (2, 3)])  3.21 us
    broadcast_in_dim x3, local copies, waits for them, and re-layouts, over_lanes(): return jnp.broadcast_to(x[:, None], (blocks * TILE, TILE))  1.95 us
  transfers between devices with their start and end apart: 34, of which 10 were waited for; matrix products, arithmetic and copies ran while one was open for 6% of the time, Pallas kernels for 32%

profile of v2, /device:TPU:0, one launch (start us, length us, event | category | flops | bytes accessed | tf_op | source)
XLA Modules:
  0.0 97.0 jit_solution(1809024012532922002)
XLA Ops:
  0.6 3.0 %collective-permute-start = (bf16[128,1024]{1,0:T(8,128)(2,1)}, bf16[128,1024]{1,0:T(8,128)(2,1)S(1)}, u32[]{:S(2)}, u32[]{:S(2)}) collective-permute-start(bf16[128,1024]{1,0:T(8,128)(2,1)} %refs_0_.3), channel_id=1, source_target_pairs={{0,8},{4,12},{8,0},{12,4},{16,24},{20,28},{24,16},{28,20},{1,9},{5... | collective-permute-start | bytes 786440 | tf_op jit(solution)/shard_map/ppermute | solution.py:30
  11.4 4.3 %shard_map.121 = (s32[16]{0:T(128)S(1)}, s32[1]{0:T(128)}, bf16[2048,1024]{1,0:T(8,128)(2,1)S(1)}) custom-call(s32[8,1,4]{2,1,0:T(1,128)S(1)} %copy.15.tiles_ref, s32[8,1]{1,0:T(8,128)S(1)} %copy.16.counts_ref, bf16[4096,1024]{1,0:T(8,128)(2,1)} %head.3), custom_call_target="tpu_custom_call" | custom-call | bytes 4194304 | tf_op jit(solution)/shard_map/pallas_call | solution.py:302
  19.2 1.6 %shard_map.124 = (f32[256,128]{1,0:T(8,128)S(1)}, s16[264,128]{1,0:T(8,128)(2,1)S(1)}, s16[264,128]{1,0:T(8,128)(2,1)S(1)}, s16[264,128]{1,0:T(8,128)(2,1)S(1)}) custom-call(s32[16]{0:T(128)S(1)} %get-tuple-element.48.blocks_ref, s32[2]{0:T(128)S(1)} %pad_add_fusion.where_ref, bf16[2048,1024]{1,0:T(8,128)(2,1)S(1)} %get-tuple-element.50.tiles, ...), custom_call_target="tpu_custom_call" | custom-call | flops 268435456 | bytes 2097152 | tf_op jit(solution)/shard_map/pallas_call | solution.py:302
  20.8 1.6 %collective-permute-start.10 = (s16[264,128]{1,0:T(8,128)(2,1)S(1)}, s16[264,128]{1,0:T(8,128)(2,1)S(1)}, u32[]{:S(2)}, u32[]{:S(2)}) collective-permute-start(s16[264,128]{1,0:T(8,128)(2,1)S(1)} %get-tuple-element.60), channel_id=1, source_target_pairs={{0,1},{1,0},{2,3},{3,2},{4,5},{5,4},{6,7},{7,6},{8,9},{9,8},{10,11... | collective-permute-start | bytes 202760 | tf_op jit(solution)/shard_map/ppermute | solution.py:30
  22.4 2.6 %collective-permute-start.11 = (s16[264,128]{1,0:T(8,128)(2,1)S(1)}, s16[264,128]{1,0:T(8,128)(2,1)S(1)}, u32[]{:S(2)}, u32[]{:S(2)}) collective-permute-start(s16[264,128]{1,0:T(8,128)(2,1)S(1)} %get-tuple-element.61), channel_id=1, source_target_pairs={{0,2},{1,3},{2,0},{3,1},{4,6},{5,7},{6,4},{7,5},{8,10},{9,11},{10,... | collective-permute-start | bytes 202760 | tf_op jit(solution)/shard_map/ppermute | solution.py:30
  25.2 1.6 %shard_map.122 = (f32[256,128]{1,0:T(8,128)S(1)}, s16[264,128]{1,0:T(8,128)(2,1)S(1)}, s16[264,128]{1,0:T(8,128)(2,1)S(1)}, s16[264,128]{1,0:T(8,128)(2,1)S(1)}) custom-call(s32[16]{0:T(128)S(1)} %get-tuple-element.48.blocks_ref, s32[2]{0:T(128)S(1)} %pad_add_fusion.where_ref, bf16[2048,1024]{1,0:T(8,128)(2,1)S(1)} %get-tuple-element.50.tiles, ...), custom_call_target="tpu_custom_call" | custom-call | flops 268435456 | bytes 2097152 | tf_op jit(solution)/shard_map/pallas_call | solution.py:302
  27.5 3.5 %collective-permute-start.8 = (s16[264,128]{1,0:T(8,128)(2,1)S(1)}, s16[264,128]{1,0:T(8,128)(2,1)S(1)}, u32[]{:S(2)}, u32[]{:S(2)}) collective-permute-start(s16[264,128]{1,0:T(8,128)(2,1)S(1)} %get-tuple-element.55), channel_id=1, source_target_pairs={{0,2},{1,3},{2,0},{3,1},{4,6},{5,7},{6,4},{7,5},{8,10},{9,11},{10,... | collective-permute-start | bytes 202760 | tf_op jit(solution)/shard_map/ppermute | solution.py:30
  32.6 2.4 %collective-permute-start.14 = (bf16[256,128]{1,0:T(8,128)(2,1)S(1)}, bf16[256,128]{1,0:T(8,128)(2,1)S(1)}, u32[]{:S(2)}, u32[]{:S(2)}) collective-permute-start(bf16[256,128]{1,0:T(8,128)(2,1)S(1)} %shard_map.125.refs_1_), channel_id=1, source_target_pairs={{0,1},{1,0},{2,3},{3,2},{4,5},{5,4},{6,7},{7,6},{8,9},{9,8},{10,11... | collective-permute-start | bytes 196616 | tf_op jit(solution)/shard_map/ppermute | solution.py:30
  35.0 1.9 %collective-permute-start.16 = (bf16[256,128]{1,0:T(8,128)(2,1)S(1)}, bf16[256,128]{1,0:T(8,128)(2,1)S(1)}, u32[]{:S(2)}, u32[]{:S(2)}) collective-permute-start(bf16[256,128]{1,0:T(8,128)(2,1)S(1)} %shard_map.125.refs_1_), channel_id=1, source_target_pairs={{0,2},{1,3},{2,0},{3,1},{4,6},{5,7},{6,4},{7,5},{8,10},{9,11},{10,... | collective-permute-start | bytes 196616 | tf_op jit(solution)/shard_map/ppermute | solution.py:30
  40.7 2.0 %collective-permute-start.15 = (bf16[256,128]{1,0:T(8,128)(2,1)S(1)}, bf16[256,128]{1,0:T(8,128)(2,1)S(1)}, u32[]{:S(2)}, u32[]{:S(2)}) collective-permute-start(bf16[256,128]{1,0:T(8,128)(2,1)S(1)} %shard_map.123.refs_0_), channel_id=1, source_target_pairs={{0,2},{1,3},{2,0},{3,1},{4,6},{5,7},{6,4},{7,5},{8,10},{9,11},{10,... | collective-permute-start | bytes 196616 | tf_op jit(solution)/shard_map/ppermute | solution.py:30
  44.1 8.5 %shard_map.126.refs_8_ = bf16[1024,1024]{1,0:T(8,128)(2,1)S(1)} custom-call(s32[1024]{0:T(1024)S(1)} %bitcast.36, s32[8]{0:T(128)S(1)} %get-tuple-element.66.count_ref, s32[8,128]{1,0:T(8,128)S(1)} %get-tuple-element.67.code, bf16[4096,1024]{1,0:T(8,128)(2,1)} %head.3), custom_call_target="tpu_custom_call" | custom-call | flops 536870912 | bytes 4194304 | tf_op jit(solution)/shard_map/pallas_call | solution.py:302
  52.6 1.7 %shard_map.127 = (f32[512,512]{1,0:T(8,128)S(1)}, f32[512,512]{1,0:T(8,128)S(1)}) custom-call(s32[16]{0:T(128)S(1)} %get-tuple-element.48.blocks_ref, s32[2]{0:T(128)S(1)} %pad_add_fusion.where_ref, bf16[2048,1024]{1,0:T(8,128)(2,1)S(1)} %get-tuple-element.50.tiles, bf16[256,128]{1,0:T(8,128)(2,1)S(1)} %shard_map.123.refs_0_, ...), custom_call_target="tpu_custom_call" | custom-call | flops 268435456 | bytes 4194304 | tf_op jit(solution)/shard_map/pallas_call | solution.py:302
  54.3 1.7 %shard_map.131 = (f32[512,512]{1,0:T(8,128)S(1)}, f32[512,512]{1,0:T(8,128)S(1)}) custom-call(s32[16]{0:T(128)S(1)} %get-tuple-element.48.blocks_ref, s32[2]{0:T(128)S(1)} %pad_add_fusion.where_ref, bf16[2048,1024]{1,0:T(8,128)(2,1)S(1)} %get-tuple-element.50.tiles, bf16[256,128]{1,0:T(8,128)(2,1)S(1)} %shard_map.123.refs_0_, ...), custom_call_target="tpu_custom_call" | custom-call | flops 268435456 | bytes 4194304 | tf_op jit(solution)/shard_map/pallas_call | solution.py:302
  57.2 1.7 %collective-permute-start.20 = (s16[136,512]{1,0:T(8,128)(2,1)S(1)}, s16[136,512]{1,0:T(8,128)(2,1)S(1)}, u32[]{:S(2)}, u32[]{:S(2)}) collective-permute-start(s16[136,512]{1,0:T(8,128)(2,1)S(1)} %get-tuple-element.75), channel_id=1, source_target_pairs={{0,8},{4,12},{8,0},{12,4},{16,24},{20,28},{24,16},{28,20},{1,9},{5... | collective-permute-start | bytes 417800 | tf_op jit(solution)/shard_map/ppermute | solution.py:30
  58.9 1.5 %collective-permute-start.21 = (s16[136,512]{1,0:T(8,128)(2,1)S(1)}, s16[136,512]{1,0:T(8,128)(2,1)S(1)}, u32[]{:S(2)}, u32[]{:S(2)}) collective-permute-start(s16[136,512]{1,0:T(8,128)(2,1)S(1)} %get-tuple-element.76), channel_id=1, source_target_pairs={{0,16},{4,20},{8,24},{12,28},{16,0},{20,4},{24,8},{28,12},{1,17},{... | collective-permute-start | bytes 417800 | tf_op jit(solution)/shard_map/ppermute | solution.py:30
  61.0 1.7 %collective-permute-start.24 = (s16[136,512]{1,0:T(8,128)(2,1)S(1)}, s16[136,512]{1,0:T(8,128)(2,1)S(1)}, u32[]{:S(2)}, u32[]{:S(2)}) collective-permute-start(s16[136,512]{1,0:T(8,128)(2,1)S(1)} %get-tuple-element.81), channel_id=1, source_target_pairs={{0,8},{4,12},{8,0},{12,4},{16,24},{20,28},{24,16},{28,20},{1,9},{5... | collective-permute-start | bytes 417800 | tf_op jit(solution)/shard_map/ppermute | solution.py:30
  62.6 3.2 %shard_map.129.refs_1_.refs_2_ = bf16[3,1792,512]{2,1,0:T(8,128)(2,1)S(1)} custom-call(s32[2]{0:T(128)S(1)} %pad_add_fusion.where_ref, bf16[1792,4096]{1,0:T(8,128)(2,1)} %refs_6_.1), custom_call_target="tpu_custom_call" | custom-call | bytes 5505024 | tf_op jit(solution)/shard_map/pallas_call | solution.py:302
  70.6 1.6 %collective-permute-start.26 = (s16[136,512]{1,0:T(8,128)(2,1)S(1)}, s16[136,512]{1,0:T(8,128)(2,1)S(1)}, u32[]{:S(2)}, u32[]{:S(2)}) collective-permute-start(s16[136,512]{1,0:T(8,128)(2,1)S(1)} %get-tuple-element.83), channel_id=1, source_target_pairs={{0,24},{4,28},{8,16},{12,20},{16,8},{20,12},{24,0},{28,4},{1,25},{... | collective-permute-start | bytes 417800 | tf_op jit(solution)/shard_map/ppermute | solution.py:30
  72.2 1.9 %collective-permute-start.27 = (bf16[128,512]{1,0:T(8,128)(2,1)S(1)}, bf16[128,512]{1,0:T(8,128)(2,1)S(1)}, u32[]{:S(2)}, u32[]{:S(2)}) collective-permute-start(bf16[128,512]{1,0:T(8,128)(2,1)S(1)} %shard_map.130.refs_0_), channel_id=1, source_target_pairs={{0,1},{1,0},{2,3},{3,2},{4,5},{5,4},{6,7},{7,6},{8,9},{9,8},{10,11... | collective-permute-start | bytes 393224 | tf_op jit(solution)/shard_map/ppermute | solution.py:30
  76.8 2.7 %collective-permute-start.33 = (bf16[128,512]{1,0:T(8,128)(2,1)S(1)}, bf16[128,512]{1,0:T(8,128)(2,1)S(1)}, u32[]{:S(2)}, u32[]{:S(2)}) collective-permute-start(bf16[128,512]{1,0:T(8,128)(2,1)S(1)} %shard_map.133.refs_1_), channel_id=1, source_target_pairs={{0,1},{1,0},{2,3},{3,2},{4,5},{5,4},{6,7},{7,6},{8,9},{9,8},{10,11... | collective-permute-start | bytes 393224 | tf_op jit(solution)/shard_map/ppermute | solution.py:30
  79.5 1.7 %collective-permute-start.31 = (bf16[128,512]{1,0:T(8,128)(2,1)S(1)}, bf16[128,512]{1,0:T(8,128)(2,1)S(1)}, u32[]{:S(2)}, u32[]{:S(2)}) collective-permute-start(bf16[128,512]{1,0:T(8,128)(2,1)S(1)} %shard_map.133.refs_1_), channel_id=1, source_target_pairs={{0,2},{1,3},{2,0},{3,1},{4,6},{5,7},{6,4},{7,5},{8,10},{9,11},{10,... | collective-permute-start | bytes 393224 | tf_op jit(solution)/shard_map/ppermute | solution.py:30
  82.6 3.2 %collective-permute-done.30.refs_5_ = bf16[128,512]{1,0:T(8,128)(2,1)S(1)} collective-permute-done((bf16[128,512]{1,0:T(8,128)(2,1)S(1)}, bf16[128,512]{1,0:T(8,128)(2,1)S(1)}, u32[]{:S(2)}, u32[]{:S(2)}) %collective-permute-start.30) | collective-permute-done | bytes 131104 | tf_op jit(solution)/shard_map/ppermute | solution.py:508
  85.8 7.0 %shard_map.134 = (f32[128,1792]{1,0:T(8,128)S(1)}, bf16[128,1024]{1,0:T(8,128)(2,1)}) custom-call(s32[2]{0:T(128)S(1)} %pad_add_fusion.where_ref, bf16[128,512]{1,0:T(8,128)(2,1)S(1)} %shard_map.130.refs_0_, bf16[128,512]{1,0:T(8,128)(2,1)S(1)} %shard_map.133.refs_1_, bf16[128,512]{1,0:T(8,128)(2,1)S(1)} %collective-permute-done.27.refs_2_, ...), custom_call_target="tpu_custom_call" | custom-call | flops 1174405120 | bytes 9175040 | tf_op jit(solution)/shard_map/pallas_call | solution.py:302
  94.2 2.9 %shard_map.136 = (bf16[128,1792]{1,0:T(8,128)(2,1)}, bf16[128,1792]{1,0:T(8,128)(2,1)}) custom-call(s32[2]{0:T(128)S(1)} %pad_add_fusion.where_ref, bf16[128,512]{1,0:T(8,128)(2,1)S(1)} %collective-permute-done.31.refs_0_, bf16[128,512]{1,0:T(8,128)(2,1)S(1)} %collective-permute-done.32.refs_1_, bf16[3,1792,512]{2,1,0:T(8,128)(2,1)S(1)} %shard_map.129.refs_1_.refs_2_, ...), custom_call_target="tpu_custom_call" | custom-call | flops 469762048 | bytes 3670016 | tf_op jit(solution)/shard_map/pallas_call | solution.py:302
  (78 shorter events, 30.6 us)
Async XLA Ops:
  0.6 15.2 %collective-permute-start = (bf16[128,1024]{1,0:T(8,128)(2,1)}, bf16[128,1024]{1,0:T(8,128)(2,1)S(1)}, u32[]{:S(2)}, u32[]{:S(2)}) collective-permute-start(bf16[128,1024]{1,0:T(8,128)(2,1)} %refs_0_.3), channel_id=1, source_target_pairs={{0,8},{4,12},{8,0},{12,4},{16,24},{20,28},{24,16},{28,20},{1,9},{5... | collective-permute-start | bytes 786440 | tf_op jit(solution)/shard_map/ppermute | solution.py:30
  3.7 13.6 %collective-permute-start.3 = (bf16[128,1024]{1,0:T(8,128)(2,1)}, bf16[128,1024]{1,0:T(8,128)(2,1)S(1)}, u32[]{:S(2)}, u32[]{:S(2)}) collective-permute-start(bf16[128,1024]{1,0:T(8,128)(2,1)} %refs_0_.3), channel_id=1, source_target_pairs={{0,16},{4,20},{8,24},{12,28},{16,0},{20,4},{24,8},{28,12},{1,17},{... | collective-permute-start | bytes 786440 | tf_op jit(solution)/shard_map/ppermute | solution.py:30
  5.2 12.1 %collective-permute-start.5 = (bf16[128,1024]{1,0:T(8,128)(2,1)}, bf16[128,1024]{1,0:T(8,128)(2,1)S(1)}, u32[]{:S(2)}, u32[]{:S(2)}) collective-permute-start(bf16[128,1024]{1,0:T(8,128)(2,1)} %refs_0_.3), channel_id=1, source_target_pairs={{0,24},{4,28},{8,16},{12,20},{16,8},{20,12},{24,0},{28,4},{1,25},{... | collective-permute-start | bytes 786440 | tf_op jit(solution)/shard_map/ppermute | solution.py:30
  5.2 12.6 %collective-permute-start.1 = (bf16[128,1024]{1,0:T(8,128)(2,1)}, bf16[128,1024]{1,0:T(8,128)(2,1)S(1)}, u32[]{:S(2)}, u32[]{:S(2)}) collective-permute-start(bf16[128,1024]{1,0:T(8,128)(2,1)} %refs_0_.3), channel_id=1, source_target_pairs={{0,4},{4,0},{8,12},{12,8},{16,20},{20,16},{24,28},{28,24},{1,5},{5... | collective-permute-start | bytes 786440 | tf_op jit(solution)/shard_map/ppermute | solution.py:30
  20.8 10.3 %collective-permute-start.10 = (s16[264,128]{1,0:T(8,128)(2,1)S(1)}, s16[264,128]{1,0:T(8,128)(2,1)S(1)}, u32[]{:S(2)}, u32[]{:S(2)}) collective-permute-start(s16[264,128]{1,0:T(8,128)(2,1)S(1)} %get-tuple-element.60), channel_id=1, source_target_pairs={{0,1},{1,0},{2,3},{3,2},{4,5},{5,4},{6,7},{7,6},{8,9},{9,8},{10,11... | collective-permute-start | bytes 202760 | tf_op jit(solution)/shard_map/ppermute | solution.py:30
  22.4 8.8 %collective-permute-start.11 = (s16[264,128]{1,0:T(8,128)(2,1)S(1)}, s16[264,128]{1,0:T(8,128)(2,1)S(1)}, u32[]{:S(2)}, u32[]{:S(2)}) collective-permute-start(s16[264,128]{1,0:T(8,128)(2,1)S(1)} %get-tuple-element.61), channel_id=1, source_target_pairs={{0,2},{1,3},{2,0},{3,1},{4,6},{5,7},{6,4},{7,5},{8,10},{9,11},{10,... | collective-permute-start | bytes 202760 | tf_op jit(solution)/shard_map/ppermute | solution.py:30
  26.8 10.1 %collective-permute-start.7 = (s16[264,128]{1,0:T(8,128)(2,1)S(1)}, s16[264,128]{1,0:T(8,128)(2,1)S(1)}, u32[]{:S(2)}, u32[]{:S(2)}) collective-permute-start(s16[264,128]{1,0:T(8,128)(2,1)S(1)} %get-tuple-element.54), channel_id=1, source_target_pairs={{0,1},{1,0},{2,3},{3,2},{4,5},{5,4},{6,7},{7,6},{8,9},{9,8},{10,11... | collective-permute-start | bytes 202760 | tf_op jit(solution)/shard_map/ppermute | solution.py:30
  27.5 10.8 %collective-permute-start.8 = (s16[264,128]{1,0:T(8,128)(2,1)S(1)}, s16[264,128]{1,0:T(8,128)(2,1)S(1)}, u32[]{:S(2)}, u32[]{:S(2)}) collective-permute-start(s16[264,128]{1,0:T(8,128)(2,1)S(1)} %get-tuple-element.55), channel_id=1, source_target_pairs={{0,2},{1,3},{2,0},{3,1},{4,6},{5,7},{6,4},{7,5},{8,10},{9,11},{10,... | collective-permute-start | bytes 202760 | tf_op jit(solution)/shard_map/ppermute | solution.py:30
  32.6 10.1 %collective-permute-start.14 = (bf16[256,128]{1,0:T(8,128)(2,1)S(1)}, bf16[256,128]{1,0:T(8,128)(2,1)S(1)}, u32[]{:S(2)}, u32[]{:S(2)}) collective-permute-start(bf16[256,128]{1,0:T(8,128)(2,1)S(1)} %shard_map.125.refs_1_), channel_id=1, source_target_pairs={{0,1},{1,0},{2,3},{3,2},{4,5},{5,4},{6,7},{7,6},{8,9},{9,8},{10,11... | collective-permute-start | bytes 196616 | tf_op jit(solution)/shard_map/ppermute | solution.py:30
  35.0 17.5 %collective-permute-start.16 = (bf16[256,128]{1,0:T(8,128)(2,1)S(1)}, bf16[256,128]{1,0:T(8,128)(2,1)S(1)}, u32[]{:S(2)}, u32[]{:S(2)}) collective-permute-start(bf16[256,128]{1,0:T(8,128)(2,1)S(1)} %shard_map.125.refs_1_), channel_id=1, source_target_pairs={{0,2},{1,3},{2,0},{3,1},{4,6},{5,7},{6,4},{7,5},{8,10},{9,11},{10,... | collective-permute-start | bytes 196616 | tf_op jit(solution)/shard_map/ppermute | solution.py:30
  36.9 15.6 %collective-permute-start.18 = (bf16[256,128]{1,0:T(8,128)(2,1)S(1)}, bf16[256,128]{1,0:T(8,128)(2,1)S(1)}, u32[]{:S(2)}, u32[]{:S(2)}) collective-permute-start(bf16[256,128]{1,0:T(8,128)(2,1)S(1)} %shard_map.125.refs_1_), channel_id=1, source_target_pairs={{0,3},{1,2},{2,1},{3,0},{4,7},{5,6},{6,5},{7,4},{8,11},{9,10},{10,... | collective-permute-start | bytes 196616 | tf_op jit(solution)/shard_map/ppermute | solution.py:30
  39.6 12.9 %collective-permute-start.13 = (bf16[256,128]{1,0:T(8,128)(2,1)S(1)}, bf16[256,128]{1,0:T(8,128)(2,1)S(1)}, u32[]{:S(2)}, u32[]{:S(2)}) collective-permute-start(bf16[256,128]{1,0:T(8,128)(2,1)S(1)} %shard_map.123.refs_0_), channel_id=1, source_target_pairs={{0,1},{1,0},{2,3},{3,2},{4,5},{5,4},{6,7},{7,6},{8,9},{9,8},{10,11... | collective-permute-start | bytes 196616 | tf_op jit(solution)/shard_map/ppermute | solution.py:30
  40.7 11.9 %collective-permute-start.15 = (bf16[256,128]{1,0:T(8,128)(2,1)S(1)}, bf16[256,128]{1,0:T(8,128)(2,1)S(1)}, u32[]{:S(2)}, u32[]{:S(2)}) collective-permute-start(bf16[256,128]{1,0:T(8,128)(2,1)S(1)} %shard_map.123.refs_0_), channel_id=1, source_target_pairs={{0,2},{1,3},{2,0},{3,1},{4,6},{5,7},{6,4},{7,5},{8,10},{9,11},{10,... | collective-permute-start | bytes 196616 | tf_op jit(solution)/shard_map/ppermute | solution.py:30
  42.7 9.9 %collective-permute-start.17 = (bf16[256,128]{1,0:T(8,128)(2,1)S(1)}, bf16[256,128]{1,0:T(8,128)(2,1)S(1)}, u32[]{:S(2)}, u32[]{:S(2)}) collective-permute-start(bf16[256,128]{1,0:T(8,128)(2,1)S(1)} %shard_map.123.refs_0_), channel_id=1, source_target_pairs={{0,3},{1,2},{2,1},{3,0},{4,7},{5,6},{6,5},{7,4},{8,11},{9,10},{10,... | collective-permute-start | bytes 196616 | tf_op jit(solution)/shard_map/ppermute | solution.py:30
  57.2 8.7 %collective-permute-start.20 = (s16[136,512]{1,0:T(8,128)(2,1)S(1)}, s16[136,512]{1,0:T(8,128)(2,1)S(1)}, u32[]{:S(2)}, u32[]{:S(2)}) collective-permute-start(s16[136,512]{1,0:T(8,128)(2,1)S(1)} %get-tuple-element.75), channel_id=1, source_target_pairs={{0,8},{4,12},{8,0},{12,4},{16,24},{20,28},{24,16},{28,20},{1,9},{5... | collective-permute-start | bytes 417800 | tf_op jit(solution)/shard_map/ppermute | solution.py:30
  58.9 7.8 %collective-permute-start.21 = (s16[136,512]{1,0:T(8,128)(2,1)S(1)}, s16[136,512]{1,0:T(8,128)(2,1)S(1)}, u32[]{:S(2)}, u32[]{:S(2)}) collective-permute-start(s16[136,512]{1,0:T(8,128)(2,1)S(1)} %get-tuple-element.76), channel_id=1, source_target_pairs={{0,16},{4,20},{8,24},{12,28},{16,0},{20,4},{24,8},{28,12},{1,17},{... | collective-permute-start | bytes 417800 | tf_op jit(solution)/shard_map/ppermute | solution.py:30
  60.4 7.5 %collective-permute-start.22 = (s16[136,512]{1,0:T(8,128)(2,1)S(1)}, s16[136,512]{1,0:T(8,128)(2,1)S(1)}, u32[]{:S(2)}, u32[]{:S(2)}) collective-permute-start(s16[136,512]{1,0:T(8,128)(2,1)S(1)} %get-tuple-element.77), channel_id=1, source_target_pairs={{0,24},{4,28},{8,16},{12,20},{16,8},{20,12},{24,0},{28,4},{1,25},{... | collective-permute-start | bytes 417800 | tf_op jit(solution)/shard_map/ppermute | solution.py:30
  61.0 13.1 %collective-permute-start.24 = (s16[136,512]{1,0:T(8,128)(2,1)S(1)}, s16[136,512]{1,0:T(8,128)(2,1)S(1)}, u32[]{:S(2)}, u32[]{:S(2)}) collective-permute-start(s16[136,512]{1,0:T(8,128)(2,1)S(1)} %get-tuple-element.81), channel_id=1, source_target_pairs={{0,8},{4,12},{8,0},{12,4},{16,24},{20,28},{24,16},{28,20},{1,9},{5... | collective-permute-start | bytes 417800 | tf_op jit(solution)/shard_map/ppermute | solution.py:30
  72.2 9.0 %collective-permute-start.27 = (bf16[128,512]{1,0:T(8,128)(2,1)S(1)}, bf16[128,512]{1,0:T(8,128)(2,1)S(1)}, u32[]{:S(2)}, u32[]{:S(2)}) collective-permute-start(bf16[128,512]{1,0:T(8,128)(2,1)S(1)} %shard_map.130.refs_0_), channel_id=1, source_target_pairs={{0,1},{1,0},{2,3},{3,2},{4,5},{5,4},{6,7},{7,6},{8,9},{9,8},{10,11... | collective-permute-start | bytes 393224 | tf_op jit(solution)/shard_map/ppermute | solution.py:30
  74.1 8.5 %collective-permute-start.29 = (bf16[128,512]{1,0:T(8,128)(2,1)S(1)}, bf16[128,512]{1,0:T(8,128)(2,1)S(1)}, u32[]{:S(2)}, u32[]{:S(2)}) collective-permute-start(bf16[128,512]{1,0:T(8,128)(2,1)S(1)} %shard_map.130.refs_0_), channel_id=1, source_target_pairs={{1,2},{2,1},{5,6},{6,5},{9,10},{10,9},{13,14},{14,13},{17,18},{18,... | collective-permute-start | bytes 393224 | tf_op jit(solution)/shard_map/ppermute | solution.py:507
  75.2 10.7 %collective-permute-start.30 = (bf16[128,512]{1,0:T(8,128)(2,1)S(1)}, bf16[128,512]{1,0:T(8,128)(2,1)S(1)}, u32[]{:S(2)}, u32[]{:S(2)}) collective-permute-start(bf16[128,512]{1,0:T(8,128)(2,1)S(1)} %collective-permute-done.28.refs_3_), channel_id=1, source_target_pairs={{1,0},{2,3},{5,4},{6,7},{9,8},{10,11},{13,12},{14,15},{17,16},{18,... | collective-permute-start | bytes 393224 | tf_op jit(solution)/shard_map/ppermute | solution.py:508
  76.8 16.1 %collective-permute-start.33 = (bf16[128,512]{1,0:T(8,128)(2,1)S(1)}, bf16[128,512]{1,0:T(8,128)(2,1)S(1)}, u32[]{:S(2)}, u32[]{:S(2)}) collective-permute-start(bf16[128,512]{1,0:T(8,128)(2,1)S(1)} %shard_map.133.refs_1_), channel_id=1, source_target_pairs={{0,1},{1,0},{2,3},{3,2},{4,5},{5,4},{6,7},{7,6},{8,9},{9,8},{10,11... | collective-permute-start | bytes 393224 | tf_op jit(solution)/shard_map/ppermute | solution.py:30
  79.5 14.6 %collective-permute-start.31 = (bf16[128,512]{1,0:T(8,128)(2,1)S(1)}, bf16[128,512]{1,0:T(8,128)(2,1)S(1)}, u32[]{:S(2)}, u32[]{:S(2)}) collective-permute-start(bf16[128,512]{1,0:T(8,128)(2,1)S(1)} %shard_map.133.refs_1_), channel_id=1, source_target_pairs={{0,2},{1,3},{2,0},{3,1},{4,6},{5,7},{6,4},{7,5},{8,10},{9,11},{10,... | collective-permute-start | bytes 393224 | tf_op jit(solution)/shard_map/ppermute | solution.py:30
  81.2 12.9 %collective-permute-start.32 = (bf16[128,512]{1,0:T(8,128)(2,1)S(1)}, bf16[128,512]{1,0:T(8,128)(2,1)S(1)}, u32[]{:S(2)}, u32[]{:S(2)}) collective-permute-start(bf16[128,512]{1,0:T(8,128)(2,1)S(1)} %shard_map.133.refs_1_), channel_id=1, source_target_pairs={{0,3},{1,2},{2,1},{3,0},{4,7},{5,6},{6,5},{7,4},{8,11},{9,10},{10,... | collective-permute-start | bytes 393224 | tf_op jit(solution)/shard_map/ppermute | solution.py:30
  (13 other events, 68.0 us)

commit v3 on v2

--- a/solution.py
+++ b/solution.py
@@ -13,7 +13,7 @@
 GROUPS = 2
 HALVES = 2
 GROUP_ROWS = 8
-AT_ONCE = 32
+AT_ONCE = 24
 LARGE = 50
 MEDIUM = 46
 LEVELS = 32767.0
@@ -339,12 +339,22 @@
     local_ids = (targets - me_w * vocab_here).reshape(blocks, TILE)
     inside = (local_ids >= 0) & (local_ids < vocab_here)
     order = jnp.arange(TILE, dtype=jnp.int32)
-    earlier = (order[None, :] < order[:, None])[None] & inside[:, None, :]
-    rank = jnp.sum(earlier.astype(jnp.int32), axis=2)
-    target_code = jnp.where(inside, rank * GROUP_ROWS + local_ids % GROUP_ROWS, -1)
-    chosen = (rank[:, None, :] == order[None, :, None]) & inside[:, None, :]
-    target_list = jnp.sum(jnp.where(chosen, (local_ids // GROUP_ROWS)[:, None, :], 0), axis=2)
-    target_count = jnp.sum(inside.astype(jnp.int32), axis=1)
+    earlier = (order[None, :] < order[:, None])[None]
+    group_ids = jnp.where(inside, local_ids // GROUP_ROWS, -1)
+    same = group_ids[:, :, None] == group_ids[:, None, :]
+    first = inside & (jnp.sum((same & earlier).astype(jnp.int32), axis=2) == 0)
+    rank = jnp.sum((earlier & first[:, None, :]).astype(jnp.int32), axis=2)
+    spot = jnp.sum(jnp.where(same & first[:, None, :], rank[:, None, :], 0), axis=2)
+    target_code = jnp.where(inside, spot * GROUP_ROWS + local_ids % GROUP_ROWS, -1)
+    chosen = first[:, None, :] & (rank[:, None, :] == order[None, :, None])
+    target_list = jnp.sum(jnp.where(chosen, group_ids[:, None, :], 0), axis=2)
+    target_count = jnp.sum(first.astype(jnp.int32), axis=1)
+    spare = jnp.arange(blocks * TILE, dtype=jnp.int32).reshape(blocks, TILE)
+    target_list = jnp.where(
+        order[None, :] < target_count[:, None],
+        target_list,
+        spare % (vocab_here // GROUP_ROWS),
+    )
 
     def over_lanes(x):
         return jnp.broadcast_to(x[:, None], (blocks * TILE, TILE))
@@ -434,7 +444,7 @@
         )
         halves.append((mine, swap(other, "wide", 1)))
     units = gate_pre.shape[1]
-    held_keys = [(k, HALVES - 1) for k in range(1, narrow)]
+    held_keys = [(k, HALVES - 1) for k in range(2, narrow)]
     chunk = units // 2 if units // 2 % TILE == 0 else units
 
     def unit(keys, kind, skip, *extra):
@@ -507,10 +517,10 @@
         near_ends = lax.ppermute(grads[0], "narrow", [(1, 2), (2, 1)])
         ends = lax.ppermute(pieces[2, 0][0], "narrow", [(1, 0), (2, 3)])
         pieces[3, 0] = (near_ends, ends)
-    early = [(0, half) for half in range(HALVES)] + [(k, 0) for k in range(1, narrow)]
+    early = [(0, half) for half in range(HALVES)] + [(k, 0) for k in range(1, narrow - 1)]
     summed, head_grad = unit(early, "first", None)
-    (summed,) = unit(held_keys[:1], "more", 0, summed)
-    gate_grad, up_grad = unit(held_keys[1:], "last", 1, summed, gate_pre, up_pre)
+    (summed,) = unit([(narrow - 1, 0), (1, 1)], "more", None, summed)
+    gate_grad, up_grad = unit(held_keys, "last", 0, summed, gate_pre, up_pre)
     return head_grad, gate_grad, up_grad
 
 

time: 97.5 us -> 94.4 us (0.968)
  Pallas kernels: 36.8 us -> 32.3 us
  other arithmetic: 2.75 us -> 4.16 us
  waiting for transfers between devices: 8.06 us -> 6.85 us
  starting transfers between devices: 45 us -> 46.1 us
    pallas_call x16, Pallas kernels: 36.8 us -> 32.3 us  [call(): pl.pallas_call(kernel, out_shape=outs, in_specs=ins, out_specs=[SMEM] * s...]
    ppermute x1, waiting for transfers between devices: 3.21 us -> 0.01 us  [on_device(): ends = lax.ppermute(pieces[2, 0][0], 'narrow', [(1, 0), (2, 3)])]
    ppermute x32, waiting for transfers between devices: 4.85 us -> 6.85 us  [swap(): return lax.ppermute(x, axis, [(i, i ^ mask) for i in range(size)])]
    ppermute x32, starting transfers between devices: 42.9 us -> 44 us  [swap(): return lax.ppermute(x, axis, [(i, i ^ mask) for i in range(size)])]
  transfers between devices with their start and end apart: 34 -> 34, of which waited for: 10 -> 9; matrix products, arithmetic and copies ran while one was open for 6% -> 8% of each run, Pallas kernels for 32% -> 28%
where the time goes in v3:
time: 94.4 us; the launch traced here: 93.9 us
  starting transfers between devices  46.1 us (49%)
  Pallas kernels  32.3 us (34%)
  waiting for transfers between devices  6.85 us (7%)
  other arithmetic  4.16 us (4%)
  local copies, waits for them, and re-layouts  3.46 us (4%)
  between operations  0.97 us (1%)
    ppermute x32, starting transfers between devices, swap(): return lax.ppermute(x, axis, [(i, i ^ mask) for i in range(size)])  44 us
    pallas_call x16, Pallas kernels, call(): pl.pallas_call(kernel, out_shape=outs, in_specs=ins, out_specs=[SMEM] * s...  32.3 us
    ppermute x32, waiting for transfers between devices, swap(): return lax.ppermute(x, axis, [(i, i ^ mask) for i in range(size)])  6.85 us
    broadcast_in_dim x3, local copies, waits for them, and re-layouts, over_lanes(): return jnp.broadcast_to(x[:, None], (blocks * TILE, TILE))  1.95 us
  transfers between devices with their start and end apart: 34, of which 9 were waited for; matrix products, arithmetic and copies ran while one was open for 8% of the time, Pallas kernels for 28%

profile of v3, /device:TPU:0, one launch (start us, length us, event | category | flops | bytes accessed | tf_op | source)
XLA Modules:
  0.0 93.9 jit_solution(3649532505807316673)
XLA Ops:
  0.6 3.0 %collective-permute-start = (bf16[128,1024]{1,0:T(8,128)(2,1)}, bf16[128,1024]{1,0:T(8,128)(2,1)S(1)}, u32[]{:S(2)}, u32[]{:S(2)}) collective-permute-start(bf16[128,1024]{1,0:T(8,128)(2,1)} %refs_0_.3), channel_id=1, source_target_pairs={{0,8},{4,12},{8,0},{12,4},{16,24},{20,28},{24,16},{28,20},{1,9},{5... | collective-permute-start | bytes 786440 | tf_op jit(solution)/shard_map/ppermute | solution.py:30
  12.9 4.3 %shard_map.121 = (s32[16]{0:T(128)S(1)}, s32[1]{0:T(128)}, bf16[2048,1024]{1,0:T(8,128)(2,1)S(1)}) custom-call(s32[8,1,4]{2,1,0:T(1,128)S(1)} %copy.15.tiles_ref, s32[8,1]{1,0:T(8,128)S(1)} %copy.16.counts_ref, bf16[4096,1024]{1,0:T(8,128)(2,1)} %head.3), custom_call_target="tpu_custom_call" | custom-call | bytes 4194304 | tf_op jit(solution)/shard_map/pallas_call | solution.py:302
  20.1 1.6 %shard_map.124 = (f32[256,128]{1,0:T(8,128)S(1)}, s16[264,128]{1,0:T(8,128)(2,1)S(1)}, s16[264,128]{1,0:T(8,128)(2,1)S(1)}, s16[264,128]{1,0:T(8,128)(2,1)S(1)}) custom-call(s32[16]{0:T(128)S(1)} %get-tuple-element.48.blocks_ref, s32[2]{0:T(128)S(1)} %pad_add_fusion.where_ref, bf16[2048,1024]{1,0:T(8,128)(2,1)S(1)} %get-tuple-element.50.tiles, ...), custom_call_target="tpu_custom_call" | custom-call | flops 268435456 | bytes 2097152 | tf_op jit(solution)/shard_map/pallas_call | solution.py:302
  21.7 2.1 %collective-permute-start.10 = (s16[264,128]{1,0:T(8,128)(2,1)S(1)}, s16[264,128]{1,0:T(8,128)(2,1)S(1)}, u32[]{:S(2)}, u32[]{:S(2)}) collective-permute-start(s16[264,128]{1,0:T(8,128)(2,1)S(1)} %get-tuple-element.60), channel_id=1, source_target_pairs={{0,1},{1,0},{2,3},{3,2},{4,5},{5,4},{6,7},{7,6},{8,9},{9,8},{10,11... | collective-permute-start | bytes 202760 | tf_op jit(solution)/shard_map/ppermute | solution.py:30
  23.8 2.6 %collective-permute-start.11 = (s16[264,128]{1,0:T(8,128)(2,1)S(1)}, s16[264,128]{1,0:T(8,128)(2,1)S(1)}, u32[]{:S(2)}, u32[]{:S(2)}) collective-permute-start(s16[264,128]{1,0:T(8,128)(2,1)S(1)} %get-tuple-element.61), channel_id=1, source_target_pairs={{0,2},{1,3},{2,0},{3,1},{4,6},{5,7},{6,4},{7,5},{8,10},{9,11},{10,... | collective-permute-start | bytes 202760 | tf_op jit(solution)/shard_map/ppermute | solution.py:30
  26.4 1.6 %shard_map.122 = (f32[256,128]{1,0:T(8,128)S(1)}, s16[264,128]{1,0:T(8,128)(2,1)S(1)}, s16[264,128]{1,0:T(8,128)(2,1)S(1)}, s16[264,128]{1,0:T(8,128)(2,1)S(1)}) custom-call(s32[16]{0:T(128)S(1)} %get-tuple-element.48.blocks_ref, s32[2]{0:T(128)S(1)} %pad_add_fusion.where_ref, bf16[2048,1024]{1,0:T(8,128)(2,1)S(1)} %get-tuple-element.50.tiles, ...), custom_call_target="tpu_custom_call" | custom-call | flops 268435456 | bytes 2097152 | tf_op jit(solution)/shard_map/pallas_call | solution.py:302
  28.9 3.5 %collective-permute-start.8 = (s16[264,128]{1,0:T(8,128)(2,1)S(1)}, s16[264,128]{1,0:T(8,128)(2,1)S(1)}, u32[]{:S(2)}, u32[]{:S(2)}) collective-permute-start(s16[264,128]{1,0:T(8,128)(2,1)S(1)} %get-tuple-element.55), channel_id=1, source_target_pairs={{0,2},{1,3},{2,0},{3,1},{4,6},{5,7},{6,4},{7,5},{8,10},{9,11},{10,... | collective-permute-start | bytes 202760 | tf_op jit(solution)/shard_map/ppermute | solution.py:30
  34.0 2.4 %collective-permute-start.14 = (bf16[256,128]{1,0:T(8,128)(2,1)S(1)}, bf16[256,128]{1,0:T(8,128)(2,1)S(1)}, u32[]{:S(2)}, u32[]{:S(2)}) collective-permute-start(bf16[256,128]{1,0:T(8,128)(2,1)S(1)} %shard_map.125.refs_1_), channel_id=1, source_target_pairs={{0,1},{1,0},{2,3},{3,2},{4,5},{5,4},{6,7},{7,6},{8,9},{9,8},{10,11... | collective-permute-start | bytes 196616 | tf_op jit(solution)/shard_map/ppermute | solution.py:30
  36.4 3.3 %collective-permute-start.16 = (bf16[256,128]{1,0:T(8,128)(2,1)S(1)}, bf16[256,128]{1,0:T(8,128)(2,1)S(1)}, u32[]{:S(2)}, u32[]{:S(2)}) collective-permute-start(bf16[256,128]{1,0:T(8,128)(2,1)S(1)} %shard_map.125.refs_1_), channel_id=1, source_target_pairs={{0,2},{1,3},{2,0},{3,1},{4,6},{5,7},{6,4},{7,5},{8,10},{9,11},{10,... | collective-permute-start | bytes 196616 | tf_op jit(solution)/shard_map/ppermute | solution.py:30
  43.0 2.4 %collective-permute-start.15 = (bf16[256,128]{1,0:T(8,128)(2,1)S(1)}, bf16[256,128]{1,0:T(8,128)(2,1)S(1)}, u32[]{:S(2)}, u32[]{:S(2)}) collective-permute-start(bf16[256,128]{1,0:T(8,128)(2,1)S(1)} %shard_map.123.refs_0_), channel_id=1, source_target_pairs={{0,2},{1,3},{2,0},{3,1},{4,6},{5,7},{6,4},{7,5},{8,10},{9,11},{10,... | collective-permute-start | bytes 196616 | tf_op jit(solution)/shard_map/ppermute | solution.py:30
  46.8 3.8 %shard_map.126.refs_8_ = bf16[1024,1024]{1,0:T(8,128)(2,1)S(1)} custom-call(s32[1024]{0:T(1024)S(1)} %fusion.3.list_ref, s32[8]{0:T(128)S(1)} %get-tuple-element.66.count_ref, s32[8,128]{1,0:T(8,128)S(1)} %fusion.5.code, bf16[4096,1024]{1,0:T(8,128)(2,1)} %head.3), custom_call_target="tpu_custom_call" | custom-call | flops 402653184 | bytes 3145728 | tf_op jit(solution)/shard_map/pallas_call | solution.py:302
  51.5 1.7 %shard_map.127 = (f32[512,512]{1,0:T(8,128)S(1)}, f32[512,512]{1,0:T(8,128)S(1)}) custom-call(s32[16]{0:T(128)S(1)} %get-tuple-element.48.blocks_ref, s32[2]{0:T(128)S(1)} %pad_add_fusion.where_ref, bf16[2048,1024]{1,0:T(8,128)(2,1)S(1)} %get-tuple-element.50.tiles, bf16[256,128]{1,0:T(8,128)(2,1)S(1)} %shard_map.123.refs_0_, ...), custom_call_target="tpu_custom_call" | custom-call | flops 268435456 | bytes 4194304 | tf_op jit(solution)/shard_map/pallas_call | solution.py:302
  53.2 1.7 %shard_map.131 = (f32[512,512]{1,0:T(8,128)S(1)}, f32[512,512]{1,0:T(8,128)S(1)}) custom-call(s32[16]{0:T(128)S(1)} %get-tuple-element.48.blocks_ref, s32[2]{0:T(128)S(1)} %pad_add_fusion.where_ref, bf16[2048,1024]{1,0:T(8,128)(2,1)S(1)} %get-tuple-element.50.tiles, bf16[256,128]{1,0:T(8,128)(2,1)S(1)} %shard_map.123.refs_0_, ...), custom_call_target="tpu_custom_call" | custom-call | flops 268435456 | bytes 4194304 | tf_op jit(solution)/shard_map/pallas_call | solution.py:302
  56.2 2.4 %collective-permute-start.21 = (s16[136,512]{1,0:T(8,128)(2,1)S(1)}, s16[136,512]{1,0:T(8,128)(2,1)S(1)}, u32[]{:S(2)}, u32[]{:S(2)}) collective-permute-start(s16[136,512]{1,0:T(8,128)(2,1)S(1)} %get-tuple-element.76), channel_id=1, source_target_pairs={{0,16},{4,20},{8,24},{12,28},{16,0},{20,4},{24,8},{28,12},{1,17},{... | collective-permute-start | bytes 417800 | tf_op jit(solution)/shard_map/ppermute | solution.py:30
  60.3 2.0 %collective-permute-start.25 = (s16[136,512]{1,0:T(8,128)(2,1)S(1)}, s16[136,512]{1,0:T(8,128)(2,1)S(1)}, u32[]{:S(2)}, u32[]{:S(2)}) collective-permute-start(s16[136,512]{1,0:T(8,128)(2,1)S(1)} %get-tuple-element.82), channel_id=1, source_target_pairs={{0,16},{4,20},{8,24},{12,28},{16,0},{20,4},{24,8},{28,12},{1,17},{... | collective-permute-start | bytes 417800 | tf_op jit(solution)/shard_map/ppermute | solution.py:30
  62.7 1.8 %collective-permute-start.26 = (s16[136,512]{1,0:T(8,128)(2,1)S(1)}, s16[136,512]{1,0:T(8,128)(2,1)S(1)}, u32[]{:S(2)}, u32[]{:S(2)}) collective-permute-start(s16[136,512]{1,0:T(8,128)(2,1)S(1)} %get-tuple-element.83), channel_id=1, source_target_pairs={{0,24},{4,28},{8,16},{12,20},{16,8},{20,12},{24,0},{28,4},{1,25},{... | collective-permute-start | bytes 417800 | tf_op jit(solution)/shard_map/ppermute | solution.py:30
  64.5 2.6 %shard_map.129.refs_2_ = bf16[2,1792,512]{2,1,0:T(8,128)(2,1)S(1)} custom-call(s32[2]{0:T(128)S(1)} %pad_add_fusion.where_ref, bf16[1792,4096]{1,0:T(8,128)(2,1)} %refs_3_.1), custom_call_target="tpu_custom_call" | custom-call | bytes 3670016 | tf_op jit(solution)/shard_map/pallas_call | solution.py:302
  71.3 1.7 %collective-permute-start.33 = (bf16[128,512]{1,0:T(8,128)(2,1)S(1)}, bf16[128,512]{1,0:T(8,128)(2,1)S(1)}, u32[]{:S(2)}, u32[]{:S(2)}) collective-permute-start(bf16[128,512]{1,0:T(8,128)(2,1)S(1)} %shard_map.133.refs_1_), channel_id=1, source_target_pairs={{0,1},{1,0},{2,3},{3,2},{4,5},{5,4},{6,7},{7,6},{8,9},{9,8},{10,11... | collective-permute-start | bytes 393224 | tf_op jit(solution)/shard_map/ppermute | solution.py:30
  73.0 2.4 %collective-permute-done.28.refs_3_ = bf16[128,512]{1,0:T(8,128)(2,1)S(1)} collective-permute-done((bf16[128,512]{1,0:T(8,128)(2,1)S(1)}, bf16[128,512]{1,0:T(8,128)(2,1)S(1)}, u32[]{:S(2)}, u32[]{:S(2)}) %collective-permute-start.28) | collective-permute-done | bytes 131104 | tf_op jit(solution)/shard_map/ppermute | solution.py:30
  76.8 3.1 %collective-permute-start.29 = (bf16[128,512]{1,0:T(8,128)(2,1)S(1)}, bf16[128,512]{1,0:T(8,128)(2,1)S(1)}, u32[]{:S(2)}, u32[]{:S(2)}) collective-permute-start(bf16[128,512]{1,0:T(8,128)(2,1)S(1)} %shard_map.133.refs_1_), channel_id=1, source_target_pairs={{0,2},{1,3},{2,0},{3,1},{4,6},{5,7},{6,4},{7,5},{8,10},{9,11},{10,... | collective-permute-start | bytes 393224 | tf_op jit(solution)/shard_map/ppermute | solution.py:30
  79.9 2.0 %collective-permute-start.30 = (bf16[128,512]{1,0:T(8,128)(2,1)S(1)}, bf16[128,512]{1,0:T(8,128)(2,1)S(1)}, u32[]{:S(2)}, u32[]{:S(2)}) collective-permute-start(bf16[128,512]{1,0:T(8,128)(2,1)S(1)} %shard_map.133.refs_1_), channel_id=1, source_target_pairs={{0,3},{1,2},{2,1},{3,0},{4,7},{5,6},{6,5},{7,4},{8,11},{9,10},{10,... | collective-permute-start | bytes 393224 | tf_op jit(solution)/shard_map/ppermute | solution.py:30
  81.9 5.6 %shard_map.134 = (f32[128,1792]{1,0:T(8,128)S(1)}, bf16[128,1024]{1,0:T(8,128)(2,1)}) custom-call(s32[2]{0:T(128)S(1)} %pad_add_fusion.where_ref, bf16[128,512]{1,0:T(8,128)(2,1)S(1)} %shard_map.130.refs_0_, bf16[128,512]{1,0:T(8,128)(2,1)S(1)} %shard_map.133.refs_1_, bf16[128,512]{1,0:T(8,128)(2,1)S(1)} %collective-permute-done.27.refs_2_, ...), custom_call_target="tpu_custom_call" | custom-call | flops 939524096 | bytes 7340032 | tf_op jit(solution)/shard_map/pallas_call | solution.py:302
  87.6 3.4 %shard_map.135.refs_3_ = f32[128,1792]{1,0:T(8,128)S(1)} custom-call(s32[2]{0:T(128)S(1)} %pad_add_fusion.where_ref, bf16[128,512]{1,0:T(8,128)(2,1)S(1)} %collective-permute-done.31.refs_0_, bf16[128,512]{1,0:T(8,128)(2,1)S(1)} %collective-permute-done.32.refs_1_, bf16[128,512]{1,0:T(8,128)(2,1)S(1)} %collective-permute-done.33.refs_2_, ...), custom_call_target="tpu_custom_call" | custom-call | flops 469762048 | bytes 3670016 | tf_op jit(solution)/shard_map/pallas_call | solution.py:302
  91.0 2.9 %shard_map.136 = (bf16[128,1792]{1,0:T(8,128)(2,1)}, bf16[128,1792]{1,0:T(8,128)(2,1)}) custom-call(s32[2]{0:T(128)S(1)} %pad_add_fusion.where_ref, bf16[128,512]{1,0:T(8,128)(2,1)S(1)} %collective-permute-done.29.refs_0_, bf16[128,512]{1,0:T(8,128)(2,1)S(1)} %collective-permute-done.30.refs_1_, bf16[2,1792,512]{2,1,0:T(8,128)(2,1)S(1)} %shard_map.129.refs_2_, ...), custom_call_target="tpu_custom_call" | custom-call | flops 469762048 | bytes 3670016 | tf_op jit(solution)/shard_map/pallas_call | solution.py:302
  (81 shorter events, 29.2 us)
Async XLA Ops:
  0.6 16.6 %collective-permute-start = (bf16[128,1024]{1,0:T(8,128)(2,1)}, bf16[128,1024]{1,0:T(8,128)(2,1)S(1)}, u32[]{:S(2)}, u32[]{:S(2)}) collective-permute-start(bf16[128,1024]{1,0:T(8,128)(2,1)} %refs_0_.3), channel_id=1, source_target_pairs={{0,8},{4,12},{8,0},{12,4},{16,24},{20,28},{24,16},{28,20},{1,9},{5... | collective-permute-start | bytes 786440 | tf_op jit(solution)/shard_map/ppermute | solution.py:30
  3.7 14.6 %collective-permute-start.3 = (bf16[128,1024]{1,0:T(8,128)(2,1)}, bf16[128,1024]{1,0:T(8,128)(2,1)S(1)}, u32[]{:S(2)}, u32[]{:S(2)}) collective-permute-start(bf16[128,1024]{1,0:T(8,128)(2,1)} %refs_0_.3), channel_id=1, source_target_pairs={{0,16},{4,20},{8,24},{12,28},{16,0},{20,4},{24,8},{28,12},{1,17},{... | collective-permute-start | bytes 786440 | tf_op jit(solution)/shard_map/ppermute | solution.py:30
  5.2 13.1 %collective-permute-start.5 = (bf16[128,1024]{1,0:T(8,128)(2,1)}, bf16[128,1024]{1,0:T(8,128)(2,1)S(1)}, u32[]{:S(2)}, u32[]{:S(2)}) collective-permute-start(bf16[128,1024]{1,0:T(8,128)(2,1)} %refs_0_.3), channel_id=1, source_target_pairs={{0,24},{4,28},{8,16},{12,20},{16,8},{20,12},{24,0},{28,4},{1,25},{... | collective-permute-start | bytes 786440 | tf_op jit(solution)/shard_map/ppermute | solution.py:30
  5.2 13.5 %collective-permute-start.1 = (bf16[128,1024]{1,0:T(8,128)(2,1)}, bf16[128,1024]{1,0:T(8,128)(2,1)S(1)}, u32[]{:S(2)}, u32[]{:S(2)}) collective-permute-start(bf16[128,1024]{1,0:T(8,128)(2,1)} %refs_0_.3), channel_id=1, source_target_pairs={{0,4},{4,0},{8,12},{12,8},{16,20},{20,16},{24,28},{28,24},{1,5},{5... | collective-permute-start | bytes 786440 | tf_op jit(solution)/shard_map/ppermute | solution.py:30
  21.7 10.7 %collective-permute-start.10 = (s16[264,128]{1,0:T(8,128)(2,1)S(1)}, s16[264,128]{1,0:T(8,128)(2,1)S(1)}, u32[]{:S(2)}, u32[]{:S(2)}) collective-permute-start(s16[264,128]{1,0:T(8,128)(2,1)S(1)} %get-tuple-element.60), channel_id=1, source_target_pairs={{0,1},{1,0},{2,3},{3,2},{4,5},{5,4},{6,7},{7,6},{8,9},{9,8},{10,11... | collective-permute-start | bytes 202760 | tf_op jit(solution)/shard_map/ppermute | solution.py:30
  23.8 8.6 %collective-permute-start.11 = (s16[264,128]{1,0:T(8,128)(2,1)S(1)}, s16[264,128]{1,0:T(8,128)(2,1)S(1)}, u32[]{:S(2)}, u32[]{:S(2)}) collective-permute-start(s16[264,128]{1,0:T(8,128)(2,1)S(1)} %get-tuple-element.61), channel_id=1, source_target_pairs={{0,2},{1,3},{2,0},{3,1},{4,6},{5,7},{6,4},{7,5},{8,10},{9,11},{10,... | collective-permute-start | bytes 202760 | tf_op jit(solution)/shard_map/ppermute | solution.py:30
  28.0 11.7 %collective-permute-start.7 = (s16[264,128]{1,0:T(8,128)(2,1)S(1)}, s16[264,128]{1,0:T(8,128)(2,1)S(1)}, u32[]{:S(2)}, u32[]{:S(2)}) collective-permute-start(s16[264,128]{1,0:T(8,128)(2,1)S(1)} %get-tuple-element.54), channel_id=1, source_target_pairs={{0,1},{1,0},{2,3},{3,2},{4,5},{5,4},{6,7},{7,6},{8,9},{9,8},{10,11... | collective-permute-start | bytes 202760 | tf_op jit(solution)/shard_map/ppermute | solution.py:30
  28.9 12.1 %collective-permute-start.8 = (s16[264,128]{1,0:T(8,128)(2,1)S(1)}, s16[264,128]{1,0:T(8,128)(2,1)S(1)}, u32[]{:S(2)}, u32[]{:S(2)}) collective-permute-start(s16[264,128]{1,0:T(8,128)(2,1)S(1)} %get-tuple-element.55), channel_id=1, source_target_pairs={{0,2},{1,3},{2,0},{3,1},{4,6},{5,7},{6,4},{7,5},{8,10},{9,11},{10,... | collective-permute-start | bytes 202760 | tf_op jit(solution)/shard_map/ppermute | solution.py:30
  32.4 8.6 %collective-permute-start.9 = (s16[264,128]{1,0:T(8,128)(2,1)S(1)}, s16[264,128]{1,0:T(8,128)(2,1)S(1)}, u32[]{:S(2)}, u32[]{:S(2)}) collective-permute-start(s16[264,128]{1,0:T(8,128)(2,1)S(1)} %get-tuple-element.56), channel_id=1, source_target_pairs={{0,3},{1,2},{2,1},{3,0},{4,7},{5,6},{6,5},{7,4},{8,11},{9,10},{10,... | collective-permute-start | bytes 202760 | tf_op jit(solution)/shard_map/ppermute | solution.py:30
  34.0 11.4 %collective-permute-start.14 = (bf16[256,128]{1,0:T(8,128)(2,1)S(1)}, bf16[256,128]{1,0:T(8,128)(2,1)S(1)}, u32[]{:S(2)}, u32[]{:S(2)}) collective-permute-start(bf16[256,128]{1,0:T(8,128)(2,1)S(1)} %shard_map.125.refs_1_), channel_id=1, source_target_pairs={{0,1},{1,0},{2,3},{3,2},{4,5},{5,4},{6,7},{7,6},{8,9},{9,8},{10,11... | collective-permute-start | bytes 196616 | tf_op jit(solution)/shard_map/ppermute | solution.py:30
  36.4 14.2 %collective-permute-start.16 = (bf16[256,128]{1,0:T(8,128)(2,1)S(1)}, bf16[256,128]{1,0:T(8,128)(2,1)S(1)}, u32[]{:S(2)}, u32[]{:S(2)}) collective-permute-start(bf16[256,128]{1,0:T(8,128)(2,1)S(1)} %shard_map.125.refs_1_), channel_id=1, source_target_pairs={{0,2},{1,3},{2,0},{3,1},{4,6},{5,7},{6,4},{7,5},{8,10},{9,11},{10,... | collective-permute-start | bytes 196616 | tf_op jit(solution)/shard_map/ppermute | solution.py:30
  39.7 10.9 %collective-permute-start.18 = (bf16[256,128]{1,0:T(8,128)(2,1)S(1)}, bf16[256,128]{1,0:T(8,128)(2,1)S(1)}, u32[]{:S(2)}, u32[]{:S(2)}) collective-permute-start(bf16[256,128]{1,0:T(8,128)(2,1)S(1)} %shard_map.125.refs_1_), channel_id=1, source_target_pairs={{0,3},{1,2},{2,1},{3,0},{4,7},{5,6},{6,5},{7,4},{8,11},{9,10},{10,... | collective-permute-start | bytes 196616 | tf_op jit(solution)/shard_map/ppermute | solution.py:30
  42.3 8.3 %collective-permute-start.13 = (bf16[256,128]{1,0:T(8,128)(2,1)S(1)}, bf16[256,128]{1,0:T(8,128)(2,1)S(1)}, u32[]{:S(2)}, u32[]{:S(2)}) collective-permute-start(bf16[256,128]{1,0:T(8,128)(2,1)S(1)} %shard_map.123.refs_0_), channel_id=1, source_target_pairs={{0,1},{1,0},{2,3},{3,2},{4,5},{5,4},{6,7},{7,6},{8,9},{9,8},{10,11... | collective-permute-start | bytes 196616 | tf_op jit(solution)/shard_map/ppermute | solution.py:30
  56.2 11.0 %collective-permute-start.21 = (s16[136,512]{1,0:T(8,128)(2,1)S(1)}, s16[136,512]{1,0:T(8,128)(2,1)S(1)}, u32[]{:S(2)}, u32[]{:S(2)}) collective-permute-start(s16[136,512]{1,0:T(8,128)(2,1)S(1)} %get-tuple-element.76), channel_id=1, source_target_pairs={{0,16},{4,20},{8,24},{12,28},{16,0},{20,4},{24,8},{28,12},{1,17},{... | collective-permute-start | bytes 417800 | tf_op jit(solution)/shard_map/ppermute | solution.py:30
  58.5 8.6 %collective-permute-start.22 = (s16[136,512]{1,0:T(8,128)(2,1)S(1)}, s16[136,512]{1,0:T(8,128)(2,1)S(1)}, u32[]{:S(2)}, u32[]{:S(2)}) collective-permute-start(s16[136,512]{1,0:T(8,128)(2,1)S(1)} %get-tuple-element.77), channel_id=1, source_target_pairs={{0,24},{4,28},{8,16},{12,20},{16,8},{20,12},{24,0},{28,4},{1,25},{... | collective-permute-start | bytes 417800 | tf_op jit(solution)/shard_map/ppermute | solution.py:30
  59.9 9.6 %collective-permute-start.24 = (s16[136,512]{1,0:T(8,128)(2,1)S(1)}, s16[136,512]{1,0:T(8,128)(2,1)S(1)}, u32[]{:S(2)}, u32[]{:S(2)}) collective-permute-start(s16[136,512]{1,0:T(8,128)(2,1)S(1)} %get-tuple-element.81), channel_id=1, source_target_pairs={{0,8},{4,12},{8,0},{12,4},{16,24},{20,28},{24,16},{28,20},{1,9},{5... | collective-permute-start | bytes 417800 | tf_op jit(solution)/shard_map/ppermute | solution.py:30
  60.3 10.9 %collective-permute-start.25 = (s16[136,512]{1,0:T(8,128)(2,1)S(1)}, s16[136,512]{1,0:T(8,128)(2,1)S(1)}, u32[]{:S(2)}, u32[]{:S(2)}) collective-permute-start(s16[136,512]{1,0:T(8,128)(2,1)S(1)} %get-tuple-element.82), channel_id=1, source_target_pairs={{0,16},{4,20},{8,24},{12,28},{16,0},{20,4},{24,8},{28,12},{1,17},{... | collective-permute-start | bytes 417800 | tf_op jit(solution)/shard_map/ppermute | solution.py:30
  62.7 8.5 %collective-permute-start.26 = (s16[136,512]{1,0:T(8,128)(2,1)S(1)}, s16[136,512]{1,0:T(8,128)(2,1)S(1)}, u32[]{:S(2)}, u32[]{:S(2)}) collective-permute-start(s16[136,512]{1,0:T(8,128)(2,1)S(1)} %get-tuple-element.83), channel_id=1, source_target_pairs={{0,24},{4,28},{8,16},{12,20},{16,8},{20,12},{24,0},{28,4},{1,25},{... | collective-permute-start | bytes 417800 | tf_op jit(solution)/shard_map/ppermute | solution.py:30
  68.4 11.5 %collective-permute-start.27 = (bf16[128,512]{1,0:T(8,128)(2,1)S(1)}, bf16[128,512]{1,0:T(8,128)(2,1)S(1)}, u32[]{:S(2)}, u32[]{:S(2)}) collective-permute-start(bf16[128,512]{1,0:T(8,128)(2,1)S(1)} %shard_map.130.refs_0_), channel_id=1, source_target_pairs={{0,1},{1,0},{2,3},{3,2},{4,5},{5,4},{6,7},{7,6},{8,9},{9,8},{10,11... | collective-permute-start | bytes 393224 | tf_op jit(solution)/shard_map/ppermute | solution.py:30
  69.4 18.1 %collective-permute-start.31 = (bf16[128,512]{1,0:T(8,128)(2,1)S(1)}, bf16[128,512]{1,0:T(8,128)(2,1)S(1)}, u32[]{:S(2)}, u32[]{:S(2)}) collective-permute-start(bf16[128,512]{1,0:T(8,128)(2,1)S(1)} %shard_map.130.refs_0_), channel_id=1, source_target_pairs={{1,2},{2,1},{5,6},{6,5},{9,10},{10,9},{13,14},{14,13},{17,18},{18,... | collective-permute-start | bytes 393224 | tf_op jit(solution)/shard_map/ppermute | solution.py:517
  71.3 16.2 %collective-permute-start.33 = (bf16[128,512]{1,0:T(8,128)(2,1)S(1)}, bf16[128,512]{1,0:T(8,128)(2,1)S(1)}, u32[]{:S(2)}, u32[]{:S(2)}) collective-permute-start(bf16[128,512]{1,0:T(8,128)(2,1)S(1)} %shard_map.133.refs_1_), channel_id=1, source_target_pairs={{0,1},{1,0},{2,3},{3,2},{4,5},{5,4},{6,7},{7,6},{8,9},{9,8},{10,11... | collective-permute-start | bytes 393224 | tf_op jit(solution)/shard_map/ppermute | solution.py:30
  75.4 12.2 %collective-permute-start.32 = (bf16[128,512]{1,0:T(8,128)(2,1)S(1)}, bf16[128,512]{1,0:T(8,128)(2,1)S(1)}, u32[]{:S(2)}, u32[]{:S(2)}) collective-permute-start(bf16[128,512]{1,0:T(8,128)(2,1)S(1)} %collective-permute-done.28.refs_3_), channel_id=1, source_target_pairs={{1,0},{2,3},{5,4},{6,7},{9,8},{10,11},{13,12},{14,15},{17,16},{18,... | collective-permute-start | bytes 393224 | tf_op jit(solution)/shard_map/ppermute | solution.py:518
  76.8 14.2 %collective-permute-start.29 = (bf16[128,512]{1,0:T(8,128)(2,1)S(1)}, bf16[128,512]{1,0:T(8,128)(2,1)S(1)}, u32[]{:S(2)}, u32[]{:S(2)}) collective-permute-start(bf16[128,512]{1,0:T(8,128)(2,1)S(1)} %shard_map.133.refs_1_), channel_id=1, source_target_pairs={{0,2},{1,3},{2,0},{3,1},{4,6},{5,7},{6,4},{7,5},{8,10},{9,11},{10,... | collective-permute-start | bytes 393224 | tf_op jit(solution)/shard_map/ppermute | solution.py:30
  79.9 11.1 %collective-permute-start.30 = (bf16[128,512]{1,0:T(8,128)(2,1)S(1)}, bf16[128,512]{1,0:T(8,128)(2,1)S(1)}, u32[]{:S(2)}, u32[]{:S(2)}) collective-permute-start(bf16[128,512]{1,0:T(8,128)(2,1)S(1)} %shard_map.133.refs_1_), channel_id=1, source_target_pairs={{0,3},{1,2},{2,1},{3,0},{4,7},{5,6},{6,5},{7,4},{8,11},{9,10},{10,... | collective-permute-start | bytes 393224 | tf_op jit(solution)/shard_map/ppermute | solution.py:30
  (13 other events, 61.8 us)

commit v4 on v3

--- a/solution.py
+++ b/solution.py
@@ -14,7 +14,7 @@
 HALVES = 2
 GROUP_ROWS = 8
 AT_ONCE = 24
-LARGE = 50
+LARGE = 47
 MEDIUM = 46
 LEVELS = 32767.0
 VMEM = pl.BlockSpec(memory_space=pltpu.VMEM)
@@ -169,36 +169,45 @@
         )
 
 
-def grads_kernel(wide, narrow, slots, half, blocks_ref, where_ref, tiles, *refs):
-    probs = refs[: narrow * GROUPS]
-    target_rows, factor, mine, other, total = refs[narrow * GROUPS :]
-    me_w, me_n = where_ref[0], where_ref[1]
+def add_slots(narrow, slots, group, blocks_ref, where_ref, tiles, probs, total, lanes):
     per = slots // narrow
     share = per // GROUPS
-    width = mine.shape[1]
+    for k in range(narrow):
+        for i in range(share):
+            slot = (where_ref[1] ^ k) * per + group * share + i
+            block = blocks_ref[slot] ^ where_ref[0]
+            rows = pl.ds(pl.multiple_of(block * TILE, TILE), TILE)
+            total[rows, :] += jnp.dot(
+                probs[k][i * TILE : (i + 1) * TILE, :],
+                tiles[pl.ds(pl.multiple_of(slot * TILE, TILE), TILE), lanes],
+                preferred_element_type=jnp.float32,
+            )
+
+
+def base_kernel(narrow, slots, blocks_ref, where_ref, tiles, *refs):
+    probs, (target_rows, factor, total) = refs[:-3], refs[-3:]
     for block in range(factor.shape[0] // TILE):
         rows = slice(block * TILE, (block + 1) * TILE)
+        start = pl.multiple_of((block ^ where_ref[0]) * TILE, TILE)
         weight = -factor[rows, :]
-        for lane in range(0, width, TILE):
-            at = half * width + lane
-            total[block ^ me_w, :, lane : lane + TILE] = weight * target_rows[
-                rows, at : at + TILE
-            ].astype(jnp.float32)
-    for k in range(narrow):
-        for group in range(GROUPS):
-            for i in range(share):
-                slot = (me_n ^ k) * per + group * share + i
-                total[blocks_ref[slot] ^ me_w] += jnp.dot(
-                    probs[k * GROUPS + group][i * TILE : (i + 1) * TILE, :],
-                    tiles[
-                        pl.ds(pl.multiple_of(slot * TILE, TILE), TILE),
-                        half * width : (half + 1) * width,
-                    ],
-                    preferred_element_type=jnp.float32,
-                )
-    for chip in range(wide // 2):
-        mine[chip * TILE : (chip + 1) * TILE, :] = total[2 * chip]
-        other[chip * TILE : (chip + 1) * TILE, :] = total[2 * chip + 1]
+        for lane in range(0, total.shape[1], TILE):
+            lanes = slice(lane, lane + TILE)
+            total[pl.ds(start, TILE), lanes] = weight * target_rows[rows, lanes].astype(jnp.float32)
+    for group in range(GROUPS - 1):
+        some = probs[group * narrow : (group + 1) * narrow]
+        add_slots(narrow, slots, group, blocks_ref, where_ref, tiles, some, total, slice(None))
+
+
+def grads_kernel(narrow, slots, half, blocks_ref, where_ref, tiles, *refs):
+    probs, (base, mine, other, total) = refs[:-4], refs[-4:]
+    width = mine.shape[1]
+    lanes = slice(half * width, (half + 1) * width)
+    total[...] = base[:, lanes]
+    add_slots(narrow, slots, GROUPS - 1, blocks_ref, where_ref, tiles, probs, total, lanes)
+    for chip in range(mine.shape[0] // TILE):
+        rows = slice(chip * TILE, (chip + 1) * TILE)
+        mine[rows, :] = total[2 * chip * TILE : (2 * chip + 1) * TILE, :]
+        other[rows, :] = total[(2 * chip + 1) * TILE : (2 * chip + 2) * TILE, :]
 
 
 def pack_kernel(chips, mine, other, own, *sends):
@@ -244,10 +253,10 @@
         copy.wait()
 
 
-def unit_kernel(keys, splits, kind, chunk, skip, where_ref, *refs):
-    count, inputs = len(keys), sum(splits)
+def unit_kernel(keys, splits, kind, chunk, ready, where_ref, *refs):
+    inputs = sum(splits)
     arrived, down, refs = list(refs[:inputs]), refs[inputs], list(refs[inputs + 1 :])
-    units = down.shape[-2]
+    units = down.shape[0]
     width = arrived[0].shape[1]
     pieces = []
     for split in splits:
@@ -255,31 +264,31 @@
         for _ in range(split - 1):
             piece = piece + arrived.pop(0)[...]
         pieces.append(piece)
+    held = refs.pop(0) if ready else None
     summed = None if kind == "first" else refs.pop(0)
     if kind == "last":
         gate, up, gate_out, up_out = refs[:4]
     else:
         sum_out = refs[0]
+    down_v, sem = refs[-2:]
+    steps = [pl.ds(at, chunk) for at in range(0, units, chunk)]
+    copies = [
+        down_copies(keys[ready:], where_ref, down, down_v.at[step], sem.at[step], rows)
+        for step, rows in enumerate(steps)
+    ]
+    for copy in sum(copies, []):
+        copy.start()
     if kind == "first":
         for at in range(HALVES):
             refs[1][:, at * width : (at + 1) * width] = pieces[at]
-    steps = [pl.ds(at, chunk) for at in range(0, units, chunk)]
-    if skip is None:
-        down_v, sem = refs[-2:]
-        copies = [
-            down_copies(keys, where_ref, down, down_v.at[step], sem.at[step], rows)
-            for step, rows in enumerate(steps)
-        ]
-        for copy in sum(copies, []):
-            copy.start()
     for step, rows in enumerate(steps):
         total = None if summed is None else summed[:, rows]
-        for at in range(count):
-            if skip is None:
-                copies[step][at].wait()
+        for at, piece in enumerate(pieces):
+            if at >= ready:
+                copies[step][at - ready].wait()
             part = lax.dot_general(
-                pieces[at],
-                down_v[step, at] if skip is None else down[skip + at, rows, :],
+                piece,
+                held[at, rows, :] if at < ready else down_v[step, at - ready],
                 (((1,), (1,)), ((), ())),
                 preferred_element_type=jnp.float32,
             )
@@ -429,50 +438,56 @@
         ],
         MEDIUM,
     )
-    all_probs = [probs[group][k] for k in range(narrow) for group in range(GROUPS)]
+    early_probs = sum(probs[:-1], [])
+    (base,) = call(
+        functools.partial(base_kernel, narrow, slots),
+        [shape_of((blocks * TILE, features), f32)],
+        [SMEM] * 2 + [VMEM] * (len(early_probs) + 3),
+        (slot_blocks, where, tiles, *early_probs, target_rows, factor),
+        slots * TILE * TILE * features,
+        blocks * TILE * features * 4,
+    )
+    probs[-1][-1], base = lax.optimization_barrier((probs[-1][-1], base))
 
     halves = []
     for half in range(HALVES):
         mine, other = call(
-            functools.partial(grads_kernel, wide, narrow, slots, half),
+            functools.partial(grads_kernel, narrow, slots, half),
             [shape_of((chips * TILE, width), f32)] * 2,
-            [SMEM] * 2 + [VMEM] * (narrow * GROUPS + 3),
-            (slot_blocks, where, tiles, *all_probs, target_rows, factor),
-            2 * slots * TILE * TILE * width,
-            slots * TILE * width * 4,
-            [pltpu.VMEM((wide, TILE, width), f32)],
+            [SMEM] * 2 + [VMEM] * (narrow + 2),
+            (slot_blocks, where, tiles, *probs[-1], base),
+            slots * TILE * TILE * width,
+            blocks * TILE * width * 4,
+            [pltpu.VMEM((blocks * TILE, width), f32)],
         )
         halves.append((mine, swap(other, "wide", 1)))
     units = gate_pre.shape[1]
     held_keys = [(k, HALVES - 1) for k in range(2, narrow)]
     chunk = units // 2 if units // 2 % TILE == 0 else units
 
-    def unit(keys, kind, skip, *extra):
+    def unit(keys, kind, ready, *extra):
         last = kind == "last"
         inputs = [part for key in keys for part in pieces[key]]
-        count = len(keys)
+        count, read = len(keys), len(keys) - ready
+        if ready:
+            extra = (held, *extra)
         return call(
             functools.partial(
-                unit_kernel, keys, [len(pieces[key]) for key in keys], kind, chunk, skip
+                unit_kernel, keys, [len(pieces[key]) for key in keys], kind, chunk, ready
             ),
             [shape_of((TILE, units), bf16)] * 2
             if last
             else [shape_of((TILE, units), f32)]
             + [shape_of((TILE, features), bf16)] * (kind == "first"),
-            [SMEM]
-            + [VMEM] * len(inputs)
-            + [HBM if skip is None else VMEM]
-            + [VMEM] * len(extra),
-            (where, *inputs, down_weight if skip is None else held, *extra),
+            [SMEM] + [VMEM] * len(inputs) + [HBM] + [VMEM] * len(extra),
+            (where, *inputs, down_weight, *extra),
             2 * count * TILE * units * width,
             count * units * width * 2,
             (
-                pltpu.VMEM((units // chunk, count, chunk, width), bf16),
-                pltpu.SemaphoreType.DMA((units // chunk, count)),
-            )
-            if skip is None
-            else (),
-            LARGE if skip is None else 16,
+                pltpu.VMEM((units // chunk, read, chunk, width), bf16),
+                pltpu.SemaphoreType.DMA((units // chunk, read)),
+            ),
+            LARGE,
         )
 
     pieces = {}
@@ -518,9 +533,11 @@
         ends = lax.ppermute(pieces[2, 0][0], "narrow", [(1, 0), (2, 3)])
         pieces[3, 0] = (near_ends, ends)
     early = [(0, half) for half in range(HALVES)] + [(k, 0) for k in range(1, narrow - 1)]
-    summed, head_grad = unit(early, "first", None)
-    (summed,) = unit([(narrow - 1, 0), (1, 1)], "more", None, summed)
-    gate_grad, up_grad = unit(held_keys, "last", 0, summed, gate_pre, up_pre)
+    summed, head_grad = unit(early, "first", 0)
+    (summed,) = unit([(1, 1)], "more", 0, summed)
+    gate_grad, up_grad = unit(
+        [*held_keys, (narrow - 1, 0)], "last", len(held_keys), summed, gate_pre, up_pre
+    )
     return head_grad, gate_grad, up_grad
 
 

time: 94.4 us -> 92.2 us (0.977)
  waiting for transfers between devices: 6.85 us -> 3.94 us
  Pallas kernels: 32.3 us -> 34 us
  starting transfers between devices: 46.1 us -> 44.5 us
    ppermute x32, waiting for transfers between devices: 6.85 us -> 3.93 us  [swap(): return lax.ppermute(x, axis, [(i, i ^ mask) for i in range(size)])]
    pallas_call x16 -> x17, Pallas kernels: 32.3 us -> 34 us  [call(): pl.pallas_call(kernel, out_shape=outs, in_specs=ins, out_specs=[SMEM] * s...]
    ppermute x32, starting transfers between devices: 44 us -> 42.4 us  [swap(): return lax.ppermute(x, axis, [(i, i ^ mask) for i in range(size)])]
  transfers between devices with their start and end apart: 34 -> 34, of which waited for: 9 -> 7; matrix products, arithmetic and copies ran while one was open for 8% -> 8% of each run, Pallas kernels for 28% -> 29%
where the time goes in v4:
time: 92.2 us; the launch traced here: 91.2 us
  starting transfers between devices  44.5 us (48%)
  Pallas kernels  34 us (37%)
  other arithmetic  4.16 us (5%)
  waiting for transfers between devices  3.94 us (4%)
  local copies, waits for them, and re-layouts  3.46 us (4%)
  between operations  1.15 us (1%)
    ppermute x32, starting transfers between devices, swap(): return lax.ppermute(x, axis, [(i, i ^ mask) for i in range(size)])  42.4 us
    pallas_call x17, Pallas kernels, call(): pl.pallas_call(kernel, out_shape=outs, in_specs=ins, out_specs=[SMEM] * s...  34 us
    ppermute x32, waiting for transfers between devices, swap(): return lax.ppermute(x, axis, [(i, i ^ mask) for i in range(size)])  3.93 us
    broadcast_in_dim x3, local copies, waits for them, and re-layouts, over_lanes(): return jnp.broadcast_to(x[:, None], (blocks * TILE, TILE))  1.95 us
  transfers between devices with their start and end apart: 34, of which 7 were waited for; matrix products, arithmetic and copies ran while one was open for 8% of the time, Pallas kernels for 29%

profile of v4, /device:TPU:0, one launch (start us, length us, event | category | flops | bytes accessed | tf_op | source)
XLA Modules:
  0.0 91.2 jit_solution(10416371954018451171)
XLA Ops:
  0.6 3.0 %collective-permute-start = (bf16[128,1024]{1,0:T(8,128)(2,1)}, bf16[128,1024]{1,0:T(8,128)(2,1)S(1)}, u32[]{:S(2)}, u32[]{:S(2)}) collective-permute-start(bf16[128,1024]{1,0:T(8,128)(2,1)} %refs_0_.3), channel_id=1, source_target_pairs={{0,8},{4,12},{8,0},{12,4},{16,24},{20,28},{24,16},{28,20},{1,9},{5... | collective-permute-start | bytes 786440 | tf_op jit(solution)/shard_map/ppermute | solution.py:30
  3.7 1.5 %collective-permute-start.3 = (bf16[128,1024]{1,0:T(8,128)(2,1)}, bf16[128,1024]{1,0:T(8,128)(2,1)S(1)}, u32[]{:S(2)}, u32[]{:S(2)}) collective-permute-start(bf16[128,1024]{1,0:T(8,128)(2,1)} %refs_0_.3), channel_id=1, source_target_pairs={{0,16},{4,20},{8,24},{12,28},{16,0},{20,4},{24,8},{28,12},{1,17},{... | collective-permute-start | bytes 786440 | tf_op jit(solution)/shard_map/ppermute | solution.py:30
  12.9 4.3 %shard_map.121 = (s32[16]{0:T(128)S(1)}, s32[1]{0:T(128)}, bf16[2048,1024]{1,0:T(8,128)(2,1)S(1)}) custom-call(s32[8,1,4]{2,1,0:T(1,128)S(1)} %copy.15.tiles_ref, s32[8,1]{1,0:T(8,128)S(1)} %copy.16.counts_ref, bf16[4096,1024]{1,0:T(8,128)(2,1)} %head.3), custom_call_target="tpu_custom_call" | custom-call | bytes 4194304 | tf_op jit(solution)/shard_map/pallas_call | solution.py:311
  20.1 1.6 %shard_map.124 = (f32[256,128]{1,0:T(8,128)S(1)}, s16[264,128]{1,0:T(8,128)(2,1)S(1)}, s16[264,128]{1,0:T(8,128)(2,1)S(1)}, s16[264,128]{1,0:T(8,128)(2,1)S(1)}) custom-call(s32[16]{0:T(128)S(1)} %get-tuple-element.50.blocks_ref, s32[2]{0:T(128)S(1)} %pad_add_fusion.where_ref, bf16[2048,1024]{1,0:T(8,128)(2,1)S(1)} %get-tuple-element.52.tiles, ...), custom_call_target="tpu_custom_call" | custom-call | flops 268435456 | bytes 2097152 | tf_op jit(solution)/shard_map/pallas_call | solution.py:311
  21.7 2.1 %collective-permute-start.13 = (s16[264,128]{1,0:T(8,128)(2,1)S(1)}, s16[264,128]{1,0:T(8,128)(2,1)S(1)}, u32[]{:S(2)}, u32[]{:S(2)}) collective-permute-start(s16[264,128]{1,0:T(8,128)(2,1)S(1)} %get-tuple-element.64), channel_id=1, source_target_pairs={{0,1},{1,0},{2,3},{3,2},{4,5},{5,4},{6,7},{7,6},{8,9},{9,8},{10,11... | collective-permute-start | bytes 202760 | tf_op jit(solution)/shard_map/ppermute | solution.py:30
  23.8 2.6 %collective-permute-start.14 = (s16[264,128]{1,0:T(8,128)(2,1)S(1)}, s16[264,128]{1,0:T(8,128)(2,1)S(1)}, u32[]{:S(2)}, u32[]{:S(2)}) collective-permute-start(s16[264,128]{1,0:T(8,128)(2,1)S(1)} %get-tuple-element.65), channel_id=1, source_target_pairs={{0,2},{1,3},{2,0},{3,1},{4,6},{5,7},{6,4},{7,5},{8,10},{9,11},{10,... | collective-permute-start | bytes 202760 | tf_op jit(solution)/shard_map/ppermute | solution.py:30
  26.4 1.6 %shard_map.122 = (f32[256,128]{1,0:T(8,128)S(1)}, s16[264,128]{1,0:T(8,128)(2,1)S(1)}, s16[264,128]{1,0:T(8,128)(2,1)S(1)}, s16[264,128]{1,0:T(8,128)(2,1)S(1)}) custom-call(s32[16]{0:T(128)S(1)} %get-tuple-element.50.blocks_ref, s32[2]{0:T(128)S(1)} %pad_add_fusion.where_ref, bf16[2048,1024]{1,0:T(8,128)(2,1)S(1)} %get-tuple-element.52.tiles, ...), custom_call_target="tpu_custom_call" | custom-call | flops 268435456 | bytes 2097152 | tf_op jit(solution)/shard_map/pallas_call | solution.py:311
  28.9 3.5 %collective-permute-start.8 = (s16[264,128]{1,0:T(8,128)(2,1)S(1)}, s16[264,128]{1,0:T(8,128)(2,1)S(1)}, u32[]{:S(2)}, u32[]{:S(2)}) collective-permute-start(s16[264,128]{1,0:T(8,128)(2,1)S(1)} %get-tuple-element.57), channel_id=1, source_target_pairs={{0,2},{1,3},{2,0},{3,1},{4,6},{5,7},{6,4},{7,5},{8,10},{9,11},{10,... | collective-permute-start | bytes 202760 | tf_op jit(solution)/shard_map/ppermute | solution.py:30
  34.0 2.4 %collective-permute-start.16 = (bf16[256,128]{1,0:T(8,128)(2,1)S(1)}, bf16[256,128]{1,0:T(8,128)(2,1)S(1)}, u32[]{:S(2)}, u32[]{:S(2)}) collective-permute-start(bf16[256,128]{1,0:T(8,128)(2,1)S(1)} %shard_map.125.refs_0_), channel_id=1, source_target_pairs={{0,1},{1,0},{2,3},{3,2},{4,5},{5,4},{6,7},{7,6},{8,9},{9,8},{10,11... | collective-permute-start | bytes 196616 | tf_op jit(solution)/shard_map/ppermute | solution.py:30
  36.4 3.3 %collective-permute-start.17 = (bf16[256,128]{1,0:T(8,128)(2,1)S(1)}, bf16[256,128]{1,0:T(8,128)(2,1)S(1)}, u32[]{:S(2)}, u32[]{:S(2)}) collective-permute-start(bf16[256,128]{1,0:T(8,128)(2,1)S(1)} %shard_map.125.refs_0_), channel_id=1, source_target_pairs={{0,2},{1,3},{2,0},{3,1},{4,6},{5,7},{6,4},{7,5},{8,10},{9,11},{10,... | collective-permute-start | bytes 196616 | tf_op jit(solution)/shard_map/ppermute | solution.py:30
  42.4 2.5 %collective-permute-start.12 = (bf16[256,128]{1,0:T(8,128)(2,1)S(1)}, bf16[256,128]{1,0:T(8,128)(2,1)S(1)}, u32[]{:S(2)}, u32[]{:S(2)}) collective-permute-start(bf16[256,128]{1,0:T(8,128)(2,1)S(1)} %shard_map.123.refs_0_), channel_id=1, source_target_pairs={{0,3},{1,2},{2,1},{3,0},{4,7},{5,6},{6,5},{7,4},{8,11},{9,10},{10,... | collective-permute-start | bytes 196616 | tf_op jit(solution)/shard_map/ppermute | solution.py:30
  45.0 1.8 %collective-permute-start.11 = (bf16[256,128]{1,0:T(8,128)(2,1)S(1)}, bf16[256,128]{1,0:T(8,128)(2,1)S(1)}, u32[]{:S(2)}, u32[]{:S(2)}) collective-permute-start(bf16[256,128]{1,0:T(8,128)(2,1)S(1)} %shard_map.123.refs_0_), channel_id=1, source_target_pairs={{0,2},{1,3},{2,0},{3,1},{4,6},{5,7},{6,4},{7,5},{8,10},{9,11},{10,... | collective-permute-start | bytes 196616 | tf_op jit(solution)/shard_map/ppermute | solution.py:30
  46.8 3.8 %shard_map.126.refs_4_ = bf16[1024,1024]{1,0:T(8,128)(2,1)S(1)} custom-call(s32[1024]{0:T(1024)S(1)} %fusion.3.list_ref, s32[8]{0:T(128)S(1)} %get-tuple-element.68.count_ref, s32[8,128]{1,0:T(8,128)S(1)} %fusion.5.code, bf16[4096,1024]{1,0:T(8,128)(2,1)} %head.3), custom_call_target="tpu_custom_call" | custom-call | flops 402653184 | bytes 3145728 | tf_op jit(solution)/shard_map/pallas_call | solution.py:311
  50.6 1.8 %shard_map.127.refs_4_ = f32[1024,1024]{1,0:T(8,128)S(1)} custom-call(s32[16]{0:T(128)S(1)} %get-tuple-element.50.blocks_ref, s32[2]{0:T(128)S(1)} %pad_add_fusion.where_ref, bf16[2048,1024]{1,0:T(8,128)(2,1)S(1)} %get-tuple-element.52.tiles, bf16[256,128]{1,0:T(8,128)(2,1)S(1)} %shard_map.125.refs_0_, bf16[256,128]{1,0:T(8,128)(2,1)S(1)} %collective-permute-done.16.refs_1_, ...), custom_call_target="tpu_custom_call" | custom-call | flops 268435456 | bytes 4194304 | tf_op jit(solution)/shard_map/pallas_call | solution.py:311
  56.7 2.2 %collective-permute-start.21 = (s16[136,512]{1,0:T(8,128)(2,1)S(1)}, s16[136,512]{1,0:T(8,128)(2,1)S(1)}, u32[]{:S(2)}, u32[]{:S(2)}) collective-permute-start(s16[136,512]{1,0:T(8,128)(2,1)S(1)} %get-tuple-element.80), channel_id=1, source_target_pairs={{0,16},{4,20},{8,24},{12,28},{16,0},{20,4},{24,8},{28,12},{1,17},{... | collective-permute-start | bytes 417800 | tf_op jit(solution)/shard_map/ppermute | solution.py:30
  60.6 2.0 %collective-permute-start.25 = (s16[136,512]{1,0:T(8,128)(2,1)S(1)}, s16[136,512]{1,0:T(8,128)(2,1)S(1)}, u32[]{:S(2)}, u32[]{:S(2)}) collective-permute-start(s16[136,512]{1,0:T(8,128)(2,1)S(1)} %get-tuple-element.86), channel_id=1, source_target_pairs={{0,16},{4,20},{8,24},{12,28},{16,0},{20,4},{24,8},{28,12},{1,17},{... | collective-permute-start | bytes 417800 | tf_op jit(solution)/shard_map/ppermute | solution.py:30
  63.2 1.7 %collective-permute-start.26 = (s16[136,512]{1,0:T(8,128)(2,1)S(1)}, s16[136,512]{1,0:T(8,128)(2,1)S(1)}, u32[]{:S(2)}, u32[]{:S(2)}) collective-permute-start(s16[136,512]{1,0:T(8,128)(2,1)S(1)} %get-tuple-element.87), channel_id=1, source_target_pairs={{0,24},{4,28},{8,16},{12,20},{16,8},{20,12},{24,0},{28,4},{1,25},{... | collective-permute-start | bytes 417800 | tf_op jit(solution)/shard_map/ppermute | solution.py:30
  64.9 2.6 %shard_map.130.refs_5_ = bf16[2,1792,512]{2,1,0:T(8,128)(2,1)S(1)} custom-call(s32[2]{0:T(128)S(1)} %pad_add_fusion.where_ref, bf16[1792,4096]{1,0:T(8,128)(2,1)} %refs_4_.3), custom_call_target="tpu_custom_call" | custom-call | bytes 3670016 | tf_op jit(solution)/shard_map/pallas_call | solution.py:311
  67.8 2.9 %collective-permute-start.28 = (bf16[128,512]{1,0:T(8,128)(2,1)S(1)}, bf16[128,512]{1,0:T(8,128)(2,1)S(1)}, u32[]{:S(2)}, u32[]{:S(2)}) collective-permute-start(bf16[128,512]{1,0:T(8,128)(2,1)S(1)} %shard_map.131.refs_0_), channel_id=1, source_target_pairs={{0,2},{1,3},{2,0},{3,1},{4,6},{5,7},{6,4},{7,5},{8,10},{9,11},{10,... | collective-permute-start | bytes 393224 | tf_op jit(solution)/shard_map/ppermute | solution.py:30
  71.8 2.9 %collective-permute-start.29 = (bf16[128,512]{1,0:T(8,128)(2,1)S(1)}, bf16[128,512]{1,0:T(8,128)(2,1)S(1)}, u32[]{:S(2)}, u32[]{:S(2)}) collective-permute-start(bf16[128,512]{1,0:T(8,128)(2,1)S(1)} %shard_map.134.refs_1_), channel_id=1, source_target_pairs={{0,2},{1,3},{2,0},{3,1},{4,6},{5,7},{6,4},{7,5},{8,10},{9,11},{10,... | collective-permute-start | bytes 393224 | tf_op jit(solution)/shard_map/ppermute | solution.py:30
  76.8 1.5 %collective-permute-start.32 = (bf16[128,512]{1,0:T(8,128)(2,1)S(1)}, bf16[128,512]{1,0:T(8,128)(2,1)S(1)}, u32[]{:S(2)}, u32[]{:S(2)}) collective-permute-start(bf16[128,512]{1,0:T(8,128)(2,1)S(1)} %collective-permute-done.28.refs_3_), channel_id=1, source_target_pairs={{1,0},{2,3},{5,4},{6,7},{9,8},{10,11},{13,12},{14,15},{17,16},{18,... | collective-permute-start | bytes 393224 | tf_op jit(solution)/shard_map/ppermute | solution.py:533
  78.3 5.6 %shard_map.135 = (f32[128,1792]{1,0:T(8,128)S(1)}, bf16[128,1024]{1,0:T(8,128)(2,1)}) custom-call(s32[2]{0:T(128)S(1)} %pad_add_fusion.where_ref, bf16[128,512]{1,0:T(8,128)(2,1)S(1)} %shard_map.131.refs_0_, bf16[128,512]{1,0:T(8,128)(2,1)S(1)} %shard_map.134.refs_1_, bf16[128,512]{1,0:T(8,128)(2,1)S(1)} %collective-permute-done.27.refs_2_, ...), custom_call_target="tpu_custom_call" | custom-call | flops 939524096 | bytes 7340032 | tf_op jit(solution)/shard_map/pallas_call | solution.py:311
  84.0 2.7 %shard_map.136.refs_6_ = f32[128,1792]{1,0:T(8,128)S(1)} custom-call(s32[2]{0:T(128)S(1)} %pad_add_fusion.where_ref, bf16[128,512]{1,0:T(8,128)(2,1)S(1)} %collective-permute-done.33.refs_0_, bf16[1792,4096]{1,0:T(8,128)(2,1)} %refs_4_.3, f32[128,1792]{1,0:T(8,128)S(1)} %get-tuple-element.90.refs_2_), custom_call_target="tpu_custom_call" | custom-call | flops 234881024 | bytes 1835008 | tf_op jit(solution)/shard_map/pallas_call | solution.py:311
  86.7 4.3 %shard_map.137 = (bf16[128,1792]{1,0:T(8,128)(2,1)}, bf16[128,1792]{1,0:T(8,128)(2,1)}) custom-call(s32[2]{0:T(128)S(1)} %pad_add_fusion.where_ref, bf16[128,512]{1,0:T(8,128)(2,1)S(1)} %collective-permute-done.29.refs_0_, bf16[128,512]{1,0:T(8,128)(2,1)S(1)} %collective-permute-done.30.refs_1_, bf16[128,512]{1,0:T(8,128)(2,1)S(1)} %collective-permute-done.31.refs_2_, ...), custom_call_target="tpu_custom_call" | custom-call | flops 704643072 | bytes 5505024 | tf_op jit(solution)/shard_map/pallas_call | solution.py:311
  (82 shorter events, 25.8 us)
Async XLA Ops:
  0.6 16.6 %collective-permute-start = (bf16[128,1024]{1,0:T(8,128)(2,1)}, bf16[128,1024]{1,0:T(8,128)(2,1)S(1)}, u32[]{:S(2)}, u32[]{:S(2)}) collective-permute-start(bf16[128,1024]{1,0:T(8,128)(2,1)} %refs_0_.3), channel_id=1, source_target_pairs={{0,8},{4,12},{8,0},{12,4},{16,24},{20,28},{24,16},{28,20},{1,9},{5... | collective-permute-start | bytes 786440 | tf_op jit(solution)/shard_map/ppermute | solution.py:30
  3.7 14.6 %collective-permute-start.3 = (bf16[128,1024]{1,0:T(8,128)(2,1)}, bf16[128,1024]{1,0:T(8,128)(2,1)S(1)}, u32[]{:S(2)}, u32[]{:S(2)}) collective-permute-start(bf16[128,1024]{1,0:T(8,128)(2,1)} %refs_0_.3), channel_id=1, source_target_pairs={{0,16},{4,20},{8,24},{12,28},{16,0},{20,4},{24,8},{28,12},{1,17},{... | collective-permute-start | bytes 786440 | tf_op jit(solution)/shard_map/ppermute | solution.py:30
  5.2 13.1 %collective-permute-start.5 = (bf16[128,1024]{1,0:T(8,128)(2,1)}, bf16[128,1024]{1,0:T(8,128)(2,1)S(1)}, u32[]{:S(2)}, u32[]{:S(2)}) collective-permute-start(bf16[128,1024]{1,0:T(8,128)(2,1)} %refs_0_.3), channel_id=1, source_target_pairs={{0,24},{4,28},{8,16},{12,20},{16,8},{20,12},{24,0},{28,4},{1,25},{... | collective-permute-start | bytes 786440 | tf_op jit(solution)/shard_map/ppermute | solution.py:30
  5.2 13.5 %collective-permute-start.1 = (bf16[128,1024]{1,0:T(8,128)(2,1)}, bf16[128,1024]{1,0:T(8,128)(2,1)S(1)}, u32[]{:S(2)}, u32[]{:S(2)}) collective-permute-start(bf16[128,1024]{1,0:T(8,128)(2,1)} %refs_0_.3), channel_id=1, source_target_pairs={{0,4},{4,0},{8,12},{12,8},{16,20},{20,16},{24,28},{28,24},{1,5},{5... | collective-permute-start | bytes 786440 | tf_op jit(solution)/shard_map/ppermute | solution.py:30
  21.7 10.7 %collective-permute-start.13 = (s16[264,128]{1,0:T(8,128)(2,1)S(1)}, s16[264,128]{1,0:T(8,128)(2,1)S(1)}, u32[]{:S(2)}, u32[]{:S(2)}) collective-permute-start(s16[264,128]{1,0:T(8,128)(2,1)S(1)} %get-tuple-element.64), channel_id=1, source_target_pairs={{0,1},{1,0},{2,3},{3,2},{4,5},{5,4},{6,7},{7,6},{8,9},{9,8},{10,11... | collective-permute-start | bytes 202760 | tf_op jit(solution)/shard_map/ppermute | solution.py:30
  23.8 8.6 %collective-permute-start.14 = (s16[264,128]{1,0:T(8,128)(2,1)S(1)}, s16[264,128]{1,0:T(8,128)(2,1)S(1)}, u32[]{:S(2)}, u32[]{:S(2)}) collective-permute-start(s16[264,128]{1,0:T(8,128)(2,1)S(1)} %get-tuple-element.65), channel_id=1, source_target_pairs={{0,2},{1,3},{2,0},{3,1},{4,6},{5,7},{6,4},{7,5},{8,10},{9,11},{10,... | collective-permute-start | bytes 202760 | tf_op jit(solution)/shard_map/ppermute | solution.py:30
  28.0 11.7 %collective-permute-start.7 = (s16[264,128]{1,0:T(8,128)(2,1)S(1)}, s16[264,128]{1,0:T(8,128)(2,1)S(1)}, u32[]{:S(2)}, u32[]{:S(2)}) collective-permute-start(s16[264,128]{1,0:T(8,128)(2,1)S(1)} %get-tuple-element.56), channel_id=1, source_target_pairs={{0,1},{1,0},{2,3},{3,2},{4,5},{5,4},{6,7},{7,6},{8,9},{9,8},{10,11... | collective-permute-start | bytes 202760 | tf_op jit(solution)/shard_map/ppermute | solution.py:30
  28.9 12.1 %collective-permute-start.8 = (s16[264,128]{1,0:T(8,128)(2,1)S(1)}, s16[264,128]{1,0:T(8,128)(2,1)S(1)}, u32[]{:S(2)}, u32[]{:S(2)}) collective-permute-start(s16[264,128]{1,0:T(8,128)(2,1)S(1)} %get-tuple-element.57), channel_id=1, source_target_pairs={{0,2},{1,3},{2,0},{3,1},{4,6},{5,7},{6,4},{7,5},{8,10},{9,11},{10,... | collective-permute-start | bytes 202760 | tf_op jit(solution)/shard_map/ppermute | solution.py:30
  32.4 8.6 %collective-permute-start.9 = (s16[264,128]{1,0:T(8,128)(2,1)S(1)}, s16[264,128]{1,0:T(8,128)(2,1)S(1)}, u32[]{:S(2)}, u32[]{:S(2)}) collective-permute-start(s16[264,128]{1,0:T(8,128)(2,1)S(1)} %get-tuple-element.58), channel_id=1, source_target_pairs={{0,3},{1,2},{2,1},{3,0},{4,7},{5,6},{6,5},{7,4},{8,11},{9,10},{10,... | collective-permute-start | bytes 202760 | tf_op jit(solution)/shard_map/ppermute | solution.py:30
  34.0 11.0 %collective-permute-start.16 = (bf16[256,128]{1,0:T(8,128)(2,1)S(1)}, bf16[256,128]{1,0:T(8,128)(2,1)S(1)}, u32[]{:S(2)}, u32[]{:S(2)}) collective-permute-start(bf16[256,128]{1,0:T(8,128)(2,1)S(1)} %shard_map.125.refs_0_), channel_id=1, source_target_pairs={{0,1},{1,0},{2,3},{3,2},{4,5},{5,4},{6,7},{7,6},{8,9},{9,8},{10,11... | collective-permute-start | bytes 196616 | tf_op jit(solution)/shard_map/ppermute | solution.py:30
  36.4 14.2 %collective-permute-start.17 = (bf16[256,128]{1,0:T(8,128)(2,1)S(1)}, bf16[256,128]{1,0:T(8,128)(2,1)S(1)}, u32[]{:S(2)}, u32[]{:S(2)}) collective-permute-start(bf16[256,128]{1,0:T(8,128)(2,1)S(1)} %shard_map.125.refs_0_), channel_id=1, source_target_pairs={{0,2},{1,3},{2,0},{3,1},{4,6},{5,7},{6,4},{7,5},{8,10},{9,11},{10,... | collective-permute-start | bytes 196616 | tf_op jit(solution)/shard_map/ppermute | solution.py:30
  39.7 10.9 %collective-permute-start.18 = (bf16[256,128]{1,0:T(8,128)(2,1)S(1)}, bf16[256,128]{1,0:T(8,128)(2,1)S(1)}, u32[]{:S(2)}, u32[]{:S(2)}) collective-permute-start(bf16[256,128]{1,0:T(8,128)(2,1)S(1)} %shard_map.125.refs_0_), channel_id=1, source_target_pairs={{0,3},{1,2},{2,1},{3,0},{4,7},{5,6},{6,5},{7,4},{8,11},{9,10},{10,... | collective-permute-start | bytes 196616 | tf_op jit(solution)/shard_map/ppermute | solution.py:30
  42.4 10.1 %collective-permute-start.12 = (bf16[256,128]{1,0:T(8,128)(2,1)S(1)}, bf16[256,128]{1,0:T(8,128)(2,1)S(1)}, u32[]{:S(2)}, u32[]{:S(2)}) collective-permute-start(bf16[256,128]{1,0:T(8,128)(2,1)S(1)} %shard_map.123.refs_0_), channel_id=1, source_target_pairs={{0,3},{1,2},{2,1},{3,0},{4,7},{5,6},{6,5},{7,4},{8,11},{9,10},{10,... | collective-permute-start | bytes 196616 | tf_op jit(solution)/shard_map/ppermute | solution.py:30
  56.7 10.8 %collective-permute-start.21 = (s16[136,512]{1,0:T(8,128)(2,1)S(1)}, s16[136,512]{1,0:T(8,128)(2,1)S(1)}, u32[]{:S(2)}, u32[]{:S(2)}) collective-permute-start(s16[136,512]{1,0:T(8,128)(2,1)S(1)} %get-tuple-element.80), channel_id=1, source_target_pairs={{0,16},{4,20},{8,24},{12,28},{16,0},{20,4},{24,8},{28,12},{1,17},{... | collective-permute-start | bytes 417800 | tf_op jit(solution)/shard_map/ppermute | solution.py:30
  58.9 8.6 %collective-permute-start.22 = (s16[136,512]{1,0:T(8,128)(2,1)S(1)}, s16[136,512]{1,0:T(8,128)(2,1)S(1)}, u32[]{:S(2)}, u32[]{:S(2)}) collective-permute-start(s16[136,512]{1,0:T(8,128)(2,1)S(1)} %get-tuple-element.81), channel_id=1, source_target_pairs={{0,24},{4,28},{8,16},{12,20},{16,8},{20,12},{24,0},{28,4},{1,25},{... | collective-permute-start | bytes 417800 | tf_op jit(solution)/shard_map/ppermute | solution.py:30
  60.4 10.4 %collective-permute-start.24 = (s16[136,512]{1,0:T(8,128)(2,1)S(1)}, s16[136,512]{1,0:T(8,128)(2,1)S(1)}, u32[]{:S(2)}, u32[]{:S(2)}) collective-permute-start(s16[136,512]{1,0:T(8,128)(2,1)S(1)} %get-tuple-element.85), channel_id=1, source_target_pairs={{0,8},{4,12},{8,0},{12,4},{16,24},{20,28},{24,16},{28,20},{1,9},{5... | collective-permute-start | bytes 417800 | tf_op jit(solution)/shard_map/ppermute | solution.py:30
  60.6 10.9 %collective-permute-start.25 = (s16[136,512]{1,0:T(8,128)(2,1)S(1)}, s16[136,512]{1,0:T(8,128)(2,1)S(1)}, u32[]{:S(2)}, u32[]{:S(2)}) collective-permute-start(s16[136,512]{1,0:T(8,128)(2,1)S(1)} %get-tuple-element.86), channel_id=1, source_target_pairs={{0,16},{4,20},{8,24},{12,28},{16,0},{20,4},{24,8},{28,12},{1,17},{... | collective-permute-start | bytes 417800 | tf_op jit(solution)/shard_map/ppermute | solution.py:30
  67.7 8.5 %collective-permute-start.27 = (bf16[128,512]{1,0:T(8,128)(2,1)S(1)}, bf16[128,512]{1,0:T(8,128)(2,1)S(1)}, u32[]{:S(2)}, u32[]{:S(2)}) collective-permute-start(bf16[128,512]{1,0:T(8,128)(2,1)S(1)} %shard_map.131.refs_0_), channel_id=1, source_target_pairs={{0,1},{1,0},{2,3},{3,2},{4,5},{5,4},{6,7},{7,6},{8,9},{9,8},{10,11... | collective-permute-start | bytes 393224 | tf_op jit(solution)/shard_map/ppermute | solution.py:30
  67.8 9.0 %collective-permute-start.28 = (bf16[128,512]{1,0:T(8,128)(2,1)S(1)}, bf16[128,512]{1,0:T(8,128)(2,1)S(1)}, u32[]{:S(2)}, u32[]{:S(2)}) collective-permute-start(bf16[128,512]{1,0:T(8,128)(2,1)S(1)} %shard_map.131.refs_0_), channel_id=1, source_target_pairs={{0,2},{1,3},{2,0},{3,1},{4,6},{5,7},{6,4},{7,5},{8,10},{9,11},{10,... | collective-permute-start | bytes 393224 | tf_op jit(solution)/shard_map/ppermute | solution.py:30
  71.7 12.2 %collective-permute-start.33 = (bf16[128,512]{1,0:T(8,128)(2,1)S(1)}, bf16[128,512]{1,0:T(8,128)(2,1)S(1)}, u32[]{:S(2)}, u32[]{:S(2)}) collective-permute-start(bf16[128,512]{1,0:T(8,128)(2,1)S(1)} %shard_map.134.refs_1_), channel_id=1, source_target_pairs={{0,1},{1,0},{2,3},{3,2},{4,5},{5,4},{6,7},{7,6},{8,9},{9,8},{10,11... | collective-permute-start | bytes 393224 | tf_op jit(solution)/shard_map/ppermute | solution.py:30
  71.8 14.8 %collective-permute-start.29 = (bf16[128,512]{1,0:T(8,128)(2,1)S(1)}, bf16[128,512]{1,0:T(8,128)(2,1)S(1)}, u32[]{:S(2)}, u32[]{:S(2)}) collective-permute-start(bf16[128,512]{1,0:T(8,128)(2,1)S(1)} %shard_map.134.refs_1_), channel_id=1, source_target_pairs={{0,2},{1,3},{2,0},{3,1},{4,6},{5,7},{6,4},{7,5},{8,10},{9,11},{10,... | collective-permute-start | bytes 393224 | tf_op jit(solution)/shard_map/ppermute | solution.py:30
  74.7 11.9 %collective-permute-start.30 = (bf16[128,512]{1,0:T(8,128)(2,1)S(1)}, bf16[128,512]{1,0:T(8,128)(2,1)S(1)}, u32[]{:S(2)}, u32[]{:S(2)}) collective-permute-start(bf16[128,512]{1,0:T(8,128)(2,1)S(1)} %shard_map.134.refs_1_), channel_id=1, source_target_pairs={{0,3},{1,2},{2,1},{3,0},{4,7},{5,6},{6,5},{7,4},{8,11},{9,10},{10,... | collective-permute-start | bytes 393224 | tf_op jit(solution)/shard_map/ppermute | solution.py:30
  76.1 10.5 %collective-permute-start.31 = (bf16[128,512]{1,0:T(8,128)(2,1)S(1)}, bf16[128,512]{1,0:T(8,128)(2,1)S(1)}, u32[]{:S(2)}, u32[]{:S(2)}) collective-permute-start(bf16[128,512]{1,0:T(8,128)(2,1)S(1)} %shard_map.131.refs_0_), channel_id=1, source_target_pairs={{1,2},{2,1},{5,6},{6,5},{9,10},{10,9},{13,14},{14,13},{17,18},{18,... | collective-permute-start | bytes 393224 | tf_op jit(solution)/shard_map/ppermute | solution.py:532
  76.8 9.9 %collective-permute-start.32 = (bf16[128,512]{1,0:T(8,128)(2,1)S(1)}, bf16[128,512]{1,0:T(8,128)(2,1)S(1)}, u32[]{:S(2)}, u32[]{:S(2)}) collective-permute-start(bf16[128,512]{1,0:T(8,128)(2,1)S(1)} %collective-permute-done.28.refs_3_), channel_id=1, source_target_pairs={{1,0},{2,3},{5,4},{6,7},{9,8},{10,11},{13,12},{14,15},{17,16},{18,... | collective-permute-start | bytes 393224 | tf_op jit(solution)/shard_map/ppermute | solution.py:533
  (13 other events, 62.5 us)

commit v5 on v4

--- a/solution.py
+++ b/solution.py
@@ -16,6 +16,7 @@
 AT_ONCE = 24
 LARGE = 47
 MEDIUM = 46
+SMALL = 42
 LEVELS = 32767.0
 VMEM = pl.BlockSpec(memory_space=pltpu.VMEM)
 SMEM = pl.BlockSpec(memory_space=pltpu.SMEM)
@@ -104,54 +105,6 @@
                 sends[k - 1][share * TILE + i : share * TILE + i + 1, :] = code.astype(jnp.int16)
 
 
-def targets_kernel(list_ref, count_ref, code, head, out, groups, more, sem, more_sem):
-    blocks = code.shape[0]
-
-    def copy(block, j, buffer, at, sem):
-        start = pl.multiple_of(list_ref[block * TILE + j] * GROUP_ROWS, GROUP_ROWS)
-        return pltpu.make_async_copy(
-            head.at[pl.ds(start, GROUP_ROWS), :],
-            buffer.at[pl.ds(pl.multiple_of(at * GROUP_ROWS, GROUP_ROWS), GROUP_ROWS), :],
-            sem,
-        )
-
-    def place(block, chunk, buffer):
-        depth = AT_ONCE * GROUP_ROWS
-        wanted = code[block : block + 1, :] - chunk * depth
-        spot = lax.broadcasted_iota(jnp.int32, (depth, TILE), 0)
-        hit = jnp.where(spot == wanted, 1.0, 0.0).astype(jnp.bfloat16)
-        return lax.dot_general(
-            hit, buffer[...], (((0,), (0,)), ((), ())), preferred_element_type=jnp.float32
-        )
-
-    for block in range(blocks):
-        for j in range(AT_ONCE):
-            copy(block, j, groups.at[block], j, sem.at[block]).start()
-    for block in range(blocks):
-        rows = pl.ds(block * TILE, TILE)
-        pltpu.make_async_copy(
-            head.at[pl.ds(0, AT_ONCE * GROUP_ROWS), :], groups.at[block], sem.at[block]
-        ).wait()
-        out[rows, :] = place(block, 0, groups.at[block]).astype(jnp.bfloat16)
-
-        @pl.when(count_ref[block] > AT_ONCE)
-        def _(block=block, rows=rows):
-            def body(chunk, carry):
-                def start(j, carry):
-                    copy(block, chunk * AT_ONCE + j, more, j, more_sem).start()
-                    return carry
-
-                lax.fori_loop(0, AT_ONCE, start, 0)
-                pltpu.make_async_copy(
-                    head.at[pl.ds(0, AT_ONCE * GROUP_ROWS), :], more, more_sem
-                ).wait()
-                added = out[rows, :].astype(jnp.float32) + place(block, chunk, more)
-                out[rows, :] = added.astype(jnp.bfloat16)
-                return carry
-
-            lax.fori_loop(1, (count_ref[block] + AT_ONCE - 1) // AT_ONCE, body, 0)
-
-
 def probs_kernel(narrow, slots, group, blocks_ref, live_ref, where_ref, own, *refs):
     recvs, lse, weight, out = refs[: narrow - 1], refs[-3], refs[-2], refs[-1]
     per = slots // narrow
@@ -184,18 +137,60 @@
             )
 
 
-def base_kernel(narrow, slots, blocks_ref, where_ref, tiles, *refs):
-    probs, (target_rows, factor, total) = refs[:-3], refs[-3:]
-    for block in range(factor.shape[0] // TILE):
-        rows = slice(block * TILE, (block + 1) * TILE)
-        start = pl.multiple_of((block ^ where_ref[0]) * TILE, TILE)
-        weight = -factor[rows, :]
+def base_kernel(narrow, slots, blocks_ref, where_ref, list_ref, count_ref, head, tiles, *refs):
+    probs, (code, factor, total, groups, more, sem, more_sem) = refs[:-7], refs[-7:]
+    blocks = code.shape[0]
+
+    def copy(block, j, buffer, at, sem):
+        start = pl.multiple_of(list_ref[block * TILE + j] * GROUP_ROWS, GROUP_ROWS)
+        return pltpu.make_async_copy(
+            head.at[pl.ds(start, GROUP_ROWS), :],
+            buffer.at[pl.ds(pl.multiple_of(at * GROUP_ROWS, GROUP_ROWS), GROUP_ROWS), :],
+            sem,
+        )
+
+    def take(block, chunk, buffer):
+        depth = AT_ONCE * GROUP_ROWS
+        wanted = code[block : block + 1, :] - chunk * depth
+        spot = lax.broadcasted_iota(jnp.int32, (depth, TILE), 0)
+        hit = jnp.where(spot == wanted, 1.0, 0.0).astype(jnp.bfloat16)
+        found = lax.dot_general(
+            hit, buffer[...], (((0,), (0,)), ((), ())), preferred_element_type=jnp.float32
+        )
+        rows = pl.ds(pl.multiple_of((block ^ where_ref[0]) * TILE, TILE), TILE)
+        weight = factor[block * TILE : (block + 1) * TILE, :]
         for lane in range(0, total.shape[1], TILE):
             lanes = slice(lane, lane + TILE)
-            total[pl.ds(start, TILE), lanes] = weight * target_rows[rows, lanes].astype(jnp.float32)
+            total[rows, lanes] -= weight * found[:, lanes]
+
+    for block in range(blocks):
+        for j in range(AT_ONCE):
+            copy(block, j, groups.at[block], j, sem.at[block]).start()
+    total[...] = jnp.zeros_like(total)
     for group in range(GROUPS - 1):
         some = probs[group * narrow : (group + 1) * narrow]
         add_slots(narrow, slots, group, blocks_ref, where_ref, tiles, some, total, slice(None))
+    for block in range(blocks):
+        pltpu.make_async_copy(
+            head.at[pl.ds(0, AT_ONCE * GROUP_ROWS), :], groups.at[block], sem.at[block]
+        ).wait()
+        take(block, 0, groups.at[block])
+
+        @pl.when(count_ref[block] > AT_ONCE)
+        def _(block=block):
+            def body(chunk, carry):
+                def start(j, carry):
+                    copy(block, chunk * AT_ONCE + j, more, j, more_sem).start()
+                    return carry
+
+                lax.fori_loop(0, AT_ONCE, start, 0)
+                pltpu.make_async_copy(
+                    head.at[pl.ds(0, AT_ONCE * GROUP_ROWS), :], more, more_sem
+                ).wait()
+                take(block, chunk, more)
+                return carry
+
+            lax.fori_loop(1, (count_ref[block] + AT_ONCE - 1) // AT_ONCE, body, 0)
 
 
 def grads_kernel(narrow, slots, half, blocks_ref, where_ref, tiles, *refs):
@@ -253,7 +248,7 @@
         copy.wait()
 
 
-def unit_kernel(keys, splits, kind, chunk, ready, where_ref, *refs):
+def unit_kernel(keys, splits, kind, chunk, ready, keep, where_ref, *refs):
     inputs = sum(splits)
     arrived, down, refs = list(refs[:inputs]), refs[inputs], list(refs[inputs + 1 :])
     units = down.shape[0]
@@ -264,13 +259,13 @@
         for _ in range(split - 1):
             piece = piece + arrived.pop(0)[...]
         pieces.append(piece)
-    held = refs.pop(0) if ready else None
+    held = [refs.pop(0).at[0] for _ in range(ready)]
     summed = None if kind == "first" else refs.pop(0)
     if kind == "last":
         gate, up, gate_out, up_out = refs[:4]
     else:
         sum_out = refs[0]
-    down_v, sem = refs[-2:]
+    down_v, sem, keep_sem = refs[-3:]
     steps = [pl.ds(at, chunk) for at in range(0, units, chunk)]
     copies = [
         down_copies(keys[ready:], where_ref, down, down_v.at[step], sem.at[step], rows)
@@ -278,6 +273,10 @@
     ]
     for copy in sum(copies, []):
         copy.start()
+    if keep:
+        kept = down_copies(keep, where_ref, down, refs[-4], keep_sem, slice(None))
+        for copy in kept:
+            copy.start()
     if kind == "first":
         for at in range(HALVES):
             refs[1][:, at * width : (at + 1) * width] = pieces[at]
@@ -288,7 +287,7 @@
                 copies[step][at - ready].wait()
             part = lax.dot_general(
                 piece,
-                held[at, rows, :] if at < ready else down_v[step, at - ready],
+                held[at][rows, :] if at < ready else down_v[step, at - ready],
                 (((1,), (1,)), ((), ())),
                 preferred_element_type=jnp.float32,
             )
@@ -301,6 +300,9 @@
         s = 1.0 / (1.0 + jnp.exp(-g))
         up_out[:, rows] = (total * g * s).astype(jnp.bfloat16)
         gate_out[:, rows] = (total * u * s * (1.0 + g * (1.0 - s))).astype(jnp.bfloat16)
+    if keep:
+        for copy in kept:
+            copy.wait()
 
 
 def shape_of(shape, dtype):
@@ -423,29 +425,24 @@
         if group == GROUPS - 1:
             prob, target_code = lax.optimization_barrier((prob, target_code))
         probs.append([swap(prob, "narrow", k) for k in range(narrow)])
-    (target_rows,) = call(
-        targets_kernel,
-        [shape_of((blocks * TILE, features), bf16)],
-        [SMEM, SMEM, VMEM, HBM],
-        (target_list, target_count, target_code, head_weight),
+    early_probs = sum(probs[:-1], [])
+    (base,) = call(
+        functools.partial(base_kernel, narrow, slots),
+        [shape_of((blocks * TILE, features), f32)],
+        [SMEM] * 4 + [HBM] + [VMEM] * (len(early_probs) + 3),
+        (
+            *(slot_blocks, where, target_list, target_count, head_weight),
+            *(tiles, *early_probs, target_code, factor),
+        ),
         2 * blocks * AT_ONCE * GROUP_ROWS * TILE * features,
-        blocks * AT_ONCE * GROUP_ROWS * features * 2,
+        blocks * TILE * features * 8,
         [
             pltpu.VMEM((blocks, AT_ONCE * GROUP_ROWS, features), bf16),
             pltpu.VMEM((AT_ONCE * GROUP_ROWS, features), bf16),
             pltpu.SemaphoreType.DMA((blocks,)),
             pltpu.SemaphoreType.DMA(()),
         ],
-        MEDIUM,
-    )
-    early_probs = sum(probs[:-1], [])
-    (base,) = call(
-        functools.partial(base_kernel, narrow, slots),
-        [shape_of((blocks * TILE, features), f32)],
-        [SMEM] * 2 + [VMEM] * (len(early_probs) + 3),
-        (slot_blocks, where, tiles, *early_probs, target_rows, factor),
-        slots * TILE * TILE * features,
-        blocks * TILE * features * 4,
+        SMALL,
     )
     probs[-1][-1], base = lax.optimization_barrier((probs[-1][-1], base))
 
@@ -462,23 +459,25 @@
         )
         halves.append((mine, swap(other, "wide", 1)))
     units = gate_pre.shape[1]
-    held_keys = [(k, HALVES - 1) for k in range(2, narrow)]
+    last_keys = [(k, HALVES - 1) for k in range(2, narrow)]
+    held_keys = last_keys[:1]
     chunk = units // 2 if units // 2 % TILE == 0 else units
 
-    def unit(keys, kind, ready, *extra):
+    def unit(keys, kind, held, keep, *extra):
         last = kind == "last"
         inputs = [part for key in keys for part in pieces[key]]
-        count, read = len(keys), len(keys) - ready
-        if ready:
-            extra = (held, *extra)
+        count, read = len(keys), len(keys) - len(held)
+        extra = (*held, *extra)
         return call(
             functools.partial(
-                unit_kernel, keys, [len(pieces[key]) for key in keys], kind, chunk, ready
+                *(unit_kernel, keys, [len(pieces[key]) for key in keys], kind, chunk),
+                *(len(held), keep),
             ),
             [shape_of((TILE, units), bf16)] * 2
             if last
             else [shape_of((TILE, units), f32)]
-            + [shape_of((TILE, features), bf16)] * (kind == "first"),
+            + [shape_of((TILE, features), bf16)] * (kind == "first")
+            + [shape_of((len(keep), units, width), bf16)] * bool(keep),
             [SMEM] + [VMEM] * len(inputs) + [HBM] + [VMEM] * len(extra),
             (where, *inputs, down_weight, *extra),
             2 * count * TILE * units * width,
@@ -486,6 +485,7 @@
             (
                 pltpu.VMEM((units // chunk, read, chunk, width), bf16),
                 pltpu.SemaphoreType.DMA((units // chunk, read)),
+                pltpu.SemaphoreType.DMA((max(1, len(keep)),)),
             ),
             LARGE,
         )
@@ -533,10 +533,11 @@
         ends = lax.ppermute(pieces[2, 0][0], "narrow", [(1, 0), (2, 3)])
         pieces[3, 0] = (near_ends, ends)
     early = [(0, half) for half in range(HALVES)] + [(k, 0) for k in range(1, narrow - 1)]
-    summed, head_grad = unit(early, "first", 0)
-    (summed,) = unit([(1, 1)], "more", 0, summed)
+    summed, head_grad = unit(early, "first", [], [])
+    summed, kept = unit([(1, 1)], "more", [], last_keys[1:2], summed)
     gate_grad, up_grad = unit(
-        [*held_keys, (narrow - 1, 0)], "last", len(held_keys), summed, gate_pre, up_pre
+        *([*last_keys, (narrow - 1, 0)], "last", [held, kept], []),
+        *(summed, gate_pre, up_pre),
     )
     return head_grad, gate_grad, up_grad
 

time: 92.2 us -> 91.5 us (level)
  Pallas kernels: 34 us -> 32.2 us
    pallas_call x17 -> x16, Pallas kernels: 34 us -> 32.2 us  [call(): pl.pallas_call(kernel, out_shape=outs, in_specs=ins, out_specs=[SMEM] * s...]
  transfers between devices with their start and end apart: 34 -> 34, of which waited for: 7 -> 7; matrix products, arithmetic and copies ran while one was open for 8% -> 8% of each run, Pallas kernels for 29% -> 28%
where the time goes in v5:
time: 91.5 us; the launch traced here: 90.3 us
  starting transfers between devices  44.7 us (49%)
  Pallas kernels  32.2 us (35%)
  waiting for transfers between devices  4.68 us (5%)
  other arithmetic  4.16 us (5%)
  local copies, waits for them, and re-layouts  3.46 us (4%)
  between operations  1.13 us (1%)
    ppermute x32, starting transfers between devices, swap(): return lax.ppermute(x, axis, [(i, i ^ mask) for i in range(size)])  42.5 us
    pallas_call x16, Pallas kernels, call(): pl.pallas_call(kernel, out_shape=outs, in_specs=ins, out_specs=[SMEM] * s...  32.2 us
    ppermute x32, waiting for transfers between devices, swap(): return lax.ppermute(x, axis, [(i, i ^ mask) for i in range(size)])  4.68 us
    broadcast_in_dim x3, local copies, waits for them, and re-layouts, over_lanes(): return jnp.broadcast_to(x[:, None], (blocks * TILE, TILE))  1.95 us
  transfers between devices with their start and end apart: 34, of which 7 were waited for; matrix products, arithmetic and copies ran while one was open for 8% of the time, Pallas kernels for 28%

profile of v5, /device:TPU:0, one launch (start us, length us, event | category | flops | bytes accessed | tf_op | source)
XLA Modules:
  0.0 90.3 jit_solution(13178513256676642879)
XLA Ops:
  0.6 3.0 %collective-permute-start = (bf16[128,1024]{1,0:T(8,128)(2,1)}, bf16[128,1024]{1,0:T(8,128)(2,1)S(1)}, u32[]{:S(2)}, u32[]{:S(2)}) collective-permute-start(bf16[128,1024]{1,0:T(8,128)(2,1)} %refs_0_.3), channel_id=1, source_target_pairs={{0,8},{4,12},{8,0},{12,4},{16,24},{20,28},{24,16},{28,20},{1,9},{5... | collective-permute-start | bytes 786440 | tf_op jit(solution)/shard_map/ppermute | solution.py:31
  3.7 1.5 %collective-permute-start.3 = (bf16[128,1024]{1,0:T(8,128)(2,1)}, bf16[128,1024]{1,0:T(8,128)(2,1)S(1)}, u32[]{:S(2)}, u32[]{:S(2)}) collective-permute-start(bf16[128,1024]{1,0:T(8,128)(2,1)} %refs_0_.3), channel_id=1, source_target_pairs={{0,16},{4,20},{8,24},{12,28},{16,0},{20,4},{24,8},{28,12},{1,17},{... | collective-permute-start | bytes 786440 | tf_op jit(solution)/shard_map/ppermute | solution.py:31
  12.9 4.3 %shard_map.121 = (s32[16]{0:T(128)S(1)}, s32[1]{0:T(128)}, bf16[2048,1024]{1,0:T(8,128)(2,1)S(1)}) custom-call(s32[8,1,4]{2,1,0:T(1,128)S(1)} %copy.15.tiles_ref, s32[8,1]{1,0:T(8,128)S(1)} %copy.16.counts_ref, bf16[4096,1024]{1,0:T(8,128)(2,1)} %head.3), custom_call_target="tpu_custom_call" | custom-call | bytes 4194304 | tf_op jit(solution)/shard_map/pallas_call | solution.py:313
  20.1 1.5 %shard_map.124 = (f32[256,128]{1,0:T(8,128)S(1)}, s16[264,128]{1,0:T(8,128)(2,1)S(1)}, s16[264,128]{1,0:T(8,128)(2,1)S(1)}, s16[264,128]{1,0:T(8,128)(2,1)S(1)}) custom-call(s32[16]{0:T(128)S(1)} %get-tuple-element.52.blocks_ref, s32[2]{0:T(128)S(1)} %pad_add_fusion.where_ref, bf16[2048,1024]{1,0:T(8,128)(2,1)S(1)} %get-tuple-element.54.tiles, ...), custom_call_target="tpu_custom_call" | custom-call | flops 268435456 | bytes 2097152 | tf_op jit(solution)/shard_map/pallas_call | solution.py:313
  21.6 2.1 %collective-permute-start.13 = (s16[264,128]{1,0:T(8,128)(2,1)S(1)}, s16[264,128]{1,0:T(8,128)(2,1)S(1)}, u32[]{:S(2)}, u32[]{:S(2)}) collective-permute-start(s16[264,128]{1,0:T(8,128)(2,1)S(1)} %get-tuple-element.68), channel_id=1, source_target_pairs={{0,1},{1,0},{2,3},{3,2},{4,5},{5,4},{6,7},{7,6},{8,9},{9,8},{10,11... | collective-permute-start | bytes 202760 | tf_op jit(solution)/shard_map/ppermute | solution.py:31
  23.7 2.6 %collective-permute-start.14 = (s16[264,128]{1,0:T(8,128)(2,1)S(1)}, s16[264,128]{1,0:T(8,128)(2,1)S(1)}, u32[]{:S(2)}, u32[]{:S(2)}) collective-permute-start(s16[264,128]{1,0:T(8,128)(2,1)S(1)} %get-tuple-element.69), channel_id=1, source_target_pairs={{0,2},{1,3},{2,0},{3,1},{4,6},{5,7},{6,4},{7,5},{8,10},{9,11},{10,... | collective-permute-start | bytes 202760 | tf_op jit(solution)/shard_map/ppermute | solution.py:31
  26.3 1.5 %shard_map.122 = (f32[256,128]{1,0:T(8,128)S(1)}, s16[264,128]{1,0:T(8,128)(2,1)S(1)}, s16[264,128]{1,0:T(8,128)(2,1)S(1)}, s16[264,128]{1,0:T(8,128)(2,1)S(1)}) custom-call(s32[16]{0:T(128)S(1)} %get-tuple-element.52.blocks_ref, s32[2]{0:T(128)S(1)} %pad_add_fusion.where_ref, bf16[2048,1024]{1,0:T(8,128)(2,1)S(1)} %get-tuple-element.54.tiles, ...), custom_call_target="tpu_custom_call" | custom-call | flops 268435456 | bytes 2097152 | tf_op jit(solution)/shard_map/pallas_call | solution.py:313
  28.8 3.5 %collective-permute-start.8 = (s16[264,128]{1,0:T(8,128)(2,1)S(1)}, s16[264,128]{1,0:T(8,128)(2,1)S(1)}, u32[]{:S(2)}, u32[]{:S(2)}) collective-permute-start(s16[264,128]{1,0:T(8,128)(2,1)S(1)} %get-tuple-element.59), channel_id=1, source_target_pairs={{0,2},{1,3},{2,0},{3,1},{4,6},{5,7},{6,4},{7,5},{8,10},{9,11},{10,... | collective-permute-start | bytes 202760 | tf_op jit(solution)/shard_map/ppermute | solution.py:31
  34.0 2.2 %collective-permute-start.16 = (bf16[256,128]{1,0:T(8,128)(2,1)S(1)}, bf16[256,128]{1,0:T(8,128)(2,1)S(1)}, u32[]{:S(2)}, u32[]{:S(2)}) collective-permute-start(bf16[256,128]{1,0:T(8,128)(2,1)S(1)} %shard_map.125.refs_0_), channel_id=1, source_target_pairs={{0,1},{1,0},{2,3},{3,2},{4,5},{5,4},{6,7},{7,6},{8,9},{9,8},{10,11... | collective-permute-start | bytes 196616 | tf_op jit(solution)/shard_map/ppermute | solution.py:31
  36.3 3.5 %collective-permute-start.17 = (bf16[256,128]{1,0:T(8,128)(2,1)S(1)}, bf16[256,128]{1,0:T(8,128)(2,1)S(1)}, u32[]{:S(2)}, u32[]{:S(2)}) collective-permute-start(bf16[256,128]{1,0:T(8,128)(2,1)S(1)} %shard_map.125.refs_0_), channel_id=1, source_target_pairs={{0,2},{1,3},{2,0},{3,1},{4,6},{5,7},{6,4},{7,5},{8,10},{9,11},{10,... | collective-permute-start | bytes 196616 | tf_op jit(solution)/shard_map/ppermute | solution.py:31
  42.5 2.5 %collective-permute-start.12 = (bf16[256,128]{1,0:T(8,128)(2,1)S(1)}, bf16[256,128]{1,0:T(8,128)(2,1)S(1)}, u32[]{:S(2)}, u32[]{:S(2)}) collective-permute-start(bf16[256,128]{1,0:T(8,128)(2,1)S(1)} %shard_map.123.refs_0_), channel_id=1, source_target_pairs={{0,3},{1,2},{2,1},{3,0},{4,7},{5,6},{6,5},{7,4},{8,11},{9,10},{10,... | collective-permute-start | bytes 196616 | tf_op jit(solution)/shard_map/ppermute | solution.py:31
  45.1 1.8 %collective-permute-start.11 = (bf16[256,128]{1,0:T(8,128)(2,1)S(1)}, bf16[256,128]{1,0:T(8,128)(2,1)S(1)}, u32[]{:S(2)}, u32[]{:S(2)}) collective-permute-start(bf16[256,128]{1,0:T(8,128)(2,1)S(1)} %shard_map.123.refs_0_), channel_id=1, source_target_pairs={{0,2},{1,3},{2,0},{3,1},{4,6},{5,7},{6,4},{7,5},{8,10},{9,11},{10,... | collective-permute-start | bytes 196616 | tf_op jit(solution)/shard_map/ppermute | solution.py:31
  46.9 4.5 %shard_map.126.refs_4_ = f32[1024,1024]{1,0:T(8,128)S(1)} custom-call(s32[16]{0:T(128)S(1)} %get-tuple-element.52.blocks_ref, s32[2]{0:T(128)S(1)} %pad_add_fusion.where_ref, s32[1024]{0:T(1024)S(1)} %fusion.3.list_ref, s32[8]{0:T(128)S(1)} %get-tuple-element.66.count_ref, bf16[4096,1024]{1,0:T(8,128)(2,1)} %head.3, ...), custom_call_target="tpu_custom_call" | custom-call | flops 402653184 | bytes 8388608 | tf_op jit(solution)/shard_map/pallas_call | solution.py:313
  55.7 2.2 %collective-permute-start.21 = (s16[136,512]{1,0:T(8,128)(2,1)S(1)}, s16[136,512]{1,0:T(8,128)(2,1)S(1)}, u32[]{:S(2)}, u32[]{:S(2)}) collective-permute-start(s16[136,512]{1,0:T(8,128)(2,1)S(1)} %get-tuple-element.82), channel_id=1, source_target_pairs={{0,16},{4,20},{8,24},{12,28},{16,0},{20,4},{24,8},{28,12},{1,17},{... | collective-permute-start | bytes 417800 | tf_op jit(solution)/shard_map/ppermute | solution.py:31
  59.7 2.0 %collective-permute-start.25 = (s16[136,512]{1,0:T(8,128)(2,1)S(1)}, s16[136,512]{1,0:T(8,128)(2,1)S(1)}, u32[]{:S(2)}, u32[]{:S(2)}) collective-permute-start(s16[136,512]{1,0:T(8,128)(2,1)S(1)} %get-tuple-element.88), channel_id=1, source_target_pairs={{0,16},{4,20},{8,24},{12,28},{16,0},{20,4},{24,8},{28,12},{1,17},{... | collective-permute-start | bytes 417800 | tf_op jit(solution)/shard_map/ppermute | solution.py:31
  62.3 1.7 %collective-permute-start.26 = (s16[136,512]{1,0:T(8,128)(2,1)S(1)}, s16[136,512]{1,0:T(8,128)(2,1)S(1)}, u32[]{:S(2)}, u32[]{:S(2)}) collective-permute-start(s16[136,512]{1,0:T(8,128)(2,1)S(1)} %get-tuple-element.89), channel_id=1, source_target_pairs={{0,24},{4,28},{8,16},{12,20},{16,8},{20,12},{24,0},{28,4},{1,25},{... | collective-permute-start | bytes 417800 | tf_op jit(solution)/shard_map/ppermute | solution.py:31
  63.9 2.1 %shard_map.129.refs_5_ = bf16[1,1792,512]{2,1,0:T(8,128)(2,1)S(1)} custom-call(s32[2]{0:T(128)S(1)} %pad_add_fusion.where_ref, bf16[1792,4096]{1,0:T(8,128)(2,1)} %refs_4_.3), custom_call_target="tpu_custom_call" | custom-call | bytes 1835008 | tf_op jit(solution)/shard_map/pallas_call | solution.py:313
  66.2 1.4 %collective-permute-start.27 = (bf16[128,512]{1,0:T(8,128)(2,1)S(1)}, bf16[128,512]{1,0:T(8,128)(2,1)S(1)}, u32[]{:S(2)}, u32[]{:S(2)}) collective-permute-start(bf16[128,512]{1,0:T(8,128)(2,1)S(1)} %shard_map.130.refs_0_), channel_id=1, source_target_pairs={{0,1},{1,0},{2,3},{3,2},{4,5},{5,4},{6,7},{7,6},{8,9},{9,8},{10,11... | collective-permute-start | bytes 393224 | tf_op jit(solution)/shard_map/ppermute | solution.py:31
  67.6 1.6 %collective-permute-start.28 = (bf16[128,512]{1,0:T(8,128)(2,1)S(1)}, bf16[128,512]{1,0:T(8,128)(2,1)S(1)}, u32[]{:S(2)}, u32[]{:S(2)}) collective-permute-start(bf16[128,512]{1,0:T(8,128)(2,1)S(1)} %shard_map.130.refs_0_), channel_id=1, source_target_pairs={{0,2},{1,3},{2,0},{3,1},{4,6},{5,7},{6,4},{7,5},{8,10},{9,11},{10,... | collective-permute-start | bytes 393224 | tf_op jit(solution)/shard_map/ppermute | solution.py:31
  72.2 1.6 %collective-permute-start.29 = (bf16[128,512]{1,0:T(8,128)(2,1)S(1)}, bf16[128,512]{1,0:T(8,128)(2,1)S(1)}, u32[]{:S(2)}, u32[]{:S(2)}) collective-permute-start(bf16[128,512]{1,0:T(8,128)(2,1)S(1)} %shard_map.133.refs_1_), channel_id=1, source_target_pairs={{0,2},{1,3},{2,0},{3,1},{4,6},{5,7},{6,4},{7,5},{8,10},{9,11},{10,... | collective-permute-start | bytes 393224 | tf_op jit(solution)/shard_map/ppermute | solution.py:31
  75.9 1.5 %collective-permute-start.32 = (bf16[128,512]{1,0:T(8,128)(2,1)S(1)}, bf16[128,512]{1,0:T(8,128)(2,1)S(1)}, u32[]{:S(2)}, u32[]{:S(2)}) collective-permute-start(bf16[128,512]{1,0:T(8,128)(2,1)S(1)} %collective-permute-done.28.refs_3_), channel_id=1, source_target_pairs={{1,0},{2,3},{5,4},{6,7},{9,8},{10,11},{13,12},{14,15},{17,16},{18,... | collective-permute-start | bytes 393224 | tf_op jit(solution)/shard_map/ppermute | solution.py:533
  77.4 5.6 %shard_map.134 = (f32[128,1792]{1,0:T(8,128)S(1)}, bf16[128,1024]{1,0:T(8,128)(2,1)}) custom-call(s32[2]{0:T(128)S(1)} %pad_add_fusion.where_ref, bf16[128,512]{1,0:T(8,128)(2,1)S(1)} %shard_map.130.refs_0_, bf16[128,512]{1,0:T(8,128)(2,1)S(1)} %shard_map.133.refs_1_, bf16[128,512]{1,0:T(8,128)(2,1)S(1)} %collective-permute-done.27.refs_2_, ...), custom_call_target="tpu_custom_call" | custom-call | flops 939524096 | bytes 7340032 | tf_op jit(solution)/shard_map/pallas_call | solution.py:313
  83.0 2.7 %shard_map.135 = (f32[128,1792]{1,0:T(8,128)S(1)}, bf16[1,1792,512]{2,1,0:T(8,128)(2,1)S(1)}) custom-call(s32[2]{0:T(128)S(1)} %pad_add_fusion.where_ref, bf16[128,512]{1,0:T(8,128)(2,1)S(1)} %collective-permute-done.33.refs_0_, bf16[1792,4096]{1,0:T(8,128)(2,1)} %refs_4_.3, f32[128,1792]{1,0:T(8,128)S(1)} %get-tuple-element.92.refs_2_), custom_call_target="tpu_custom_call" | custom-call | flops 234881024 | bytes 1835008 | tf_op jit(solution)/shard_map/pallas_call | solution.py:313
  85.8 4.3 %shard_map.136 = (bf16[128,1792]{1,0:T(8,128)(2,1)}, bf16[128,1792]{1,0:T(8,128)(2,1)}) custom-call(s32[2]{0:T(128)S(1)} %pad_add_fusion.where_ref, bf16[128,512]{1,0:T(8,128)(2,1)S(1)} %collective-permute-done.29.refs_0_, bf16[128,512]{1,0:T(8,128)(2,1)S(1)} %collective-permute-done.30.refs_1_, bf16[128,512]{1,0:T(8,128)(2,1)S(1)} %collective-permute-done.31.refs_2_, ...), custom_call_target="tpu_custom_call" | custom-call | flops 704643072 | bytes 5505024 | tf_op jit(solution)/shard_map/pallas_call | solution.py:313
  (81 shorter events, 27.7 us)
Async XLA Ops:
  0.6 16.6 %collective-permute-start = (bf16[128,1024]{1,0:T(8,128)(2,1)}, bf16[128,1024]{1,0:T(8,128)(2,1)S(1)}, u32[]{:S(2)}, u32[]{:S(2)}) collective-permute-start(bf16[128,1024]{1,0:T(8,128)(2,1)} %refs_0_.3), channel_id=1, source_target_pairs={{0,8},{4,12},{8,0},{12,4},{16,24},{20,28},{24,16},{28,20},{1,9},{5... | collective-permute-start | bytes 786440 | tf_op jit(solution)/shard_map/ppermute | solution.py:31
  3.7 14.6 %collective-permute-start.3 = (bf16[128,1024]{1,0:T(8,128)(2,1)}, bf16[128,1024]{1,0:T(8,128)(2,1)S(1)}, u32[]{:S(2)}, u32[]{:S(2)}) collective-permute-start(bf16[128,1024]{1,0:T(8,128)(2,1)} %refs_0_.3), channel_id=1, source_target_pairs={{0,16},{4,20},{8,24},{12,28},{16,0},{20,4},{24,8},{28,12},{1,17},{... | collective-permute-start | bytes 786440 | tf_op jit(solution)/shard_map/ppermute | solution.py:31
  5.2 13.1 %collective-permute-start.5 = (bf16[128,1024]{1,0:T(8,128)(2,1)}, bf16[128,1024]{1,0:T(8,128)(2,1)S(1)}, u32[]{:S(2)}, u32[]{:S(2)}) collective-permute-start(bf16[128,1024]{1,0:T(8,128)(2,1)} %refs_0_.3), channel_id=1, source_target_pairs={{0,24},{4,28},{8,16},{12,20},{16,8},{20,12},{24,0},{28,4},{1,25},{... | collective-permute-start | bytes 786440 | tf_op jit(solution)/shard_map/ppermute | solution.py:31
  5.2 13.5 %collective-permute-start.1 = (bf16[128,1024]{1,0:T(8,128)(2,1)}, bf16[128,1024]{1,0:T(8,128)(2,1)S(1)}, u32[]{:S(2)}, u32[]{:S(2)}) collective-permute-start(bf16[128,1024]{1,0:T(8,128)(2,1)} %refs_0_.3), channel_id=1, source_target_pairs={{0,4},{4,0},{8,12},{12,8},{16,20},{20,16},{24,28},{28,24},{1,5},{5... | collective-permute-start | bytes 786440 | tf_op jit(solution)/shard_map/ppermute | solution.py:31
  21.6 10.6 %collective-permute-start.13 = (s16[264,128]{1,0:T(8,128)(2,1)S(1)}, s16[264,128]{1,0:T(8,128)(2,1)S(1)}, u32[]{:S(2)}, u32[]{:S(2)}) collective-permute-start(s16[264,128]{1,0:T(8,128)(2,1)S(1)} %get-tuple-element.68), channel_id=1, source_target_pairs={{0,1},{1,0},{2,3},{3,2},{4,5},{5,4},{6,7},{7,6},{8,9},{9,8},{10,11... | collective-permute-start | bytes 202760 | tf_op jit(solution)/shard_map/ppermute | solution.py:31
  23.7 8.6 %collective-permute-start.14 = (s16[264,128]{1,0:T(8,128)(2,1)S(1)}, s16[264,128]{1,0:T(8,128)(2,1)S(1)}, u32[]{:S(2)}, u32[]{:S(2)}) collective-permute-start(s16[264,128]{1,0:T(8,128)(2,1)S(1)} %get-tuple-element.69), channel_id=1, source_target_pairs={{0,2},{1,3},{2,0},{3,1},{4,6},{5,7},{6,4},{7,5},{8,10},{9,11},{10,... | collective-permute-start | bytes 202760 | tf_op jit(solution)/shard_map/ppermute | solution.py:31
  27.8 12.0 %collective-permute-start.7 = (s16[264,128]{1,0:T(8,128)(2,1)S(1)}, s16[264,128]{1,0:T(8,128)(2,1)S(1)}, u32[]{:S(2)}, u32[]{:S(2)}) collective-permute-start(s16[264,128]{1,0:T(8,128)(2,1)S(1)} %get-tuple-element.58), channel_id=1, source_target_pairs={{0,1},{1,0},{2,3},{3,2},{4,5},{5,4},{6,7},{7,6},{8,9},{9,8},{10,11... | collective-permute-start | bytes 202760 | tf_op jit(solution)/shard_map/ppermute | solution.py:31
  28.8 12.4 %collective-permute-start.8 = (s16[264,128]{1,0:T(8,128)(2,1)S(1)}, s16[264,128]{1,0:T(8,128)(2,1)S(1)}, u32[]{:S(2)}, u32[]{:S(2)}) collective-permute-start(s16[264,128]{1,0:T(8,128)(2,1)S(1)} %get-tuple-element.59), channel_id=1, source_target_pairs={{0,2},{1,3},{2,0},{3,1},{4,6},{5,7},{6,4},{7,5},{8,10},{9,11},{10,... | collective-permute-start | bytes 202760 | tf_op jit(solution)/shard_map/ppermute | solution.py:31
  32.3 8.9 %collective-permute-start.9 = (s16[264,128]{1,0:T(8,128)(2,1)S(1)}, s16[264,128]{1,0:T(8,128)(2,1)S(1)}, u32[]{:S(2)}, u32[]{:S(2)}) collective-permute-start(s16[264,128]{1,0:T(8,128)(2,1)S(1)} %get-tuple-element.60), channel_id=1, source_target_pairs={{0,3},{1,2},{2,1},{3,0},{4,7},{5,6},{6,5},{7,4},{8,11},{9,10},{10,... | collective-permute-start | bytes 202760 | tf_op jit(solution)/shard_map/ppermute | solution.py:31
  34.0 11.1 %collective-permute-start.16 = (bf16[256,128]{1,0:T(8,128)(2,1)S(1)}, bf16[256,128]{1,0:T(8,128)(2,1)S(1)}, u32[]{:S(2)}, u32[]{:S(2)}) collective-permute-start(bf16[256,128]{1,0:T(8,128)(2,1)S(1)} %shard_map.125.refs_0_), channel_id=1, source_target_pairs={{0,1},{1,0},{2,3},{3,2},{4,5},{5,4},{6,7},{7,6},{8,9},{9,8},{10,11... | collective-permute-start | bytes 196616 | tf_op jit(solution)/shard_map/ppermute | solution.py:31
  36.3 10.7 %collective-permute-start.17 = (bf16[256,128]{1,0:T(8,128)(2,1)S(1)}, bf16[256,128]{1,0:T(8,128)(2,1)S(1)}, u32[]{:S(2)}, u32[]{:S(2)}) collective-permute-start(bf16[256,128]{1,0:T(8,128)(2,1)S(1)} %shard_map.125.refs_0_), channel_id=1, source_target_pairs={{0,2},{1,3},{2,0},{3,1},{4,6},{5,7},{6,4},{7,5},{8,10},{9,11},{10,... | collective-permute-start | bytes 196616 | tf_op jit(solution)/shard_map/ppermute | solution.py:31
  42.5 9.0 %collective-permute-start.12 = (bf16[256,128]{1,0:T(8,128)(2,1)S(1)}, bf16[256,128]{1,0:T(8,128)(2,1)S(1)}, u32[]{:S(2)}, u32[]{:S(2)}) collective-permute-start(bf16[256,128]{1,0:T(8,128)(2,1)S(1)} %shard_map.123.refs_0_), channel_id=1, source_target_pairs={{0,3},{1,2},{2,1},{3,0},{4,7},{5,6},{6,5},{7,4},{8,11},{9,10},{10,... | collective-permute-start | bytes 196616 | tf_op jit(solution)/shard_map/ppermute | solution.py:31
  55.7 10.3 %collective-permute-start.21 = (s16[136,512]{1,0:T(8,128)(2,1)S(1)}, s16[136,512]{1,0:T(8,128)(2,1)S(1)}, u32[]{:S(2)}, u32[]{:S(2)}) collective-permute-start(s16[136,512]{1,0:T(8,128)(2,1)S(1)} %get-tuple-element.82), channel_id=1, source_target_pairs={{0,16},{4,20},{8,24},{12,28},{16,0},{20,4},{24,8},{28,12},{1,17},{... | collective-permute-start | bytes 417800 | tf_op jit(solution)/shard_map/ppermute | solution.py:31
  58.0 8.1 %collective-permute-start.22 = (s16[136,512]{1,0:T(8,128)(2,1)S(1)}, s16[136,512]{1,0:T(8,128)(2,1)S(1)}, u32[]{:S(2)}, u32[]{:S(2)}) collective-permute-start(s16[136,512]{1,0:T(8,128)(2,1)S(1)} %get-tuple-element.83), channel_id=1, source_target_pairs={{0,24},{4,28},{8,16},{12,20},{16,8},{20,12},{24,0},{28,4},{1,25},{... | collective-permute-start | bytes 417800 | tf_op jit(solution)/shard_map/ppermute | solution.py:31
  59.4 9.8 %collective-permute-start.24 = (s16[136,512]{1,0:T(8,128)(2,1)S(1)}, s16[136,512]{1,0:T(8,128)(2,1)S(1)}, u32[]{:S(2)}, u32[]{:S(2)}) collective-permute-start(s16[136,512]{1,0:T(8,128)(2,1)S(1)} %get-tuple-element.87), channel_id=1, source_target_pairs={{0,8},{4,12},{8,0},{12,4},{16,24},{20,28},{24,16},{28,20},{1,9},{5... | collective-permute-start | bytes 417800 | tf_op jit(solution)/shard_map/ppermute | solution.py:31
  59.7 10.9 %collective-permute-start.25 = (s16[136,512]{1,0:T(8,128)(2,1)S(1)}, s16[136,512]{1,0:T(8,128)(2,1)S(1)}, u32[]{:S(2)}, u32[]{:S(2)}) collective-permute-start(s16[136,512]{1,0:T(8,128)(2,1)S(1)} %get-tuple-element.88), channel_id=1, source_target_pairs={{0,16},{4,20},{8,24},{12,28},{16,0},{20,4},{24,8},{28,12},{1,17},{... | collective-permute-start | bytes 417800 | tf_op jit(solution)/shard_map/ppermute | solution.py:31
  62.3 8.4 %collective-permute-start.26 = (s16[136,512]{1,0:T(8,128)(2,1)S(1)}, s16[136,512]{1,0:T(8,128)(2,1)S(1)}, u32[]{:S(2)}, u32[]{:S(2)}) collective-permute-start(s16[136,512]{1,0:T(8,128)(2,1)S(1)} %get-tuple-element.89), channel_id=1, source_target_pairs={{0,24},{4,28},{8,16},{12,20},{16,8},{20,12},{24,0},{28,4},{1,25},{... | collective-permute-start | bytes 417800 | tf_op jit(solution)/shard_map/ppermute | solution.py:31
  66.2 9.0 %collective-permute-start.27 = (bf16[128,512]{1,0:T(8,128)(2,1)S(1)}, bf16[128,512]{1,0:T(8,128)(2,1)S(1)}, u32[]{:S(2)}, u32[]{:S(2)}) collective-permute-start(bf16[128,512]{1,0:T(8,128)(2,1)S(1)} %shard_map.130.refs_0_), channel_id=1, source_target_pairs={{0,1},{1,0},{2,3},{3,2},{4,5},{5,4},{6,7},{7,6},{8,9},{9,8},{10,11... | collective-permute-start | bytes 393224 | tf_op jit(solution)/shard_map/ppermute | solution.py:31
  67.6 8.3 %collective-permute-start.28 = (bf16[128,512]{1,0:T(8,128)(2,1)S(1)}, bf16[128,512]{1,0:T(8,128)(2,1)S(1)}, u32[]{:S(2)}, u32[]{:S(2)}) collective-permute-start(bf16[128,512]{1,0:T(8,128)(2,1)S(1)} %shard_map.130.refs_0_), channel_id=1, source_target_pairs={{0,2},{1,3},{2,0},{3,1},{4,6},{5,7},{6,4},{7,5},{8,10},{9,11},{10,... | collective-permute-start | bytes 393224 | tf_op jit(solution)/shard_map/ppermute | solution.py:31
  70.7 12.3 %collective-permute-start.33 = (bf16[128,512]{1,0:T(8,128)(2,1)S(1)}, bf16[128,512]{1,0:T(8,128)(2,1)S(1)}, u32[]{:S(2)}, u32[]{:S(2)}) collective-permute-start(bf16[128,512]{1,0:T(8,128)(2,1)S(1)} %shard_map.133.refs_1_), channel_id=1, source_target_pairs={{0,1},{1,0},{2,3},{3,2},{4,5},{5,4},{6,7},{7,6},{8,9},{9,8},{10,11... | collective-permute-start | bytes 393224 | tf_op jit(solution)/shard_map/ppermute | solution.py:31
  72.2 13.6 %collective-permute-start.29 = (bf16[128,512]{1,0:T(8,128)(2,1)S(1)}, bf16[128,512]{1,0:T(8,128)(2,1)S(1)}, u32[]{:S(2)}, u32[]{:S(2)}) collective-permute-start(bf16[128,512]{1,0:T(8,128)(2,1)S(1)} %shard_map.133.refs_1_), channel_id=1, source_target_pairs={{0,2},{1,3},{2,0},{3,1},{4,6},{5,7},{6,4},{7,5},{8,10},{9,11},{10,... | collective-permute-start | bytes 393224 | tf_op jit(solution)/shard_map/ppermute | solution.py:31
  73.8 11.9 %collective-permute-start.30 = (bf16[128,512]{1,0:T(8,128)(2,1)S(1)}, bf16[128,512]{1,0:T(8,128)(2,1)S(1)}, u32[]{:S(2)}, u32[]{:S(2)}) collective-permute-start(bf16[128,512]{1,0:T(8,128)(2,1)S(1)} %shard_map.133.refs_1_), channel_id=1, source_target_pairs={{0,3},{1,2},{2,1},{3,0},{4,7},{5,6},{6,5},{7,4},{8,11},{9,10},{10,... | collective-permute-start | bytes 393224 | tf_op jit(solution)/shard_map/ppermute | solution.py:31
  75.2 10.6 %collective-permute-start.31 = (bf16[128,512]{1,0:T(8,128)(2,1)S(1)}, bf16[128,512]{1,0:T(8,128)(2,1)S(1)}, u32[]{:S(2)}, u32[]{:S(2)}) collective-permute-start(bf16[128,512]{1,0:T(8,128)(2,1)S(1)} %shard_map.130.refs_0_), channel_id=1, source_target_pairs={{1,2},{2,1},{5,6},{6,5},{9,10},{10,9},{13,14},{14,13},{17,18},{18,... | collective-permute-start | bytes 393224 | tf_op jit(solution)/shard_map/ppermute | solution.py:532
  75.9 9.9 %collective-permute-start.32 = (bf16[128,512]{1,0:T(8,128)(2,1)S(1)}, bf16[128,512]{1,0:T(8,128)(2,1)S(1)}, u32[]{:S(2)}, u32[]{:S(2)}) collective-permute-start(bf16[128,512]{1,0:T(8,128)(2,1)S(1)} %collective-permute-done.28.refs_3_), channel_id=1, source_target_pairs={{1,0},{2,3},{5,4},{6,7},{9,8},{10,11},{13,12},{14,15},{17,16},{18,... | collective-permute-start | bytes 393224 | tf_op jit(solution)/shard_map/ppermute | solution.py:533
  (13 other events, 59.3 us)

commit v6 on v4

--- a/solution.py
+++ b/solution.py
@@ -245,12 +245,24 @@
     return [copy(at) for at in range(len(keys))]
 
 
-def hold_kernel(keys, where_ref, down, out, sem):
-    copies = down_copies(keys, where_ref, down, out, sem, slice(None))
-    for copy in copies:
-        copy.start()
-    for copy in copies:
-        copy.wait()
+def hold_kernel(keys, chunk, where_ref, down, out, read, sem):
+    units, width = down.shape[0], out.shape[1]
+    steps = range(0, units, chunk)
+    copies = [
+        down_copies(keys, where_ref, down, read.at[step], sem.at[step], pl.ds(at, chunk))
+        for step, at in enumerate(steps)
+    ]
+    for at in range(len(keys)):
+        for some in copies:
+            some[at].start()
+    for at in range(len(keys)):
+        for step, start in enumerate(steps):
+            copies[step][at].wait()
+            for row in range(0, chunk, TILE):
+                for lane in range(0, width, TILE):
+                    out[at, lane : lane + TILE, start + row : start + row + TILE] = read[
+                        step, at, row : row + TILE, lane : lane + TILE
+                    ].T
 
 
 def unit_kernel(keys, splits, kind, chunk, ready, where_ref, *refs):
@@ -288,8 +300,8 @@
                 copies[step][at - ready].wait()
             part = lax.dot_general(
                 piece,
-                held[at, rows, :] if at < ready else down_v[step, at - ready],
-                (((1,), (1,)), ((), ())),
+                held[at, :, rows] if at < ready else down_v[step, at - ready],
+                (((1,), (0 if at < ready else 1,)), ((), ())),
                 preferred_element_type=jnp.float32,
             )
             total = part if total is None else total + part
@@ -506,13 +518,16 @@
         if half == 0:
             kept, here = lax.optimization_barrier((kept, where))
             (held,) = call(
-                functools.partial(hold_kernel, held_keys),
-                [shape_of((len(held_keys), units, width), bf16)],
+                functools.partial(hold_kernel, held_keys, chunk),
+                [shape_of((len(held_keys), width, units), bf16)],
                 [SMEM, HBM],
                 (here, down_weight),
                 0,
                 len(held_keys) * units * width * 2,
-                [pltpu.SemaphoreType.DMA((len(held_keys),))],
+                [
+                    pltpu.VMEM((units // chunk, len(held_keys), chunk, width), bf16),
+                    pltpu.SemaphoreType.DMA((units // chunk, len(held_keys))),
+                ],
                 MEDIUM,
             )
             kept, held = lax.optimization_barrier((kept, held))

time: 92.2 us -> 92.5 us (level)
  transfers between devices with their start and end apart: 34 -> 34, of which waited for: 7 -> 7; matrix products, arithmetic and copies ran while one was open for 8% -> 8% of each run, Pallas kernels for 29% -> 30%
where the time goes in v6:
time: 92.5 us; the launch traced here: 91.1 us
  starting transfers between devices  44.3 us (48%)
  Pallas kernels  34.3 us (37%)
  other arithmetic  4.16 us (4%)
  waiting for transfers between devices  3.65 us (4%)
  local copies, waits for them, and re-layouts  3.46 us (4%)
  between operations  1.15 us (1%)
    ppermute x32, starting transfers between devices, swap(): return lax.ppermute(x, axis, [(i, i ^ mask) for i in range(size)])  42.4 us
    pallas_call x17, Pallas kernels, call(): pl.pallas_call(kernel, out_shape=outs, in_specs=ins, out_specs=[SMEM] * s...  34.3 us
    ppermute x32, waiting for transfers between devices, swap(): return lax.ppermute(x, axis, [(i, i ^ mask) for i in range(size)])  3.64 us
    broadcast_in_dim x3, local copies, waits for them, and re-layouts, over_lanes(): return jnp.broadcast_to(x[:, None], (blocks * TILE, TILE))  1.95 us
  transfers between devices with their start and end apart: 34, of which 7 were waited for; matrix products, arithmetic and copies ran while one was open for 8% of the time, Pallas kernels for 30%

profile of v6, /device:TPU:0, one launch (start us, length us, event | category | flops | bytes accessed | tf_op | source)
XLA Modules:
  0.0 91.1 jit_solution(10131025840587552)
XLA Ops:
  0.6 3.0 %collective-permute-start = (bf16[128,1024]{1,0:T(8,128)(2,1)}, bf16[128,1024]{1,0:T(8,128)(2,1)S(1)}, u32[]{:S(2)}, u32[]{:S(2)}) collective-permute-start(bf16[128,1024]{1,0:T(8,128)(2,1)} %refs_0_.3), channel_id=1, source_target_pairs={{0,8},{4,12},{8,0},{12,4},{16,24},{20,28},{24,16},{28,20},{1,9},{5... | collective-permute-start | bytes 786440 | tf_op jit(solution)/shard_map/ppermute | solution.py:30
  3.7 1.5 %collective-permute-start.3 = (bf16[128,1024]{1,0:T(8,128)(2,1)}, bf16[128,1024]{1,0:T(8,128)(2,1)S(1)}, u32[]{:S(2)}, u32[]{:S(2)}) collective-permute-start(bf16[128,1024]{1,0:T(8,128)(2,1)} %refs_0_.3), channel_id=1, source_target_pairs={{0,16},{4,20},{8,24},{12,28},{16,0},{20,4},{24,8},{28,12},{1,17},{... | collective-permute-start | bytes 786440 | tf_op jit(solution)/shard_map/ppermute | solution.py:30
  12.9 4.3 %shard_map.121 = (s32[16]{0:T(128)S(1)}, s32[1]{0:T(128)}, bf16[2048,1024]{1,0:T(8,128)(2,1)S(1)}) custom-call(s32[8,1,4]{2,1,0:T(1,128)S(1)} %copy.15.tiles_ref, s32[8,1]{1,0:T(8,128)S(1)} %copy.16.counts_ref, bf16[4096,1024]{1,0:T(8,128)(2,1)} %head.3), custom_call_target="tpu_custom_call" | custom-call | bytes 4194304 | tf_op jit(solution)/shard_map/pallas_call | solution.py:323
  20.1 1.6 %shard_map.124 = (f32[256,128]{1,0:T(8,128)S(1)}, s16[264,128]{1,0:T(8,128)(2,1)S(1)}, s16[264,128]{1,0:T(8,128)(2,1)S(1)}, s16[264,128]{1,0:T(8,128)(2,1)S(1)}) custom-call(s32[16]{0:T(128)S(1)} %get-tuple-element.50.blocks_ref, s32[2]{0:T(128)S(1)} %pad_add_fusion.where_ref, bf16[2048,1024]{1,0:T(8,128)(2,1)S(1)} %get-tuple-element.52.tiles, ...), custom_call_target="tpu_custom_call" | custom-call | flops 268435456 | bytes 2097152 | tf_op jit(solution)/shard_map/pallas_call | solution.py:323
  21.7 2.1 %collective-permute-start.13 = (s16[264,128]{1,0:T(8,128)(2,1)S(1)}, s16[264,128]{1,0:T(8,128)(2,1)S(1)}, u32[]{:S(2)}, u32[]{:S(2)}) collective-permute-start(s16[264,128]{1,0:T(8,128)(2,1)S(1)} %get-tuple-element.64), channel_id=1, source_target_pairs={{0,1},{1,0},{2,3},{3,2},{4,5},{5,4},{6,7},{7,6},{8,9},{9,8},{10,11... | collective-permute-start | bytes 202760 | tf_op jit(solution)/shard_map/ppermute | solution.py:30
  23.8 2.6 %collective-permute-start.14 = (s16[264,128]{1,0:T(8,128)(2,1)S(1)}, s16[264,128]{1,0:T(8,128)(2,1)S(1)}, u32[]{:S(2)}, u32[]{:S(2)}) collective-permute-start(s16[264,128]{1,0:T(8,128)(2,1)S(1)} %get-tuple-element.65), channel_id=1, source_target_pairs={{0,2},{1,3},{2,0},{3,1},{4,6},{5,7},{6,4},{7,5},{8,10},{9,11},{10,... | collective-permute-start | bytes 202760 | tf_op jit(solution)/shard_map/ppermute | solution.py:30
  26.4 1.6 %shard_map.122 = (f32[256,128]{1,0:T(8,128)S(1)}, s16[264,128]{1,0:T(8,128)(2,1)S(1)}, s16[264,128]{1,0:T(8,128)(2,1)S(1)}, s16[264,128]{1,0:T(8,128)(2,1)S(1)}) custom-call(s32[16]{0:T(128)S(1)} %get-tuple-element.50.blocks_ref, s32[2]{0:T(128)S(1)} %pad_add_fusion.where_ref, bf16[2048,1024]{1,0:T(8,128)(2,1)S(1)} %get-tuple-element.52.tiles, ...), custom_call_target="tpu_custom_call" | custom-call | flops 268435456 | bytes 2097152 | tf_op jit(solution)/shard_map/pallas_call | solution.py:323
  28.9 3.5 %collective-permute-start.8 = (s16[264,128]{1,0:T(8,128)(2,1)S(1)}, s16[264,128]{1,0:T(8,128)(2,1)S(1)}, u32[]{:S(2)}, u32[]{:S(2)}) collective-permute-start(s16[264,128]{1,0:T(8,128)(2,1)S(1)} %get-tuple-element.57), channel_id=1, source_target_pairs={{0,2},{1,3},{2,0},{3,1},{4,6},{5,7},{6,4},{7,5},{8,10},{9,11},{10,... | collective-permute-start | bytes 202760 | tf_op jit(solution)/shard_map/ppermute | solution.py:30
  34.0 2.4 %collective-permute-start.16 = (bf16[256,128]{1,0:T(8,128)(2,1)S(1)}, bf16[256,128]{1,0:T(8,128)(2,1)S(1)}, u32[]{:S(2)}, u32[]{:S(2)}) collective-permute-start(bf16[256,128]{1,0:T(8,128)(2,1)S(1)} %shard_map.125.refs_0_), channel_id=1, source_target_pairs={{0,1},{1,0},{2,3},{3,2},{4,5},{5,4},{6,7},{7,6},{8,9},{9,8},{10,11... | collective-permute-start | bytes 196616 | tf_op jit(solution)/shard_map/ppermute | solution.py:30
  36.4 3.3 %collective-permute-start.17 = (bf16[256,128]{1,0:T(8,128)(2,1)S(1)}, bf16[256,128]{1,0:T(8,128)(2,1)S(1)}, u32[]{:S(2)}, u32[]{:S(2)}) collective-permute-start(bf16[256,128]{1,0:T(8,128)(2,1)S(1)} %shard_map.125.refs_0_), channel_id=1, source_target_pairs={{0,2},{1,3},{2,0},{3,1},{4,6},{5,7},{6,4},{7,5},{8,10},{9,11},{10,... | collective-permute-start | bytes 196616 | tf_op jit(solution)/shard_map/ppermute | solution.py:30
  42.4 2.5 %collective-permute-start.12 = (bf16[256,128]{1,0:T(8,128)(2,1)S(1)}, bf16[256,128]{1,0:T(8,128)(2,1)S(1)}, u32[]{:S(2)}, u32[]{:S(2)}) collective-permute-start(bf16[256,128]{1,0:T(8,128)(2,1)S(1)} %shard_map.123.refs_0_), channel_id=1, source_target_pairs={{0,3},{1,2},{2,1},{3,0},{4,7},{5,6},{6,5},{7,4},{8,11},{9,10},{10,... | collective-permute-start | bytes 196616 | tf_op jit(solution)/shard_map/ppermute | solution.py:30
  45.0 1.8 %collective-permute-start.11 = (bf16[256,128]{1,0:T(8,128)(2,1)S(1)}, bf16[256,128]{1,0:T(8,128)(2,1)S(1)}, u32[]{:S(2)}, u32[]{:S(2)}) collective-permute-start(bf16[256,128]{1,0:T(8,128)(2,1)S(1)} %shard_map.123.refs_0_), channel_id=1, source_target_pairs={{0,2},{1,3},{2,0},{3,1},{4,6},{5,7},{6,4},{7,5},{8,10},{9,11},{10,... | collective-permute-start | bytes 196616 | tf_op jit(solution)/shard_map/ppermute | solution.py:30
  46.8 4.0 %shard_map.126.refs_4_ = bf16[1024,1024]{1,0:T(8,128)(2,1)S(1)} custom-call(s32[1024]{0:T(1024)S(1)} %fusion.3.list_ref, s32[8]{0:T(128)S(1)} %get-tuple-element.68.count_ref, s32[8,128]{1,0:T(8,128)S(1)} %fusion.5.code, bf16[4096,1024]{1,0:T(8,128)(2,1)} %head.3), custom_call_target="tpu_custom_call" | custom-call | flops 402653184 | bytes 3145728 | tf_op jit(solution)/shard_map/pallas_call | solution.py:323
  50.8 1.8 %shard_map.127.refs_4_ = f32[1024,1024]{1,0:T(8,128)S(1)} custom-call(s32[16]{0:T(128)S(1)} %get-tuple-element.50.blocks_ref, s32[2]{0:T(128)S(1)} %pad_add_fusion.where_ref, bf16[2048,1024]{1,0:T(8,128)(2,1)S(1)} %get-tuple-element.52.tiles, bf16[256,128]{1,0:T(8,128)(2,1)S(1)} %shard_map.125.refs_0_, bf16[256,128]{1,0:T(8,128)(2,1)S(1)} %collective-permute-done.16.refs_1_, ...), custom_call_target="tpu_custom_call" | custom-call | flops 268435456 | bytes 4194304 | tf_op jit(solution)/shard_map/pallas_call | solution.py:323
  56.9 2.2 %collective-permute-start.21 = (s16[136,512]{1,0:T(8,128)(2,1)S(1)}, s16[136,512]{1,0:T(8,128)(2,1)S(1)}, u32[]{:S(2)}, u32[]{:S(2)}) collective-permute-start(s16[136,512]{1,0:T(8,128)(2,1)S(1)} %get-tuple-element.80), channel_id=1, source_target_pairs={{0,16},{4,20},{8,24},{12,28},{16,0},{20,4},{24,8},{28,12},{1,17},{... | collective-permute-start | bytes 417800 | tf_op jit(solution)/shard_map/ppermute | solution.py:30
  60.8 2.0 %collective-permute-start.25 = (s16[136,512]{1,0:T(8,128)(2,1)S(1)}, s16[136,512]{1,0:T(8,128)(2,1)S(1)}, u32[]{:S(2)}, u32[]{:S(2)}) collective-permute-start(s16[136,512]{1,0:T(8,128)(2,1)S(1)} %get-tuple-element.86), channel_id=1, source_target_pairs={{0,16},{4,20},{8,24},{12,28},{16,0},{20,4},{24,8},{28,12},{1,17},{... | collective-permute-start | bytes 417800 | tf_op jit(solution)/shard_map/ppermute | solution.py:30
  63.4 1.7 %collective-permute-start.26 = (s16[136,512]{1,0:T(8,128)(2,1)S(1)}, s16[136,512]{1,0:T(8,128)(2,1)S(1)}, u32[]{:S(2)}, u32[]{:S(2)}) collective-permute-start(s16[136,512]{1,0:T(8,128)(2,1)S(1)} %get-tuple-element.87), channel_id=1, source_target_pairs={{0,24},{4,28},{8,16},{12,20},{16,8},{20,12},{24,0},{28,4},{1,25},{... | collective-permute-start | bytes 417800 | tf_op jit(solution)/shard_map/ppermute | solution.py:30
  65.1 2.9 %shard_map.130.refs_5_ = bf16[2,512,1792]{2,1,0:T(8,128)(2,1)S(1)} custom-call(s32[2]{0:T(128)S(1)} %pad_add_fusion.where_ref, bf16[1792,4096]{1,0:T(8,128)(2,1)} %refs_4_.3), custom_call_target="tpu_custom_call" | custom-call | bytes 3670016 | tf_op jit(solution)/shard_map/pallas_call | solution.py:323
  68.3 2.9 %collective-permute-start.28 = (bf16[128,512]{1,0:T(8,128)(2,1)S(1)}, bf16[128,512]{1,0:T(8,128)(2,1)S(1)}, u32[]{:S(2)}, u32[]{:S(2)}) collective-permute-start(bf16[128,512]{1,0:T(8,128)(2,1)S(1)} %shard_map.131.refs_0_), channel_id=1, source_target_pairs={{0,2},{1,3},{2,0},{3,1},{4,6},{5,7},{6,4},{7,5},{8,10},{9,11},{10,... | collective-permute-start | bytes 393224 | tf_op jit(solution)/shard_map/ppermute | solution.py:30
  72.0 2.9 %collective-permute-start.29 = (bf16[128,512]{1,0:T(8,128)(2,1)S(1)}, bf16[128,512]{1,0:T(8,128)(2,1)S(1)}, u32[]{:S(2)}, u32[]{:S(2)}) collective-permute-start(bf16[128,512]{1,0:T(8,128)(2,1)S(1)} %shard_map.134.refs_1_), channel_id=1, source_target_pairs={{0,2},{1,3},{2,0},{3,1},{4,6},{5,7},{6,4},{7,5},{8,10},{9,11},{10,... | collective-permute-start | bytes 393224 | tf_op jit(solution)/shard_map/ppermute | solution.py:30
  74.9 1.4 %collective-permute-start.30 = (bf16[128,512]{1,0:T(8,128)(2,1)S(1)}, bf16[128,512]{1,0:T(8,128)(2,1)S(1)}, u32[]{:S(2)}, u32[]{:S(2)}) collective-permute-start(bf16[128,512]{1,0:T(8,128)(2,1)S(1)} %shard_map.134.refs_1_), channel_id=1, source_target_pairs={{0,3},{1,2},{2,1},{3,0},{4,7},{5,6},{6,5},{7,4},{8,11},{9,10},{10,... | collective-permute-start | bytes 393224 | tf_op jit(solution)/shard_map/ppermute | solution.py:30
  78.3 5.6 %shard_map.135 = (f32[128,1792]{1,0:T(8,128)S(1)}, bf16[128,1024]{1,0:T(8,128)(2,1)}) custom-call(s32[2]{0:T(128)S(1)} %pad_add_fusion.where_ref, bf16[128,512]{1,0:T(8,128)(2,1)S(1)} %shard_map.131.refs_0_, bf16[128,512]{1,0:T(8,128)(2,1)S(1)} %shard_map.134.refs_1_, bf16[128,512]{1,0:T(8,128)(2,1)S(1)} %collective-permute-done.27.refs_2_, ...), custom_call_target="tpu_custom_call" | custom-call | flops 939524096 | bytes 7340032 | tf_op jit(solution)/shard_map/pallas_call | solution.py:323
  84.0 2.7 %shard_map.136.refs_6_ = f32[128,1792]{1,0:T(8,128)S(1)} custom-call(s32[2]{0:T(128)S(1)} %pad_add_fusion.where_ref, bf16[128,512]{1,0:T(8,128)(2,1)S(1)} %collective-permute-done.33.refs_0_, bf16[1792,4096]{1,0:T(8,128)(2,1)} %refs_4_.3, f32[128,1792]{1,0:T(8,128)S(1)} %get-tuple-element.90.refs_2_), custom_call_target="tpu_custom_call" | custom-call | flops 234881024 | bytes 1835008 | tf_op jit(solution)/shard_map/pallas_call | solution.py:323
  86.7 4.2 %shard_map.137 = (bf16[128,1792]{1,0:T(8,128)(2,1)}, bf16[128,1792]{1,0:T(8,128)(2,1)}) custom-call(s32[2]{0:T(128)S(1)} %pad_add_fusion.where_ref, bf16[128,512]{1,0:T(8,128)(2,1)S(1)} %collective-permute-done.29.refs_0_, bf16[128,512]{1,0:T(8,128)(2,1)S(1)} %collective-permute-done.30.refs_1_, bf16[128,512]{1,0:T(8,128)(2,1)S(1)} %collective-permute-done.31.refs_2_, ...), custom_call_target="tpu_custom_call" | custom-call | flops 704643072 | bytes 5505024 | tf_op jit(solution)/shard_map/pallas_call | solution.py:323
  (82 shorter events, 25.5 us)
Async XLA Ops:
  0.6 16.6 %collective-permute-start = (bf16[128,1024]{1,0:T(8,128)(2,1)}, bf16[128,1024]{1,0:T(8,128)(2,1)S(1)}, u32[]{:S(2)}, u32[]{:S(2)}) collective-permute-start(bf16[128,1024]{1,0:T(8,128)(2,1)} %refs_0_.3), channel_id=1, source_target_pairs={{0,8},{4,12},{8,0},{12,4},{16,24},{20,28},{24,16},{28,20},{1,9},{5... | collective-permute-start | bytes 786440 | tf_op jit(solution)/shard_map/ppermute | solution.py:30
  3.7 14.6 %collective-permute-start.3 = (bf16[128,1024]{1,0:T(8,128)(2,1)}, bf16[128,1024]{1,0:T(8,128)(2,1)S(1)}, u32[]{:S(2)}, u32[]{:S(2)}) collective-permute-start(bf16[128,1024]{1,0:T(8,128)(2,1)} %refs_0_.3), channel_id=1, source_target_pairs={{0,16},{4,20},{8,24},{12,28},{16,0},{20,4},{24,8},{28,12},{1,17},{... | collective-permute-start | bytes 786440 | tf_op jit(solution)/shard_map/ppermute | solution.py:30
  5.2 13.1 %collective-permute-start.5 = (bf16[128,1024]{1,0:T(8,128)(2,1)}, bf16[128,1024]{1,0:T(8,128)(2,1)S(1)}, u32[]{:S(2)}, u32[]{:S(2)}) collective-permute-start(bf16[128,1024]{1,0:T(8,128)(2,1)} %refs_0_.3), channel_id=1, source_target_pairs={{0,24},{4,28},{8,16},{12,20},{16,8},{20,12},{24,0},{28,4},{1,25},{... | collective-permute-start | bytes 786440 | tf_op jit(solution)/shard_map/ppermute | solution.py:30
  5.2 13.5 %collective-permute-start.1 = (bf16[128,1024]{1,0:T(8,128)(2,1)}, bf16[128,1024]{1,0:T(8,128)(2,1)S(1)}, u32[]{:S(2)}, u32[]{:S(2)}) collective-permute-start(bf16[128,1024]{1,0:T(8,128)(2,1)} %refs_0_.3), channel_id=1, source_target_pairs={{0,4},{4,0},{8,12},{12,8},{16,20},{20,16},{24,28},{28,24},{1,5},{5... | collective-permute-start | bytes 786440 | tf_op jit(solution)/shard_map/ppermute | solution.py:30
  21.7 10.7 %collective-permute-start.13 = (s16[264,128]{1,0:T(8,128)(2,1)S(1)}, s16[264,128]{1,0:T(8,128)(2,1)S(1)}, u32[]{:S(2)}, u32[]{:S(2)}) collective-permute-start(s16[264,128]{1,0:T(8,128)(2,1)S(1)} %get-tuple-element.64), channel_id=1, source_target_pairs={{0,1},{1,0},{2,3},{3,2},{4,5},{5,4},{6,7},{7,6},{8,9},{9,8},{10,11... | collective-permute-start | bytes 202760 | tf_op jit(solution)/shard_map/ppermute | solution.py:30
  23.8 8.6 %collective-permute-start.14 = (s16[264,128]{1,0:T(8,128)(2,1)S(1)}, s16[264,128]{1,0:T(8,128)(2,1)S(1)}, u32[]{:S(2)}, u32[]{:S(2)}) collective-permute-start(s16[264,128]{1,0:T(8,128)(2,1)S(1)} %get-tuple-element.65), channel_id=1, source_target_pairs={{0,2},{1,3},{2,0},{3,1},{4,6},{5,7},{6,4},{7,5},{8,10},{9,11},{10,... | collective-permute-start | bytes 202760 | tf_op jit(solution)/shard_map/ppermute | solution.py:30
  28.0 11.7 %collective-permute-start.7 = (s16[264,128]{1,0:T(8,128)(2,1)S(1)}, s16[264,128]{1,0:T(8,128)(2,1)S(1)}, u32[]{:S(2)}, u32[]{:S(2)}) collective-permute-start(s16[264,128]{1,0:T(8,128)(2,1)S(1)} %get-tuple-element.56), channel_id=1, source_target_pairs={{0,1},{1,0},{2,3},{3,2},{4,5},{5,4},{6,7},{7,6},{8,9},{9,8},{10,11... | collective-permute-start | bytes 202760 | tf_op jit(solution)/shard_map/ppermute | solution.py:30
  28.9 12.1 %collective-permute-start.8 = (s16[264,128]{1,0:T(8,128)(2,1)S(1)}, s16[264,128]{1,0:T(8,128)(2,1)S(1)}, u32[]{:S(2)}, u32[]{:S(2)}) collective-permute-start(s16[264,128]{1,0:T(8,128)(2,1)S(1)} %get-tuple-element.57), channel_id=1, source_target_pairs={{0,2},{1,3},{2,0},{3,1},{4,6},{5,7},{6,4},{7,5},{8,10},{9,11},{10,... | collective-permute-start | bytes 202760 | tf_op jit(solution)/shard_map/ppermute | solution.py:30
  32.4 8.6 %collective-permute-start.9 = (s16[264,128]{1,0:T(8,128)(2,1)S(1)}, s16[264,128]{1,0:T(8,128)(2,1)S(1)}, u32[]{:S(2)}, u32[]{:S(2)}) collective-permute-start(s16[264,128]{1,0:T(8,128)(2,1)S(1)} %get-tuple-element.58), channel_id=1, source_target_pairs={{0,3},{1,2},{2,1},{3,0},{4,7},{5,6},{6,5},{7,4},{8,11},{9,10},{10,... | collective-permute-start | bytes 202760 | tf_op jit(solution)/shard_map/ppermute | solution.py:30
  34.0 11.0 %collective-permute-start.16 = (bf16[256,128]{1,0:T(8,128)(2,1)S(1)}, bf16[256,128]{1,0:T(8,128)(2,1)S(1)}, u32[]{:S(2)}, u32[]{:S(2)}) collective-permute-start(bf16[256,128]{1,0:T(8,128)(2,1)S(1)} %shard_map.125.refs_0_), channel_id=1, source_target_pairs={{0,1},{1,0},{2,3},{3,2},{4,5},{5,4},{6,7},{7,6},{8,9},{9,8},{10,11... | collective-permute-start | bytes 196616 | tf_op jit(solution)/shard_map/ppermute | solution.py:30
  36.4 14.4 %collective-permute-start.17 = (bf16[256,128]{1,0:T(8,128)(2,1)S(1)}, bf16[256,128]{1,0:T(8,128)(2,1)S(1)}, u32[]{:S(2)}, u32[]{:S(2)}) collective-permute-start(bf16[256,128]{1,0:T(8,128)(2,1)S(1)} %shard_map.125.refs_0_), channel_id=1, source_target_pairs={{0,2},{1,3},{2,0},{3,1},{4,6},{5,7},{6,4},{7,5},{8,10},{9,11},{10,... | collective-permute-start | bytes 196616 | tf_op jit(solution)/shard_map/ppermute | solution.py:30
  39.7 11.1 %collective-permute-start.18 = (bf16[256,128]{1,0:T(8,128)(2,1)S(1)}, bf16[256,128]{1,0:T(8,128)(2,1)S(1)}, u32[]{:S(2)}, u32[]{:S(2)}) collective-permute-start(bf16[256,128]{1,0:T(8,128)(2,1)S(1)} %shard_map.125.refs_0_), channel_id=1, source_target_pairs={{0,3},{1,2},{2,1},{3,0},{4,7},{5,6},{6,5},{7,4},{8,11},{9,10},{10,... | collective-permute-start | bytes 196616 | tf_op jit(solution)/shard_map/ppermute | solution.py:30
  42.4 10.2 %collective-permute-start.12 = (bf16[256,128]{1,0:T(8,128)(2,1)S(1)}, bf16[256,128]{1,0:T(8,128)(2,1)S(1)}, u32[]{:S(2)}, u32[]{:S(2)}) collective-permute-start(bf16[256,128]{1,0:T(8,128)(2,1)S(1)} %shard_map.123.refs_0_), channel_id=1, source_target_pairs={{0,3},{1,2},{2,1},{3,0},{4,7},{5,6},{6,5},{7,4},{8,11},{9,10},{10,... | collective-permute-start | bytes 196616 | tf_op jit(solution)/shard_map/ppermute | solution.py:30
  56.9 11.1 %collective-permute-start.21 = (s16[136,512]{1,0:T(8,128)(2,1)S(1)}, s16[136,512]{1,0:T(8,128)(2,1)S(1)}, u32[]{:S(2)}, u32[]{:S(2)}) collective-permute-start(s16[136,512]{1,0:T(8,128)(2,1)S(1)} %get-tuple-element.80), channel_id=1, source_target_pairs={{0,16},{4,20},{8,24},{12,28},{16,0},{20,4},{24,8},{28,12},{1,17},{... | collective-permute-start | bytes 417800 | tf_op jit(solution)/shard_map/ppermute | solution.py:30
  59.1 8.9 %collective-permute-start.22 = (s16[136,512]{1,0:T(8,128)(2,1)S(1)}, s16[136,512]{1,0:T(8,128)(2,1)S(1)}, u32[]{:S(2)}, u32[]{:S(2)}) collective-permute-start(s16[136,512]{1,0:T(8,128)(2,1)S(1)} %get-tuple-element.81), channel_id=1, source_target_pairs={{0,24},{4,28},{8,16},{12,20},{16,8},{20,12},{24,0},{28,4},{1,25},{... | collective-permute-start | bytes 417800 | tf_op jit(solution)/shard_map/ppermute | solution.py:30
  60.5 10.7 %collective-permute-start.24 = (s16[136,512]{1,0:T(8,128)(2,1)S(1)}, s16[136,512]{1,0:T(8,128)(2,1)S(1)}, u32[]{:S(2)}, u32[]{:S(2)}) collective-permute-start(s16[136,512]{1,0:T(8,128)(2,1)S(1)} %get-tuple-element.85), channel_id=1, source_target_pairs={{0,8},{4,12},{8,0},{12,4},{16,24},{20,28},{24,16},{28,20},{1,9},{5... | collective-permute-start | bytes 417800 | tf_op jit(solution)/shard_map/ppermute | solution.py:30
  60.8 10.9 %collective-permute-start.25 = (s16[136,512]{1,0:T(8,128)(2,1)S(1)}, s16[136,512]{1,0:T(8,128)(2,1)S(1)}, u32[]{:S(2)}, u32[]{:S(2)}) collective-permute-start(s16[136,512]{1,0:T(8,128)(2,1)S(1)} %get-tuple-element.86), channel_id=1, source_target_pairs={{0,16},{4,20},{8,24},{12,28},{16,0},{20,4},{24,8},{28,12},{1,17},{... | collective-permute-start | bytes 417800 | tf_op jit(solution)/shard_map/ppermute | solution.py:30
  63.4 8.3 %collective-permute-start.26 = (s16[136,512]{1,0:T(8,128)(2,1)S(1)}, s16[136,512]{1,0:T(8,128)(2,1)S(1)}, u32[]{:S(2)}, u32[]{:S(2)}) collective-permute-start(s16[136,512]{1,0:T(8,128)(2,1)S(1)} %get-tuple-element.87), channel_id=1, source_target_pairs={{0,24},{4,28},{8,16},{12,20},{16,8},{20,12},{24,0},{28,4},{1,25},{... | collective-permute-start | bytes 417800 | tf_op jit(solution)/shard_map/ppermute | solution.py:30
  68.3 8.7 %collective-permute-start.28 = (bf16[128,512]{1,0:T(8,128)(2,1)S(1)}, bf16[128,512]{1,0:T(8,128)(2,1)S(1)}, u32[]{:S(2)}, u32[]{:S(2)}) collective-permute-start(bf16[128,512]{1,0:T(8,128)(2,1)S(1)} %shard_map.131.refs_0_), channel_id=1, source_target_pairs={{0,2},{1,3},{2,0},{3,1},{4,6},{5,7},{6,4},{7,5},{8,10},{9,11},{10,... | collective-permute-start | bytes 393224 | tf_op jit(solution)/shard_map/ppermute | solution.py:30
  71.9 12.1 %collective-permute-start.33 = (bf16[128,512]{1,0:T(8,128)(2,1)S(1)}, bf16[128,512]{1,0:T(8,128)(2,1)S(1)}, u32[]{:S(2)}, u32[]{:S(2)}) collective-permute-start(bf16[128,512]{1,0:T(8,128)(2,1)S(1)} %shard_map.134.refs_1_), channel_id=1, source_target_pairs={{0,1},{1,0},{2,3},{3,2},{4,5},{5,4},{6,7},{7,6},{8,9},{9,8},{10,11... | collective-permute-start | bytes 393224 | tf_op jit(solution)/shard_map/ppermute | solution.py:30
  72.0 14.7 %collective-permute-start.29 = (bf16[128,512]{1,0:T(8,128)(2,1)S(1)}, bf16[128,512]{1,0:T(8,128)(2,1)S(1)}, u32[]{:S(2)}, u32[]{:S(2)}) collective-permute-start(bf16[128,512]{1,0:T(8,128)(2,1)S(1)} %shard_map.134.refs_1_), channel_id=1, source_target_pairs={{0,2},{1,3},{2,0},{3,1},{4,6},{5,7},{6,4},{7,5},{8,10},{9,11},{10,... | collective-permute-start | bytes 393224 | tf_op jit(solution)/shard_map/ppermute | solution.py:30
  74.9 11.7 %collective-permute-start.30 = (bf16[128,512]{1,0:T(8,128)(2,1)S(1)}, bf16[128,512]{1,0:T(8,128)(2,1)S(1)}, u32[]{:S(2)}, u32[]{:S(2)}) collective-permute-start(bf16[128,512]{1,0:T(8,128)(2,1)S(1)} %shard_map.134.refs_1_), channel_id=1, source_target_pairs={{0,3},{1,2},{2,1},{3,0},{4,7},{5,6},{6,5},{7,4},{8,11},{9,10},{10,... | collective-permute-start | bytes 393224 | tf_op jit(solution)/shard_map/ppermute | solution.py:30
  76.3 10.4 %collective-permute-start.31 = (bf16[128,512]{1,0:T(8,128)(2,1)S(1)}, bf16[128,512]{1,0:T(8,128)(2,1)S(1)}, u32[]{:S(2)}, u32[]{:S(2)}) collective-permute-start(bf16[128,512]{1,0:T(8,128)(2,1)S(1)} %shard_map.131.refs_0_), channel_id=1, source_target_pairs={{1,2},{2,1},{5,6},{6,5},{9,10},{10,9},{13,14},{14,13},{17,18},{18,... | collective-permute-start | bytes 393224 | tf_op jit(solution)/shard_map/ppermute | solution.py:547
  77.0 9.7 %collective-permute-start.32 = (bf16[128,512]{1,0:T(8,128)(2,1)S(1)}, bf16[128,512]{1,0:T(8,128)(2,1)S(1)}, u32[]{:S(2)}, u32[]{:S(2)}) collective-permute-start(bf16[128,512]{1,0:T(8,128)(2,1)S(1)} %collective-permute-done.28.refs_3_), channel_id=1, source_target_pairs={{1,0},{2,3},{5,4},{6,7},{9,8},{10,11},{13,12},{14,15},{17,16},{18,... | collective-permute-start | bytes 393224 | tf_op jit(solution)/shard_map/ppermute | solution.py:548
  (13 other events, 62.6 us)
